TPU v7x, 32 devices: a whole 2x2x4 slice. The times are simulated.
32 devices in a mesh: dp: 32 (over z, y, x, core).
Axes of the slice: x: 2, y: 2, z: 4, core: 2. Of those that a mesh axis runs over, the one named last changes fastest.
Arguments:
- tokens: bfloat16 [64, 577, 1024], P('dp'), may hold values from -6 to 6
- cotangent: bfloat16 [64, 577, 1024], P('dp'), may hold values from -6 to 6
- params: float32 [12595200], P('dp'), may hold values from -0.8 to 0.8
- moment_one: float32 [12595200], P('dp'), may hold values from -0.00024414062 to 0.00024414062
- moment_two: float32 [12595200], P('dp'), may hold values from 1.5879065e-09 to 7.939533e-09
Outputs:
- outputs: bfloat16 [64, 577, 1024], P('dp')
- grad_tokens: bfloat16 [64, 577, 1024], P('dp')
- weight_grad: float32 [12595200], P('dp')
- params_new: float32 [12595200], P('dp')
- moment_one_new: float32 [12595200], P('dp')
- moment_two_new: float32 [12595200], P('dp')
All inputs are finite; a program needn't handle non-finite values.
Results may differ from a plain program's by a relative error of at most 0.0095.
Values may be sent and summed in bfloat16 or wider, within the bound.
A program may use at most 448 MiB of HBM per device.

v0:
```python
import jax
import jax.numpy as jnp
from jax import lax
from jax.sharding import PartitionSpec as P

D = 1024
HEADS = 16
HEAD = 64
FF = 4096
MICRO = 2
STEP = 4


norm_eps = 1e-06
max_norm = 1.0
beta_one = 0.9
beta_two = 0.95
learn_rate = 0.02
decay_rate = 0.05
adam_eps = 1e-08
root_half = 0.7071067811865476
inv_root_tau = 0.3989422804014327


def unpack(flat):
    lengths = [3 * D * D, D * D, D * FF, FF * D, D, D, D, FF, D, D, D, D, D]
    pieces = []
    offset = 0
    for length in lengths:
        pieces.append(flat[offset : offset + length])
        offset = offset + length
    matrices = (
        pieces[0].reshape(D, 3 * D),
        pieces[1].reshape(D, D),
        pieces[2].reshape(D, FF),
        pieces[3].reshape(FF, D),
    )
    vectors = tuple((segment.astype(jnp.float32) for segment in pieces[4:]))
    return (matrices, vectors)


def norm_forward(values, shift, bias):
    center = values - jnp.mean(values, axis=-1, keepdims=True)
    recip = lax.rsqrt(jnp.mean(center * center, axis=-1, keepdims=True) + norm_eps)
    scaled = center * recip
    return (scaled * (1.0 + shift) + bias, scaled, recip)


def norm_backward(d_normed, scaled, recip, shift):
    grad_shift = jnp.sum(d_normed * scaled, axis=(0, 1))
    grad_bias = jnp.sum(d_normed, axis=(0, 1))
    expand = d_normed * (1.0 + shift)
    centered = expand - jnp.mean(expand, axis=-1, keepdims=True)
    d_values = recip * (centered - scaled * jnp.mean(expand * scaled, axis=-1, keepdims=True))
    return (d_values, grad_shift, grad_bias)


def gelu_parts(pre):
    cdf_value = 0.5 * (1.0 + lax.erf(pre * root_half))
    return (pre * cdf_value, cdf_value + pre * inv_root_tau * jnp.exp(-0.5 * pre * pre))


def head_scores(query_low, key_low):
    rows = query_low.shape[0]
    heads_q = query_low.reshape(rows, HEADS, HEAD)
    heads_k = key_low.reshape(rows, HEADS, HEAD)
    scores = jnp.einsum(
        "qhd,khd->hqk", heads_q, heads_k, preferred_element_type=jnp.float32
    ) * HEAD ** (-0.5)
    return (scores, heads_q, heads_k)


def attend(triple):
    query_low, key_low, value_low = triple
    rows = query_low.shape[0]
    scores, heads_q, heads_k = head_scores(query_low, key_low)
    heads_v = value_low.reshape(rows, HEADS, HEAD)
    row_max = jnp.max(scores, axis=-1, keepdims=True)
    expo = jnp.exp(scores - row_max)
    totals = jnp.sum(expo, axis=-1, keepdims=True)
    probs = expo / totals
    log_total = row_max + jnp.log(totals)
    mixed = jnp.einsum(
        "hqk,khd->qhd", probs.astype(jnp.bfloat16), heads_v, preferred_element_type=jnp.float32
    )
    return (mixed.reshape(rows, D).astype(jnp.bfloat16), log_total)


def attend_back(items):
    query_low, key_low, value_low, log_total, d_mixed = items
    rows = query_low.shape[0]
    scores, heads_q, heads_k = head_scores(query_low, key_low)
    heads_v = value_low.reshape(rows, HEADS, HEAD)
    probs = jnp.exp(scores - log_total)
    d_heads = d_mixed.reshape(rows, HEADS, HEAD)
    d_value = jnp.einsum(
        "hqk,qhd->khd", probs.astype(jnp.bfloat16), d_heads, preferred_element_type=jnp.float32
    )
    d_probs = jnp.einsum("qhd,khd->hqk", d_heads, heads_v, preferred_element_type=jnp.float32)
    d_scores = (probs * (d_probs - jnp.sum(probs * d_probs, axis=-1, keepdims=True))).astype(
        jnp.bfloat16
    )
    d_query = jnp.einsum(
        "hqk,khd->qhd", d_scores, heads_k, preferred_element_type=jnp.float32
    ) * HEAD ** (-0.5)
    d_key = jnp.einsum(
        "hqk,qhd->khd", d_scores, heads_q, preferred_element_type=jnp.float32
    ) * HEAD ** (-0.5)
    joined = jnp.concatenate(
        [d_query.reshape(rows, D), d_key.reshape(rows, D), d_value.reshape(rows, D)], axis=1
    )
    return joined.astype(jnp.bfloat16)


def forward_pass(flat, images_now):
    matrices, vectors = unpack(flat)
    w_qkv, w_out, w_up, w_down = matrices
    b_query, b_value, b_out, b_up, b_down, shift_one, bias_one, shift_two, bias_two = vectors
    inputs = images_now.astype(jnp.float32)
    normed, scaled_one, recip_one = norm_forward(inputs, shift_one, bias_one)
    project = jnp.einsum(
        "bsd,de->bse", normed.astype(jnp.bfloat16), w_qkv, preferred_element_type=jnp.float32
    )
    query_low = (project[:, :, :D] + b_query).astype(jnp.bfloat16)
    key_low = project[:, :, D : 2 * D].astype(jnp.bfloat16)
    value_low = (project[:, :, 2 * D :] + b_value).astype(jnp.bfloat16)
    mixed_low, log_total = lax.map(attend, (query_low, key_low, value_low))
    hidden = inputs + (
        jnp.einsum("bsd,de->bse", mixed_low, w_out, preferred_element_type=jnp.float32) + b_out
    )
    normed_two, scaled_two, recip_two = norm_forward(hidden, shift_two, bias_two)
    pre = (
        jnp.einsum(
            "bsd,df->bsf", normed_two.astype(jnp.bfloat16), w_up, preferred_element_type=jnp.float32
        )
        + b_up
    )
    active, slope = gelu_parts(pre)
    result = hidden + (
        jnp.einsum(
            "bsf,fd->bsd", active.astype(jnp.bfloat16), w_down, preferred_element_type=jnp.float32
        )
        + b_down
    )
    return (
        result.astype(jnp.bfloat16),
        (query_low, key_low, value_low, log_total, mixed_low, hidden, pre),
    )


def backward_pass(flat, images_now, tangent, saved):
    matrices, vectors = unpack(flat)
    w_qkv, w_out, w_up, w_down = matrices
    b_query, b_value, b_out, b_up, b_down, shift_one, bias_one, shift_two, bias_two = vectors
    query_low, key_low, value_low, log_total, mixed_low, hidden, pre = saved
    inputs = images_now.astype(jnp.float32)
    normed, scaled_one, recip_one = norm_forward(inputs, shift_one, bias_one)
    normed_low = normed.astype(jnp.bfloat16)
    normed_two, scaled_two, recip_two = norm_forward(hidden, shift_two, bias_two)
    active, slope = gelu_parts(pre)
    tangent_wide = tangent.astype(jnp.float32)
    grad_down = jnp.einsum(
        "bsf,bsd->fd", active.astype(jnp.bfloat16), tangent, preferred_element_type=jnp.float32
    )
    grad_bdown = jnp.sum(tangent_wide, axis=(0, 1))
    d_active = jnp.einsum("bsd,fd->bsf", tangent, w_down, preferred_element_type=jnp.float32)
    d_pre = (d_active * slope).astype(jnp.bfloat16)
    grad_up = jnp.einsum(
        "bsd,bsf->df", normed_two.astype(jnp.bfloat16), d_pre, preferred_element_type=jnp.float32
    )
    grad_bup = jnp.sum(d_pre, axis=(0, 1), dtype=jnp.float32)
    d_normtwo = jnp.einsum("bsf,df->bsd", d_pre, w_up, preferred_element_type=jnp.float32)
    d_lntwo, grad_stwo, grad_btwo = norm_backward(d_normtwo, scaled_two, recip_two, shift_two)
    d_hidden = tangent_wide + d_lntwo
    d_branch = d_hidden.astype(jnp.bfloat16)
    grad_out = jnp.einsum("bsd,bse->de", mixed_low, d_branch, preferred_element_type=jnp.float32)
    grad_bout = jnp.sum(d_branch, axis=(0, 1), dtype=jnp.float32)
    d_mixed = jnp.einsum("bse,de->bsd", d_branch, w_out, preferred_element_type=jnp.float32).astype(
        jnp.bfloat16
    )
    d_project = lax.map(attend_back, (query_low, key_low, value_low, log_total, d_mixed))
    grad_qkv = jnp.einsum("bsd,bse->de", normed_low, d_project, preferred_element_type=jnp.float32)
    grad_bquery = jnp.sum(d_project[:, :, :D], axis=(0, 1), dtype=jnp.float32)
    grad_bvalue = jnp.sum(d_project[:, :, 2 * D :], axis=(0, 1), dtype=jnp.float32)
    d_normone = jnp.einsum("bse,de->bsd", d_project, w_qkv, preferred_element_type=jnp.float32)
    d_lnone, grad_sone, grad_bone = norm_backward(d_normone, scaled_one, recip_one, shift_one)
    grad_in = (d_hidden + d_lnone).astype(jnp.bfloat16)
    flat_grad = jnp.concatenate(
        [
            grad_qkv.reshape(-1),
            grad_out.reshape(-1),
            grad_up.reshape(-1),
            grad_down.reshape(-1),
            grad_bquery,
            grad_bvalue,
            grad_bout,
            grad_bup,
            grad_bdown,
            grad_sone,
            grad_bone,
            grad_stwo,
            grad_btwo,
        ]
    )
    return (flat_grad, grad_in)


def shards(tokens, cotangent, params, moment_one, moment_two):
    dev_count = lax.axis_size("dp")
    shard_len = params.shape[0]
    per_micro = tokens.shape[0] // MICRO
    images_all = tokens.shape[0] * dev_count
    shard_low = params.astype(jnp.bfloat16)
    local_grad = jnp.zeros((shard_len * dev_count,), jnp.float32)
    results = []
    input_grads = []
    for micro_index in range(MICRO):
        images_now = tokens[micro_index * per_micro : (micro_index + 1) * per_micro]
        tangent = cotangent[micro_index * per_micro : (micro_index + 1) * per_micro]
        front_weights = lax.all_gather(shard_low, "dp", axis=0, tiled=True)
        result, saved = forward_pass(front_weights, images_now)
        back_weights = lax.all_gather(shard_low, "dp", axis=0, tiled=True)
        flat_grad, grad_in = backward_pass(back_weights, images_now, tangent, saved)
        local_grad = local_grad + flat_grad
        results.append(result)
        input_grads.append(grad_in)
    arrived = lax.all_to_all(
        local_grad.reshape(dev_count, shard_len).astype(jnp.bfloat16),
        "dp",
        split_axis=0,
        concat_axis=0,
        tiled=True,
    ).astype(jnp.float32)
    shard_grad = jnp.sum(arrived, axis=0)
    weight_grad = shard_grad / images_all
    square_sum = lax.psum(jnp.sum(weight_grad * weight_grad), "dp")
    clip_factor = jnp.minimum(1.0, max_norm / (jnp.sqrt(square_sum) + 1e-06))
    clipped = clip_factor * weight_grad
    moment_one_new = beta_one * moment_one + (1.0 - beta_one) * clipped
    moment_two_new = beta_two * moment_two + (1.0 - beta_two) * clipped * clipped
    correct_one = 1.0 - beta_one**STEP
    correct_two = 1.0 - beta_two**STEP
    params_new = params - learn_rate * (
        moment_one_new / correct_one / (jnp.sqrt(moment_two_new / correct_two) + adam_eps)
        + decay_rate * params
    )
    outputs = jnp.concatenate(results, axis=0)
    grad_tokens = jnp.concatenate(input_grads, axis=0)
    return (outputs, grad_tokens, weight_grad, params_new, moment_one_new, moment_two_new)


def solution(mesh):
    in_specs = (P("dp", None, None), P("dp", None, None), P("dp"), P("dp"), P("dp"))
    out_specs = (P("dp", None, None), P("dp", None, None), P("dp"), P("dp"), P("dp"), P("dp"))
    return jax.shard_map(shards, mesh=mesh, in_specs=in_specs, out_specs=out_specs, check_vma=False)
```

profile of v0, /device:TPU:0, one launch (start us, length us, event | category | flops | bytes accessed | tf_op | source)
XLA Modules:
  0.0 2362.3 jit_solution(2931164241218497350)
XLA Ops:
  32.0 264.6 %all-gather.3.cloned.1.call-done = bf16[32,1,393600]{2,1,0:T(2,128)(2,1)} async-done(((bf16[1,1,393600]{2,1,0:T(2,128)(2,1)}), bf16[32,1,393600]{2,1,0:T(2,128)(2,1)}) %all-gather.3.cloned.1.call-update) | async-done | bytes 25190416 | tf_op jit(solution)/shard_map/all_gather | solution.py:220
  296.5 148.7 %reduce.37 = bf16[32,393600]{1,0:T(8,128)(2,1)} reduce(bf16[32,1,393600]{2,1,0:T(2,128)(2,1)} %all-gather.3.cloned.1.call-done, bf16[]{:T(256)} %constant.129), dimensions={1}, to_apply=%all-gather.reduce_sub_computation | reduce | bytes 50380800 | tf_op jit(solution)/shard_map/all_gather | solution.py:220
  445.3 59.3 %reshape.702 = bf16[12595200]{0:T(1024)(128)(2,1)} reshape(bf16[32,393600]{1,0:T(8,128)(2,1)} %reduce.37) | data formatting | bytes 50380800
  513.7 11.3 fusion.116
  577.4 11.5 fusion.74
  591.4 13.3 slice.160
  616.6 13.5 multiply_reduce_fusion.3
  654.9 13.5 slice.163
  676.7 20.3 multiply_convert_fusion.3
  697.0 12.1 convert_reduce_fusion.2
  719.3 12.1 convert_reduce_fusion.1
  750.8 11.8 convert_reduce_fusion.7
  762.6 15.1 multiply_reduce_fusion
  777.7 20.4 multiply_convert_fusion
  818.0 11.2 convert_reduce_fusion.9
  829.2 15.1 multiply_reduce_fusion.1
  844.3 20.5 multiply_convert_fusion.1
  886.8 12.1 convolution_bitcast_fusion.7
  918.5 12.7 convolution_bitcast_fusion.6
  947.2 12.1 copy.98
  959.3 11.2 constant_dynamic-update-slice_fusion.24
  998.5 12.1 copy.102
  1010.6 11.3 constant_dynamic-update-slice_fusion.25
  1058.3 13.7 constant_dynamic-update-slice_fusion.20
  1112.7 39.9 %add_convert_fusion = bf16[12595200]{0:T(1024)(128)(2,1)} fusion(f32[12595200]{0:T(1024)} %constant_dynamic-update-slice_fusion, f32[12595200]{0:T(1024)} %constant_dynamic-update-slice_fusion.1), kind=kLoop, calls=%fused_computation.1 | loop fusion | flops 25190400 | bytes 125952000 | tf_op jit(solution)/shard_map/convert_element_type | solution.py:228
  1152.6 49.1 %convert_element_type.315 = bf16[32,1,393600]{2,1,0:T(2,128)(2,1)} reshape(bf16[12595200]{0:T(1024)(128)(2,1)} %add_convert_fusion) | data formatting | bytes 50380800 | tf_op jit(solution)/shard_map/convert_element_type | solution.py:228
  1202.2 149.4 %reduce.42 = bf16[32,393600]{1,0:T(8,128)(2,1)} reduce(bf16[32,1,393600]{2,1,0:T(2,128)(2,1)} %convert_element_type.315, bf16[]{:T(256)} %broadcast.342), dimensions={1}, to_apply=%convert_element_type.315.reduce_sub_computation | reduce | bytes 50380800 | tf_op jit(solution)/shard_map/convert_element_type | solution.py:228
  1351.6 44.2 %reshape.704 = bf16[32,2,196800]{2,1,0:T(2,128)(2,1)} reshape(bf16[32,393600]{1,0:T(8,128)(2,1)} %reduce.42) | data formatting | bytes 50380800
  1428.0 534.1 %all-to-all-done = bf16[32,2,196800]{2,1,0:T(2,128)(2,1)} async-done(((bf16[32,2,196800]{2,1,0:T(2,128)(2,1)}), bf16[32,2,196800]{2,1,0:T(2,128)(2,1)}, u32[]{:S(2)}, u32[]{:S(2)}) %all-to-all-start) | async-done | bytes 25190432 | tf_op jit(solution)/shard_map/all_to_all | solution.py:227
  1962.2 87.2 %reshape.705 = bf16[32,1,393600]{2,1,0:T(2,128)(2,1)} reshape(bf16[32,2,196800]{2,1,0:T(2,128)(2,1)} %all-to-all-done) | data formatting | bytes 50380800
  2049.4 261.1 %convert_reduce_fusion = f32[393600]{0:T(1024)S(1)} fusion(bf16[32,1,393600]{2,1,0:T(2,128)(2,1)} %reshape.705), kind=kLoop, calls=%fused_computation | loop fusion | flops 24796800 | bytes 26764800 | tf_op jit(solution)/shard_map/reduce_sum | solution.py:234
  2312.6 37.0 %psum.7 = f32[]{:T(128)} all-reduce(f32[]{:T(128)} %get-tuple-element.121), channel_id=1, replica_groups=mesh['dp'=32] {'dp'}, use_global_device_ids=true, to_apply=%region_42.43 | all-reduce | flops 1 | bytes 8 | tf_op jit(solution)/shard_map/psum | solution.py:236
  (396 shorter events, 384.4 us)
Async XLA Ops:
  7.2 289.4 %all-gather.3.cloned.1.call-start = ((), (), s32[]{:S(2)}) async-start(), calls=%async_computation.1 | async-start | bytes 51955200 | tf_op jit(solution)/shard_map/all_gather | solution.py:220
  22.8 512.5 %copy-start.9 = (bf16[1,577,1024]{2,1,0:T(8,128)(2,1)}, bf16[1,577,1024]{2,1,0:T(8,128)(2,1)S(1)}, u32[]{:S(2)}) copy-start(bf16[1,577,1024]{2,1,0:T(8,128)(2,1)S(1)} %get-tuple-element.134) | copy-start | bytes 3545092
  22.8 519.7 %copy-start.20 = (bf16[1,577,1024]{2,1,0:T(8,128)(2,1)}, bf16[1,577,1024]{2,1,0:T(8,128)(2,1)S(1)}, u32[]{:S(2)}) copy-start(bf16[1,577,1024]{2,1,0:T(8,128)(2,1)S(1)} %get-tuple-element.192) | copy-start | bytes 3545092
  22.8 512.5 %copy-start.64 = (f32[577]{0:T(1024)}, f32[577]{0:T(1024)S(1)}, u32[]{:S(2)}) copy-start(f32[577]{0:T(1024)S(1)} %broadcast_multiply_fusion.10) | copy-start | bytes 6928
  23.3 519.2 %copy-start.73 = (f32[577]{0:T(1024)}, f32[577]{0:T(1024)S(1)}, u32[]{:S(2)}) copy-start(f32[577]{0:T(1024)S(1)} %broadcast_multiply_fusion.12) | copy-start | bytes 6928
  23.8 511.6 %copy-start.70 = (f32[577]{0:T(1024)}, f32[577]{0:T(1024)S(1)}, u32[]{:S(2)}) copy-start(f32[577]{0:T(1024)S(1)} %add_rsqrt_fusion.1) | copy-start | bytes 6928
  25.3 517.2 %copy-start.79 = (f32[577]{0:T(1024)}, f32[577]{0:T(1024)S(1)}, u32[]{:S(2)}) copy-start(f32[577]{0:T(1024)S(1)} %add_rsqrt_fusion.3) | copy-start | bytes 6928
  505.9 36.7 %copy-start.91 = (f32[1024]{0:T(1024)}, f32[1024]{0:T(1024)S(1)}, u32[]{:S(2)}) copy-start(f32[1024]{0:T(1024)S(1)} %get-tuple-element.140) | copy-start | bytes 12292
  505.9 170.8 %copy-start.53 = (f32[1024]{0:T(1024)}, f32[1024]{0:T(1024)S(1)}, u32[]{:S(2)}) copy-start(f32[1024]{0:T(1024)S(1)} %get-tuple-element.136) | copy-start | bytes 12292
  513.0 29.6 %copy-start.67 = (f32[1024]{0:T(1024)}, f32[1024]{0:T(1024)S(1)}, u32[]{:S(2)}) copy-start(f32[1024]{0:T(1024)S(1)} %get-tuple-element.144) | copy-start | bytes 12292
  608.6 137.0 %copy-start = (f32[1,577,1024]{2,1,0:T(8,128)}, f32[1,577,1024]{2,1,0:T(8,128)S(1)}, u32[]{:S(2)}) copy-start(f32[1,577,1024]{2,1,0:T(8,128)S(1)} %get-tuple-element.171) | copy-start | bytes 7090180
  608.6 137.0 %copy-start.56 = (f32[577]{0:T(1024)}, f32[577]{0:T(1024)S(1)}, u32[]{:S(2)}) copy-start(f32[577]{0:T(1024)S(1)} %broadcast_multiply_fusion.9) | copy-start | bytes 6928
  609.0 136.6 %copy-start.58 = (f32[577]{0:T(1024)}, f32[577]{0:T(1024)S(1)}, u32[]{:S(2)}) copy-start(f32[577]{0:T(1024)S(1)} %add_rsqrt_fusion) | copy-start | bytes 6928
  668.4 28.5 %slice-start.21 = ((s8[8388608]{0:T(1024)(128)(4,1)}), s8[4194304]{0:T(1024)(128)(4,1)S(1)}, s32[]{:S(2)}) async-start(s8[8388608]{0:T(1024)(128)(4,1)} %bitcast.238), calls=%async_computation.23 | async-start | bytes 8388608
  676.6 20.3 copy-start.98
  676.6 20.3 slice-start.22
  676.7 20.3 copy-start.40
  777.7 20.4 copy-start.18
  844.3 20.5 copy-start.19
  864.8 16.2 slice-start.23
  881.1 21.6 slice-start.27
  886.8 59.3 %copy-start.28 = (f32[577,1024]{1,0:T(8,128)}, f32[577,1024]{1,0:T(8,128)S(1)}, u32[]{:S(2)}) copy-start(f32[577,1024]{1,0:T(8,128)S(1)} %get-tuple-element.178) | copy-start | bytes 7090180
  913.9 21.1 slice-start.25
  918.4 131.0 %copy-start.7 = (f32[577,1024]{1,0:T(8,128)}, f32[577,1024]{1,0:T(8,128)S(1)}, u32[]{:S(2)}) copy-start(f32[577,1024]{1,0:T(8,128)S(1)} %fusion.66) | copy-start | bytes 7090180
  918.5 16.5 slice-start.26
  1055.9 16.1 slice-start.9
  1058.3 32.1 %slice-start.1 = ((s8[16777216]{0:T(1024)(128)(4,1)}), s8[4194304]{0:T(1024)(128)(4,1)S(1)}, s32[]{:S(2)}) async-start(s8[16777216]{0:T(1024)(128)(4,1)} %bitcast.208), calls=%async_computation.3 | async-start | bytes 8388608
  1058.3 32.1 %slice-start.2 = ((s8[16777216]{0:T(1024)(128)(4,1)}), s8[4194304]{0:T(1024)(128)(4,1)S(1)}, s32[]{:S(2)}) async-start(s8[16777216]{0:T(1024)(128)(4,1)} %bitcast.208), calls=%async_computation.4 | async-start | bytes 8388608
  1074.2 16.2 slice-start.3
  1074.2 16.2 slice-start.4
  1395.8 566.4 %all-to-all-start = ((bf16[32,2,196800]{2,1,0:T(2,128)(2,1)}), bf16[32,2,196800]{2,1,0:T(2,128)(2,1)}, u32[]{:S(2)}, u32[]{:S(2)}) async-start(bf16[32,2,196800]{2,1,0:T(2,128)(2,1)} %reshape.704), calls=%async_computation | async-start | bytes 50397184 | tf_op jit(solution)/shard_map/all_to_all | solution.py:227
  2310.5 39.8 %copy-start.31 = (f32[393600]{0:T(1024)S(1)}, f32[393600]{0:T(1024)}, u32[]{:S(2)}) copy-start(f32[393600]{0:T(1024)} %param.7) | copy-start | bytes 4723204
  (102 other events, 871.3 us)
Sparse Core Ops, SparseCore 0:
  18.7 277.7 all-gather.2
where the time goes:
time: 2370 us; the launch traced here: 2360 us
  waiting for transfers between devices  799 us (34%)
  other arithmetic  697 us (29%)
  local copies, waits for them, and re-layouts  488 us (21%)
  matrix products  321 us (14%)
  blocking collectives  37 us (2%)
    all_to_all x1, waiting for transfers between devices, shards(): lax.all_to_all(local_grad.reshape(dev_count, shard_len).astype(jnp.bfloat...  534 us
    unnamed x300, local copies, waits for them, and re-layouts  357 us
    all_gather x1, waiting for transfers between devices, shards(): front_weights = lax.all_gather(shard_low, 'dp', axis=0, tiled=True)  265 us
    reduce_sum x1, other arithmetic, shards(): shard_grad = jnp.sum(arrived, axis=0)  261 us
    convert_element_type x2, other arithmetic, shards(): local_grad.reshape(dev_count, shard_len).astype(jnp.bfloat16)  189 us
    all_gather x1, other arithmetic, shards(): front_weights = lax.all_gather(shard_low, 'dp', axis=0, tiled=True)  149 us
    slice x8, local copies, waits for them, and re-layouts, unpack(): pieces.append(flat[offset:offset + length])  57.3 us
    convert_element_type x2, local copies, waits for them, and re-layouts, shards(): local_grad.reshape(dev_count, shard_len).astype(jnp.bfloat16)  49.6 us
  transfers between devices with their start and end apart: 2, of which 2 were waited for; matrix products, arithmetic and copies ran while one was open for 2% of the time, Pallas kernels for 0%

commit v1 on v0

v1 whole, which is shorter than its diff:
```python
import functools

import jax
import jax.numpy as jnp
from jax import lax
from jax.experimental import pallas as pl
from jax.experimental.pallas import tpu as pltpu
from jax.sharding import PartitionSpec as P

D = 1024
FF = 4096
S = 577
SQ = 592
M = 2 * SQ
CH = 32
PIECES = 96
STEP = 4
BF = jnp.bfloat16
F32 = jnp.float32
MESH = pl.DeviceIdType.MESH
VMEM_ALL = 67043328

EPS = 1e-06
max_norm = 1.0
beta_one = 0.9
beta_two = 0.95
learn_rate = 0.02
decay_rate = 0.05
adam_eps = 1e-08
SCORE = 0.125 * 1.4426950408889634


def nt(a, b):
    return lax.dot_general(a, b, (((1,), (1,)), ((), ())), preferred_element_type=F32)


def nn(a, b):
    return jnp.dot(a, b, preferred_element_type=F32)


def tn(a, b):
    return lax.dot_general(a, b, (((0,), (0,)), ((), ())), preferred_element_type=F32)


def rows_at(c):
    return pl.ds(pl.multiple_of(c * CH, CH), CH)


def full(shape):
    return pl.BlockSpec(shape, lambda *_: (0,) * len(shape), pipeline_mode=pl.Buffered(1))


class Ctx:
    def __init__(s):
        me=lax.axis_index("dp"); s.me=me
        s.core=me%2; s.x=(me//2)%2; s.y=(me//4)%2; s.z=me//8
        s.sib=me+1-2*s.core
        xp=me+2*(1-2*s.x); yp=me+4*(1-2*s.y)
        s.ap=xp+(yp-xp)*s.core
        s.bp=yp+(xp-yp)*s.core
        s.astep=2+2*s.core; s.bstep=4-2*s.core
        s.abit=s.x+(s.y-s.x)*s.core; s.bbit=s.y+(s.x-s.y)*s.core
        s.up=me+8; s.dn=me-8
        s.hasup=s.z<3; s.hasdn=s.z>0
    def barrier(s):
        bar=pltpu.get_barrier_semaphore()
        for p in (s.sib,s.ap,s.bp): pl.semaphore_signal(bar,inc=1,device_id=(p,),device_id_type=MESH)
        @pl.when(s.hasup)
        def _(): pl.semaphore_signal(bar,inc=1,device_id=(s.up,),device_id_type=MESH)
        @pl.when(s.hasdn)
        def _(): pl.semaphore_signal(bar,inc=1,device_id=(s.dn,),device_id_type=MESH)
        pl.semaphore_wait(bar,3+jnp.where(s.hasup,1,0)+jnp.where(s.hasdn,1,0))
class Gather:
    NSEND=3*(5+6*4+7*2+7+7)
    def __init__(s,own,w,ssem,rsem,lsem,K=3,vec=None):
        c=s.c=Ctx(); s.own,s.w,s.ssem,s.rsem,s.lsem=own,w,ssem,rsem,lsem
        s.K=K; s.pend=[]; s.ns=0; s.steps=[]
        TRUE=None
        s.start=s._start
        for dist in range(1,6):
            for sg in (1,-1):
                for kind in ("z","a","b","ba"):
                    extra={"z":0,"a":1,"b":1,"ba":2}[kind]
                    dz=dist-extra
                    if dz<0 or dz>3 or (kind=="z" and dz==0) or (dz==0 and sg<0): continue
                    s.steps.append(functools.partial(s._item,kind,sg*dz))
        s.steps.append(s._finish)
    def _send(s,src,p,to,cond):
        i=s.ns; s.ns+=1
        cp=pltpu.make_async_remote_copy(src,s.w.at[p],s.ssem.at[i],s.rsem.at[p],device_id=(to,),device_id_type=MESH)
        if cond is None: cp.start()
        else:
            @pl.when(cond)
            def _(): cp.start()
        s.pend.append((cp,cond))
    def _start(s):
        c=s.c
        for k in range(s.K):
            p=c.me*s.K+k; src=s.own.at[k]
            s._send(src,p,c.up,c.hasup); s._send(src,p,c.dn,c.hasdn)
            s._send(src,p,c.bp,None); s._send(src,p,c.ap,None); s._send(src,p,c.sib,None)
        s.loc=[]
        for k in range(s.K):
            cp=pltpu.make_async_copy(s.own.at[k],s.w.at[c.me*s.K+k],s.lsem.at[k]); cp.start(); s.loc.append(cp)
    def _wait(s,p):
        pltpu.make_async_copy(s.w.at[p],s.w.at[p],s.rsem.at[p]).wait()
    def _item(s,kind,dz):
        c=s.c
        zz=c.z+dz
        fl=jnp.int32(0)
        src=c.me+8*dz
        if "a" in kind: src=src+c.astep*(1-2*c.abit)
        if "b" in kind: src=src+c.bstep*(1-2*c.bbit)
        valid=None if dz==0 else ((zz<4) if dz>0 else (zz>=0))
        def body():
            for k in range(s.K):
                p=src*s.K+k
                s._wait(p)
                sends=[]
                if kind=="z":
                    sends.append((c.dn,c.hasdn) if dz>0 else (c.up,c.hasup))
                if kind in("z","a"): sends.append((c.bp,None))
                if kind=="z": sends.append((c.ap,None))
                sends.append((c.sib,None))
                for to,cond in sends:
                    i=s.ns; s.ns+=1
                    cp=pltpu.make_async_remote_copy(s.w.at[p],s.w.at[p],s.ssem.at[i],s.rsem.at[p],device_id=(to,),device_id_type=MESH)
                    if cond is None: cp.start()
                    else:
                        @pl.when(cond)
                        def _(): cp.start()
                    s.pend.append((kind,dz,p,i,to,cond,valid))
        if valid is None: body()
        else: pl.when(valid)(body)
    def _finish(s):
        c=s.c
        def sibw(i,_):
            chip=i//s.K; k=i%s.K
            s._wait((2*chip+1-c.core)*s.K+k)
            return 0
        lax.fori_loop(0,16*s.K,sibw,0)
        for e in s.pend:
            if len(e)==2:
                cp,cond=e
                if cond is None: cp.wait_send()
                else: pl.when(cond)(cp.wait_send)
            else:
                kind,dz,p,i,to,cond,valid=e
                def w(i=i):
                    pltpu.make_async_copy(s.w.at[0],s.w.at[0],s.ssem.at[i]).wait()
                cc=cond if valid is None else (valid if cond is None else jnp.logical_and(cond,valid))
                if cc is None: w()
                else: pl.when(cc)(w)
        for cp in s.loc: cp.wait()
def gather_kernel(own_ref,w_ref,ssem,rsem,lsem):
    g=Gather(own_ref,w_ref,ssem,rsem,lsem)
    g.c.barrier()
    g.start()
    for st in g.steps: st()
def gather(own):
    return pl.pallas_call(gather_kernel,out_shape=jax.ShapeDtypeStruct((96,128,1024),BF),
       in_specs=[pl.BlockSpec(memory_space=pltpu.VMEM)],out_specs=pl.BlockSpec(memory_space=pl.ANY),
       scratch_shapes=[pltpu.SemaphoreType.DMA((Gather.NSEND,)),pltpu.SemaphoreType.DMA((96,)),pltpu.SemaphoreType.DMA((3,))],
       compiler_params=pltpu.CompilerParams(collective_id=1,has_side_effects=True),name="gather")(own)

class Reduce:
    K=3
    @staticmethod
    def counts(lo,hi):
        nz=hi-lo+1; K=Reduce.K
        return dict(S=nz*4*K,B=nz*2*K,A=nz*K,Z=(nz+1)*K,send=nz*2*K+nz*K+6*K)
    @staticmethod
    def scratch(lo,hi,nst=4):
        c=Reduce.counts(lo,hi); pc=lambda n: pltpu.VMEM((n,128,1024),BF); sem=lambda n: pltpu.SemaphoreType.DMA((n,))
        return [pc(c["S"]),pc(c["B"]),pc(c["A"]),pc(c["Z"]),pc(nst),sem(c["S"]),sem(c["S"]),sem(c["B"]),sem(c["A"]),sem(c["Z"]),sem(c["send"]),sem(nst)]
    def __init__(s,c,lo,hi,parts,out,scr,scale):
        s.c,s.lo,s.hi,s.parts,s.out,s.scale=c,lo,hi,parts,out,scale
        s.S,s.B,s.A,s.Z,s.st,s.sS,s.rS,s.rB,s.rA,s.rZ,s.ss,s.ls=scr
        s.nst=s.st.shape[0]; s.nz=hi-lo+1
        s.deferred=[]; s.ns=0; s.waits=[]
        K=s.K
        its=[]
        for zz in range(hi,lo-1,-1):
            for fa in (1,0):
                for k in range(K): its.append(("b",zz,1,fa,k))
        for zz in range(hi,lo-1,-1):
            for k in range(K): its.append(("a",zz,0,1,k))
        for dist in (3,2,1,0):
            for sg in ((1,-1) if dist else (1,)):
                for k in range(K): its.append(("z",sg*dist,0,0,k))
        s.its=its
        s.steps=[functools.partial(s._item,i) for i in range(len(its))]+[s._finish]
    def _dest(s,zz,fb,fa,color_core):
        c=s.c
        cc=color_core
        astep=2+2*cc; bstep=4-2*cc
        abit=c.x+(c.y-c.x)*cc; bbit=c.y+(c.x-c.y)*cc
        b=bbit+fb*(1-2*bbit); a=abit+fa*(1-2*abit)
        return zz*8+cc+bstep*b+astep*a
    def _src(s,p,fn):
        if len(s.parts)==1:
            lo,hi,ref=s.parts[0]; fn(ref.at[p-lo]); return
        for lo,hi,ref in s.parts:
            @pl.when(jnp.logical_and(p>=lo,p<hi))
            def _(): fn(ref.at[jnp.clip(p-lo,0,hi-lo-1)])
    def _slotS(s,zz,fb,fa,k): return (((zz-s.lo)*2+fb)*2+fa)*s.K+k
    def send_sibling(s):
        c=s.c; oc=1-c.core
        for (kind,zz,fb,fa,k) in s._order():
            p=s._dest(zz,fb,fa,oc)*s.K+k; sl=s._slotS(zz,fb,fa,k)
            def go(r): pltpu.make_async_remote_copy(r,s.S.at[sl],s.sS.at[sl],s.rS.at[sl],device_id=(c.sib,),device_id_type=MESH).start()
            s._src(p,go)
    def _order(s):
        o=[]
        for it in s.its:
            if it[0] in "ba": o.append(it)
        for zz in range(s.hi,s.lo-1,-1):
            for k in range(s.K): o.append(("z",zz,0,0,k))
        return o
    def _info(s,i):
        kind,zz,fb,fa,k=s.its[i]; valid=None
        if kind=="z":
            zz=s.c.z+zz; valid=jnp.logical_and(zz>=s.lo,zz<=s.hi)
        return kind,zz,fb,fa,k,valid
    def _load(s,i):
        if i>=len(s.its): return
        kind,zz,fb,fa,k,valid=s._info(i)
        p=s._dest(zz,fb,fa,s.c.core)*s.K+k
        def go(r): pltpu.make_async_copy(r,s.st.at[i%s.nst],s.ls.at[i%s.nst]).start()
        if valid is None: s._src(p,go)
        else: pl.when(valid)(lambda: s._src(p,go))
    def prefetch(s):
        for i in range(s.nst-1): s._load(i)
    def _flush(s):
        for f in s.deferred: f()
        s.deferred=[]
    def _wait(s,ref,sem): pltpu.make_async_copy(ref,ref,sem).wait()
    def _sum(s,srcs,dst,scale=None):
        def body(r,_):
            rr=pl.ds(pl.multiple_of(r*16,16),16)
            t=srcs[0][rr,:].astype(F32)
            for q in srcs[1:]: t=t+q[rr,:].astype(F32)
            if scale is not None: t=t*scale
            dst[rr,:]=t.astype(dst.dtype)
            return 0
        lax.fori_loop(0,8,body,0)
    def _item(s,i):
        c=s.c; K=s.K
        kind,zz,fb,fa,k,valid=s._info(i)
        dist=s.its[i][1] if kind=="z" else None
        def main():
            own=s.st.at[i%s.nst]
            s._wait(own,s.ls.at[i%s.nst])
            sl=s._slotS(zz,fb,fa,k)
            srcs=[own,s.S.at[sl]]; s._wait(s.S.at[sl],s.rS.at[sl])
            if kind in "az":
                bi=((zz-s.lo)*2+fa)*K+k; srcs.append(s.B.at[bi]); s._wait(s.B.at[bi],s.rB.at[bi])
            if kind=="z":
                ai=(zz-s.lo)*K+k; srcs.append(s.A.at[ai]); s._wait(s.A.at[ai],s.rA.at[ai])
            return sl,srcs
        def send(sl,dst,rsem,to,n):
            return pltpu.make_async_remote_copy(s.S.at[sl],dst,s.ss.at[n],rsem,device_id=(to,),device_id_type=MESH)
        prev=s.deferred; s.deferred=[]
        if kind in "ba":
            sl,srcs=main()
            s._sum(srcs,s.S.at[sl])
            n=s.ns; s.ns+=1
            if kind=="b":
                bi=((zz-s.lo)*2+fa)*K+k; cp=send(sl,s.B.at[bi],s.rB.at[bi],c.bp,n)
            else:
                ai=(zz-s.lo)*K+k; cp=send(sl,s.A.at[ai],s.rA.at[ai],c.ap,n)
            s.deferred.append(cp.start); s.waits.append((n,None))
        elif dist!=0:
            n=s.ns; s.ns+=1
            upw=dist>0
            zi=(zz-s.lo)*K+k
            has=c.hasdn if upw else c.hasup
            @pl.when(valid)
            def _():
                sl,srcs=main()
                @pl.when(has)
                def _():
                    s._wait(s.Z.at[zi],s.rZ.at[zi]); s._sum(srcs+[s.Z.at[zi]],s.S.at[sl])
                @pl.when(jnp.logical_not(has))
                def _(): s._sum(srcs,s.S.at[sl])
            last=jnp.logical_and(zz==c.z-1,not upw)
            zo=jnp.where(last,s.nz*K+k,zi)
            def st():
                @pl.when(valid)
                def _():
                    send(s._slotS(zz,fb,fa,k),s.Z.at[zo],s.rZ.at[zo],c.up if upw else c.dn,n).start()
            s.deferred.append(st); s.waits.append((n,valid))
        else:
            @pl.when(valid)
            def _():
                sl,srcs=main()
                z1=s.Z.at[(zz-s.lo)*K+k]; r1=s.rZ.at[(zz-s.lo)*K+k]; z2=s.Z.at[s.nz*K+k]; r2=s.rZ.at[s.nz*K+k]
                @pl.when(jnp.logical_and(c.hasdn,c.hasup))
                def _():
                    s._wait(z1,r1); s._wait(z2,r2); s._sum(srcs+[z1,z2],s.out.at[k],s.scale)
                @pl.when(jnp.logical_not(c.hasup))
                def _():
                    s._wait(z1,r1); s._sum(srcs+[z1],s.out.at[k],s.scale)
                @pl.when(jnp.logical_not(c.hasdn))
                def _():
                    s._wait(z2,r2); s._sum(srcs+[z2],s.out.at[k],s.scale)
        for f in prev: f()
        s._load(i+s.nst-1)
    def _finish(s):
        s._flush()
        for n,valid in s.waits:
            w=functools.partial(s._wait,s.S.at[0],s.ss.at[n])
            if valid is None: w()
            else: pl.when(valid)(w)
        def sw(i,_):
            s._wait(s.S.at[0],s.sS.at[i]); return 0
        lax.fori_loop(0,s.S.shape[0],sw,0)
def reduce_kernel(*refs,lo,hi,ranges,scale):
    n=len(ranges)
    parts=[(a,b,r) for (a,b),r in zip(ranges,refs[:n])]
    out=refs[n]; scr=refs[n+1:]
    c=Ctx()
    rd=Reduce(c,lo,hi,parts,out,scr,scale)
    c.barrier()
    rd.send_sibling(); rd.prefetch()
    for st in rd.steps: st()
def reduce_(arrs,lo,hi,ranges,scale,cid=2):
    return pl.pallas_call(functools.partial(reduce_kernel,lo=lo,hi=hi,ranges=ranges,scale=scale),out_shape=jax.ShapeDtypeStruct((3,128,1024),F32),
       in_specs=[pl.BlockSpec(memory_space=pl.ANY)]*len(arrs),out_specs=pl.BlockSpec(memory_space=pltpu.VMEM),
       scratch_shapes=Reduce.scratch(lo,hi),
       compiler_params=pltpu.CompilerParams(collective_id=cid,has_side_effects=True,vmem_limit_bytes=60<<20),name=f"reduce{lo}{hi}")(*arrs)


def qkv_kernel(x_ref, vec_ref, w_ref, out_ref, n_ref):
    j = pl.program_id(0)

    @pl.when(j == 0)
    def _():
        for i in range(2):

            def block(rows, dst):
                v = x_ref[i, rows, :].astype(F32)
                c = v - jnp.mean(v, axis=1, keepdims=True)
                rc = lax.rsqrt(jnp.mean(c * c, axis=1, keepdims=True) + EPS)
                return (c * rc * (1.0 + vec_ref[8:9, :]) + vec_ref[9:10, :]).astype(BF)

            def one(c, _):
                n_ref[i, rows_at(c), :] = block(rows_at(c), None)
                return 0

            lax.fori_loop(0, 18, one, 0)
            last = block(slice(576, 577), None).astype(F32)
            n_ref[i, 576:592, :] = jnp.concatenate([last, jnp.zeros((15, D), F32)], axis=0).astype(BF)

    w = w_ref[...].reshape(D, D)
    bias = jnp.where(j == 0, vec_ref[0:1, :], jnp.where(j == 2, vec_ref[1:2, :], 0.0))
    for i in range(2):
        out_ref[0, i] = (nn(n_ref[i], w) + bias).astype(BF)


def qkv(x, vec, w):
    return pl.pallas_call(
        qkv_kernel,
        grid=(3,),
        in_specs=[full((2, S, D)), full((16, D)), pl.BlockSpec((8, 1, 128, D), lambda j: (0, j, 0, 0))],
        out_specs=[pl.BlockSpec((1, 2, SQ, D), lambda j: (j, 0, 0, 0)), full((2, SQ, D))],
        out_shape=[jax.ShapeDtypeStruct((3, 2, SQ, D), BF), jax.ShapeDtypeStruct((2, SQ, D), BF)],
        compiler_params=pltpu.CompilerParams(vmem_limit_bytes=VMEM_ALL),
        name="qkv",
    )(x, vec, w.reshape(32, 3, 128, D))


def padded(v):
    return jnp.concatenate([v, jnp.zeros((640 - SQ, 128), v.dtype)], axis=0)


def attend_pair(q, k, v):
    lane = lax.broadcasted_iota(jnp.int32, (1, 128), 1)
    k = padded(k)
    v = padded(v)
    outs = []
    for h in range(2):
        mine = lane < 64 if h == 0 else lane >= 64
        s = nt(jnp.where(mine, q, jnp.zeros_like(q)), k)
        s = jnp.concatenate([s[:, :512], jnp.where(lane < S - 512, s[:, 512:], -1e30)], axis=1)
        top = jnp.max(s, axis=1, keepdims=True)
        p = jnp.exp2((s - top) * SCORE)
        total = jnp.sum(p, axis=1, keepdims=True)
        outs.append(nn(p.astype(BF), v) * (1.0 / total))
    return jnp.where(lane < 64, outs[0], outs[1]).astype(BF)


def attend_kernel(q_ref, k_ref, v_ref, o_ref):
    half = SQ // 2
    for r in range(2):
        rows = slice(r * half, (r + 1) * half)
        o_ref[0, rows, :] = attend_pair(q_ref[0, 0, rows, :], k_ref[0, 0], v_ref[0, 0])


def attend(z):
    spec = lambda j: pl.BlockSpec((1, 1, SQ, 128), lambda i, h: (j, i, 0, h))
    return pl.pallas_call(
        attend_kernel,
        grid=(2, 8),
        in_specs=[spec(0), spec(1), spec(2)],
        out_specs=pl.BlockSpec((1, SQ, 128), lambda i, h: (i, 0, h)),
        out_shape=jax.ShapeDtypeStruct((2, SQ, D), BF),
        compiler_params=pltpu.CompilerParams(vmem_limit_bytes=VMEM_ALL),
        name="attend",
    )(z, z, z)


def attend_back_pair(q, k, v, do):
    lane = lax.broadcasted_iota(jnp.int32, (1, 128), 1)
    real = lax.broadcasted_iota(jnp.int32, (16, 1), 0) < S - 576
    q = padded(q)
    do = padded(do)
    dqs, dks, dvs = [], [], []
    for h in range(2):
        mine = lane < 64 if h == 0 else lane >= 64
        s = nt(jnp.where(mine, k, jnp.zeros_like(k)), q)
        s = jnp.concatenate([s[:576], jnp.where(real, s[576:], -1e30)], axis=0)
        top = jnp.max(s, axis=0, keepdims=True)
        p = jnp.exp2((s - top) * SCORE)
        p = p * (1.0 / jnp.sum(p, axis=0, keepdims=True))
        dvs.append(nn(p.astype(BF), do))
        dp = nt(jnp.where(mine, v, jnp.zeros_like(v)), do)
        ds = (p * (dp - jnp.sum(p * dp, axis=0, keepdims=True))).astype(BF)
        dks.append(nn(ds, q))
        dqs.append(tn(ds, k))
    pick = lambda pair, scale: (jnp.where(lane < 64, pair[0], pair[1]) * scale).astype(BF)
    return pick(dqs, 0.125)[:SQ], pick(dks, 0.125), pick(dvs, 1.0)


def attend_back_kernel(q_ref, k_ref, v_ref, do_ref, out_ref):
    dq, dk, dv = attend_back_pair(q_ref[0, 0], k_ref[0, 0], v_ref[0, 0], do_ref[0])
    out_ref[0, 0] = dq
    out_ref[1, 0] = dk
    out_ref[2, 0] = dv


def attend_back(z, do):
    spec = lambda j: pl.BlockSpec((1, 1, SQ, 128), lambda i, h: (j, i, 0, h))
    return pl.pallas_call(
        attend_back_kernel,
        grid=(2, 8),
        in_specs=[spec(0), spec(1), spec(2), pl.BlockSpec((1, SQ, 128), lambda i, h: (i, 0, h))],
        out_specs=pl.BlockSpec((3, 1, SQ, 128), lambda i, h: (0, i, 0, h)),
        out_shape=jax.ShapeDtypeStruct((3, 2, SQ, D), BF),
        compiler_params=pltpu.CompilerParams(vmem_limit_bytes=VMEM_ALL),
        name="attend_back",
    )(z, z, z, do)


def mlp_kernel(x_ref,g_ref,mix_ref,vec_ref,wo_ref,wu_ref,wd_ref,
               out_ref,gup_ref,gdn_ref,gout_ref,dmix_ref,dhid_ref,gvec_ref,
               n2,gs,acc,dn,stat,*,FB,NB):
    jb=pl.program_id(0)
    hid=dhid_ref
    @pl.when(jb==0)
    def _():
        wo=wo_ref[...].reshape(D,D)
        for i in range(2):
            hid[i*SQ:(i+1)*SQ,:]=nn(mix_ref[i],wo)
            gs[i*SQ:i*SQ+576,:]=g_ref[i,:576,:]
            gs[i*SQ+576:(i+1)*SQ,:]=jnp.concatenate([g_ref[i,576:577,:].astype(F32),jnp.zeros((15,D),F32)],axis=0).astype(BF)
            def addx(c,_):
                r=pl.multiple_of(c*CH,CH)
                hid[pl.ds(i*SQ+r,CH),:]+=x_ref[i,pl.ds(r,CH),:].astype(F32)+vec_ref[2:3,:]
                return 0
            lax.fori_loop(0,18,addx,0)
            hid[i*SQ+576:i*SQ+577,:]+=x_ref[i,576:577,:].astype(F32)+vec_ref[2:3,:]
        acc[...]=jnp.zeros_like(acc); dn[...]=jnp.zeros_like(dn)
        gvec_ref[...]=jnp.zeros_like(gvec_ref)
        def ln(c,_):
            r=pl.ds(pl.multiple_of(c*CH,CH),CH)
            h=hid[r,:]
            mu=jnp.mean(h,axis=1,keepdims=True)
            ce=h-mu
            rc=lax.rsqrt(jnp.mean(ce*ce,axis=1,keepdims=True)+EPS)
            n2[r,:]=(ce*rc*(1.0+vec_ref[10:11,:])+vec_ref[11:12,:]).astype(BF)
            stat[r,0:1]=mu; stat[r,1:2]=rc
            return 0
        lax.fori_loop(0,M//CH,ln,0)
        def gsum(c,a):
            r=pl.ds(pl.multiple_of(c*CH,CH),CH)
            return a+gs[r,:].astype(F32)
        t=lax.fori_loop(0,M//CH,gsum,jnp.zeros((CH,D),F32))
        gvec_ref[7:8,:]=jnp.sum(t,axis=0,keepdims=True)
    wu=wu_ref[...].reshape(D,FB); wd=wd_ref[...].reshape(FB,D)
    nper=D//FB
    row=vec_ref[pl.ds(3+jb//nper,1),:]
    bup=row[:,:FB]
    for t in range(1,nper): bup=jnp.where(jb%nper==t,row[:,t*FB:(t+1)*FB],bup)
    g=gs[...]; n=n2[...]
    pre=nn(n,wu)+bup
    cdf=0.5*(1.0+lax.erf(pre*0.7071067811865476))
    act=(pre*cdf).astype(BF)
    slope=cdf+pre*0.3989422804014327*jnp.exp(-0.5*pre*pre)
    dpf=nt(g,wd)*slope
    dp=dpf.astype(BF)
    acc[...]+=nn(act,wd)
    dn[...]+=nt(dp,wu)
    gup_ref[...]=tn(n,dp).astype(BF).reshape(gup_ref.shape)
    gdn_ref[...]=tn(act,g).astype(BF).reshape(gdn_ref.shape)
    bsum=jnp.sum(dp.astype(F32),axis=0,keepdims=True)
    for t in range(nper):
        @pl.when(jb%nper==t)
        def _(): gvec_ref[pl.ds(3+jb//nper,1),t*FB:(t+1)*FB]=bsum
    @pl.when(jb==NB-1)
    def _():
        for i in range(2):
            def ob(c,_):
                r=pl.multiple_of(c*CH,CH)
                out_ref[i,pl.ds(r,CH),:]=(hid[pl.ds(i*SQ+r,CH),:]+(acc[pl.ds(i*SQ+r,CH),:]+vec_ref[7:8,:])).astype(BF)
                return 0
            lax.fori_loop(0,18,ob,0)
            out_ref[i,576:577,:]=(hid[i*SQ+576:i*SQ+577,:]+(acc[i*SQ+576:i*SQ+577,:]+vec_ref[7:8,:])).astype(BF)
        def bk(c,car):
            a,b,d=car
            r=pl.ds(pl.multiple_of(c*CH,CH),CH)
            mu=stat[r,0:1]; rc=stat[r,1:2]
            xh=(hid[r,:]-mu)*rc
            dd=dn[r,:]
            e=dd*(1.0+vec_ref[10:11,:])
            dh=gs[r,:].astype(F32)+rc*(e-jnp.mean(e,axis=1,keepdims=True)-xh*jnp.mean(e*xh,axis=1,keepdims=True))
            dhid_ref[r,:]=dh
            db=dh.astype(BF)
            n2[r,:]=db
            return (a+dd*xh,b+dd,d+db.astype(F32))
        zz=jnp.zeros((CH,D),F32)
        a,b,d=lax.fori_loop(0,M//CH,bk,(zz,zz,zz))
        gvec_ref[10:11,:]=jnp.sum(a,axis=0,keepdims=True)
        gvec_ref[11:12,:]=jnp.sum(b,axis=0,keepdims=True)
        gvec_ref[2:3,:]=jnp.sum(d,axis=0,keepdims=True)
        db=n2[...]
        wo=wo_ref[...].reshape(D,D)
        dmix_ref[...]=nt(db,wo).astype(BF).reshape(2,SQ,D)
        gout_ref[...]=tn(mix_ref[...].reshape(M,D),db).astype(BF).reshape(8,128,D)
def mlp(x,g,mix,vec,W,FB=512):
    NB=4096//FB; nper=D//FB
    W4=W.reshape(96,4,32,1024)
    return pl.pallas_call(functools.partial(mlp_kernel,FB=FB,NB=NB),grid=(NB,),
      in_specs=[full((2,S,D)),full((2,S,D)),full((2,SQ,D)),full((16,D)),
        pl.BlockSpec((8,128,D),lambda j:(3,0,0),pipeline_mode=pl.Buffered(1)),
        pl.BlockSpec((32,1,32,FB),lambda j:(1,j//nper,0,j%nper)),
        pl.BlockSpec((FB//128,128,D),lambda j:(64//(FB//128)+j,0,0))],
      out_specs=[full((2,S,D)),pl.BlockSpec((32,1,32,FB),lambda j:(0,j//nper,0,j%nper)),
        pl.BlockSpec((FB//128,128,D),lambda j:(j,0,0)),full((8,128,D)),full((2,SQ,D)),full((M,D)),full((16,D))],
      out_shape=[jax.ShapeDtypeStruct((2,S,D),BF),jax.ShapeDtypeStruct((32,4,32,D),BF),jax.ShapeDtypeStruct((32,128,D),BF),
        jax.ShapeDtypeStruct((8,128,D),BF),jax.ShapeDtypeStruct((2,SQ,D),BF),jax.ShapeDtypeStruct((M,D),F32),jax.ShapeDtypeStruct((16,D),F32)],
      scratch_shapes=[pltpu.VMEM((M,D),BF),pltpu.VMEM((M,D),BF),pltpu.VMEM((M,D),F32),pltpu.VMEM((M,D),F32),pltpu.VMEM((M,128),F32)],
      compiler_params=pltpu.CompilerParams(vmem_limit_bytes=67043328),name=f"mlp{FB}")(x,g,mix,vec,W,W4,W)


def tail_kernel(x_ref, dz_ref, n_ref, dhid_ref, vec_ref, w_ref, gvin_ref, gx_ref, gw_ref, gvec_ref, acc):
    j = pl.program_id(0)

    @pl.when(j == 0)
    def _():
        gvec_ref[...] = gvin_ref[...]
        acc[...] = jnp.zeros_like(acc)

    w = w_ref[...].reshape(D, D)
    dz = dz_ref[0].reshape(M, D)
    acc[...] += nt(dz, w)
    gw_ref[...] = tn(n_ref[...].reshape(M, D), dz).astype(BF).reshape(8, 1, 128, D)

    @pl.when(j != 1)
    def _():
        def add(c, t):
            return t + dz_ref[0, 0, pl.ds(c * 16, 16), :].astype(F32) + dz_ref[0, 1, pl.ds(c * 16, 16), :].astype(F32)

        t = lax.fori_loop(0, SQ // 16, add, jnp.zeros((16, D), F32))
        gvec_ref[pl.ds(j // 2, 1), :] = jnp.sum(t, axis=0, keepdims=True)

    @pl.when(j == 2)
    def _():
        def back(x, dd, dh):
            v = x.astype(F32)
            ce = v - jnp.mean(v, axis=1, keepdims=True)
            rc = lax.rsqrt(jnp.mean(ce * ce, axis=1, keepdims=True) + EPS)
            xh = ce * rc
            e = dd * (1.0 + vec_ref[8:9, :])
            g = dh + rc * (e - jnp.mean(e, axis=1, keepdims=True) - xh * jnp.mean(e * xh, axis=1, keepdims=True))
            return g.astype(BF), dd * xh, dd

        a = b = jnp.zeros((CH, D), F32)
        la = lb = jnp.zeros((1, D), F32)
        for i in range(2):

            def one(c, carry):
                r = rows_at(c)
                r2 = pl.ds(pl.multiple_of(i * SQ + c * CH, 16), CH)
                g, s1, s2 = back(x_ref[i, r, :], acc[r2, :], dhid_ref[r2, :])
                gx_ref[i, r, :] = g
                return carry[0] + s1, carry[1] + s2

            a, b = lax.fori_loop(0, 18, one, (a, b))
            r2 = slice(i * SQ + 576, i * SQ + 577)
            g, s1, s2 = back(x_ref[i, 576:577, :], acc[r2, :], dhid_ref[r2, :])
            gx_ref[i, 576:577, :] = g
            la, lb = la + s1, lb + s2
        gvec_ref[8:9, :] = jnp.sum(a, axis=0, keepdims=True) + la
        gvec_ref[9:10, :] = jnp.sum(b, axis=0, keepdims=True) + lb


def tail(x, dz, n1, dhid, vec, w, gvec):
    return pl.pallas_call(
        tail_kernel,
        grid=(3,),
        in_specs=[
            full((2, S, D)),
            pl.BlockSpec((1, 2, SQ, D), lambda j: (j, 0, 0, 0)),
            full((2, SQ, D)),
            full((M, D)),
            full((16, D)),
            pl.BlockSpec((8, 1, 128, D), lambda j: (0, j, 0, 0)),
            full((16, D)),
        ],
        out_specs=[full((2, S, D)), pl.BlockSpec((8, 1, 128, D), lambda j: (0, j, 0, 0)), full((16, D))],
        out_shape=[
            jax.ShapeDtypeStruct((2, S, D), BF),
            jax.ShapeDtypeStruct((8, 3, 128, D), BF),
            jax.ShapeDtypeStruct((16, D), F32),
        ],
        scratch_shapes=[pltpu.VMEM((M, D), F32)],
        compiler_params=pltpu.CompilerParams(vmem_limit_bytes=VMEM_ALL),
        name="tail",
    )(x, dz, n1, dhid, vec, w.reshape(32, 3, 128, D), gvec)


def to_pieces(rows, first):
    n = rows.shape[0] // 128
    plain = rows.reshape(n, 128, D)
    three = rows.reshape(n // 3, 128, 3, D).transpose(0, 2, 1, 3).reshape(n, 128, D)
    four = rows.reshape(n, 32, 4, D).transpose(0, 2, 1, 3).reshape(n, 128, D)
    p = first + lax.broadcasted_iota(jnp.int32, (n, 1, 1), 0)
    return jnp.where(p < 24, three, jnp.where((p >= 32) & (p < 64), four, plain))


def from_pieces(pieces, first):
    n = pieces.shape[0]
    plain = pieces.reshape(n * 128, D)
    three = pieces.reshape(n // 3, 3, 128, D).transpose(0, 2, 1, 3).reshape(n * 128, D)
    four = pieces.reshape(n, 4, 32, D).transpose(0, 2, 1, 3).reshape(n * 128, D)
    p = first + lax.broadcasted_iota(jnp.int32, (n * 128, 1), 0) // 128
    return jnp.where(p < 24, three, jnp.where((p >= 32) & (p < 64), four, plain))


def update(params, moment_one, moment_two, weight_grad, square_sum):
    clip_factor = jnp.minimum(1.0, max_norm / (jnp.sqrt(square_sum) + 1e-06))
    clipped = clip_factor * weight_grad
    moment_one_new = beta_one * moment_one + (1.0 - beta_one) * clipped
    moment_two_new = beta_two * moment_two + (1.0 - beta_two) * clipped * clipped
    correct_one = 1.0 - beta_one**STEP
    correct_two = 1.0 - beta_two**STEP
    params_new = params - learn_rate * (
        moment_one_new / correct_one / (jnp.sqrt(moment_two_new / correct_two) + adam_eps) + decay_rate * params
    )
    return params_new, moment_one_new, moment_two_new


def shards(tokens, cotangent, params, moment_one, moment_two):
    n = lax.axis_size("dp")
    me = lax.axis_index("dp")
    shard_len = params.shape[0]
    images_all = tokens.shape[0] * n
    mats = PIECES * 128 * D
    quick = n == 32
    if quick:
        unit = 128
        extra = 12 * D // unit
        own_units = shard_len // unit
        gap = extra // n
        low = params.reshape(own_units, unit)
        before = lax.ppermute(low[own_units - extra :].astype(BF), "dp", [(i, (i + 1) % n) for i in range(n)])
        joined = jnp.concatenate([before.astype(F32), low], axis=0)
        aligned = lax.dynamic_slice(joined, (extra - gap * me, 0), (own_units - gap, unit))
        own = to_pieces(aligned.reshape(-1, D), 3 * me).astype(BF)
        vec_own = low[own_units - extra :].reshape(12, D).astype(BF).astype(F32)
        vec = lax.psum(jnp.where(me == n - 1, vec_own, 0.0), "dp")
        w = gather(own)
    else:
        flat = lax.all_gather(params.astype(BF), "dp", axis=0, tiled=True)
        w = to_pieces(flat[:mats].reshape(-1, D), 0)
        vec = flat[mats:].reshape(12, D).astype(F32)
    vec = jnp.pad(vec, ((0, 4), (0, 0)))
    z, n1 = qkv(tokens, vec, w)
    mixed = attend(z)
    outputs, gup, gdn, gout, dmix, dhid, gvec = mlp(tokens, cotangent, mixed, vec, w)
    dz = attend_back(z, dmix)
    grad_tokens, gqkv, gvec = tail(tokens, dz, n1, dhid, vec, w, gvec)
    parts = [gqkv.reshape(24, 128, D), gout, gup.reshape(32, 128, D), gdn]
    if quick:
        chunk = reduce_(parts, 0, 3, [(0, 24), (24, 32), (32, 64), (64, 96)], 1.0 / images_all)
        gv = lax.psum(gvec[:12], "dp") / images_all
        rows = from_pieces(chunk, 3 * me).reshape(own_units - gap, unit)
        after = lax.ppermute(rows[:extra], "dp", [(i, (i - 1) % n) for i in range(n)])
        after = jnp.where(me == n - 1, gv.reshape(extra, unit), after)
        joined = jnp.concatenate([rows, after], axis=0)
        weight_grad = lax.dynamic_slice(joined, (gap * me, 0), (own_units, unit)).reshape(shard_len)
    else:
        flat = jnp.concatenate([from_pieces(jnp.concatenate(parts, axis=0), 0).reshape(-1), gvec[:12].reshape(-1).astype(BF)])
        arrived = lax.all_to_all(flat.reshape(n, shard_len), "dp", split_axis=0, concat_axis=0, tiled=True)
        weight_grad = jnp.sum(arrived.astype(F32), axis=0) / images_all
    square_sum = lax.psum(jnp.sum(weight_grad * weight_grad), "dp")
    news = update(params, moment_one, moment_two, weight_grad, square_sum)
    return (outputs, grad_tokens, weight_grad, *news)


def solution(mesh):
    in_specs = (P("dp", None, None), P("dp", None, None), P("dp"), P("dp"), P("dp"))
    out_specs = (P("dp", None, None), P("dp", None, None), P("dp"), P("dp"), P("dp"), P("dp"))
    return jax.shard_map(shards, mesh=mesh, in_specs=in_specs, out_specs=out_specs, check_vma=False)
```

time: 2370 us -> 692 us (0.29)
  waiting for transfers between devices: 799 us -> 0.01 us
  other arithmetic: 697 us -> 14.4 us
  Pallas kernels: 0 us -> 502 us
  local copies, waits for them, and re-layouts: 488 us -> 36.8 us
  matrix products: 321 us -> 0 us
  blocking collectives: 37 us -> 126 us
    all_to_all x1 -> x0, waiting for transfers between devices: 534 us -> none  [shards(): lax.all_to_all(local_grad.reshape(dev_count, shard_len).astype(jnp.bfloat...]
    pallas_call x0 -> x7, Pallas kernels: none -> 502 us  [the longest x1 150 us: reduce_(): pl.pallas_call(functools.partial(reduce_kernel, lo=lo, hi=hi, ranges=rang...]
    unnamed x300 -> x34, local copies, waits for them, and re-layouts: 357 us -> 17.8 us
    dot_general x36 -> x0, matrix products: 321 us -> none  [the longest x2 30.2 us: attend_back(): jnp.einsum('qhd,khd->hqk', d_heads, heads_v, preferred_element_type=jnp.f...]
    reduce_sum x14 -> x0, other arithmetic: 302 us -> none  [the longest x1 261 us: shards(): shard_grad = jnp.sum(arrived, axis=0)]
    all_gather x1 -> x0, waiting for transfers between devices: 265 us -> none  [shards(): front_weights = lax.all_gather(shard_low, 'dp', axis=0, tiled=True)]
    convert_element_type x9 -> x1, other arithmetic: 237 us -> 1.49 us  [shards(): own = to_pieces(aligned.reshape(-1, D), 3 * me).astype(BF)]
    all_gather x1 -> x0, other arithmetic: 149 us -> none  [shards(): front_weights = lax.all_gather(shard_low, 'dp', axis=0, tiled=True)]
  transfers between devices with their start and end apart: 2 -> 2, of which waited for: 2 -> 0; matrix products, arithmetic and copies ran while one was open for 2% -> 3% of each run, Pallas kernels for 0% -> 0%
where the time goes in v1:
time: 692 us; the launch traced here: 684 us
  Pallas kernels  502 us (73%)
  blocking collectives  126 us (18%)
  local copies, waits for them, and re-layouts  36.8 us (5%)
  other arithmetic  14.4 us (2%)
    pallas_call x1, Pallas kernels, reduce_(): pl.pallas_call(functools.partial(reduce_kernel, lo=lo, hi=hi, ranges=rang...  150 us
    pallas_call x1, Pallas kernels, gather(): pl.pallas_call(gather_kernel, out_shape=jax.ShapeDtypeStruct((96, 128, 10...  110 us
    pallas_call x1, Pallas kernels, mlp(): pl.pallas_call(functools.partial(mlp_kernel, FB=FB, NB=NB), grid=(NB,), i...  106 us
    pallas_call x1, Pallas kernels, attend_back(): pl.pallas_call(attend_back_kernel, grid=(2, 8), in_specs=[spec(0), spec(1...  52.9 us
    psum x1, blocking collectives, shards(): gv = lax.psum(gvec[:12], 'dp') / images_all  46.4 us
    psum x1, blocking collectives, shards(): vec = lax.psum(jnp.where(me == n - 1, vec_own, 0.0), 'dp')  41.9 us
    psum x1, blocking collectives, shards(): square_sum = lax.psum(jnp.sum(weight_grad * weight_grad), 'dp')  37.6 us
    pallas_call x1, Pallas kernels, tail(): pl.pallas_call(tail_kernel, grid=(3,), in_specs=[full((2, S, D)), pl.Bloc...  36.5 us
  transfers between devices with their start and end apart: 2, of which 0 were waited for; matrix products, arithmetic and copies ran while one was open for 3% of the time, Pallas kernels for 0%

profile of v1, /device:TPU:0, one launch (start us, length us, event | category | flops | bytes accessed | tf_op | source)
XLA Modules:
  0.0 684.0 jit_solution(7238517728740435378)
XLA Ops:
  0.6 0.8 fusion.5
  1.9 0.8 convert_select_fusion
  2.8 3.9 copy.22.x_ref
  6.8 2.1 copy.23.g_ref
  10.6 41.9 %psum.21 = f32[12,1024]{1,0:T(8,128)S(1)} all-reduce(f32[12,1024]{1,0:T(8,128)S(1)} %select_n.60), channel_id=1, replica_groups=mesh['dp'=32] {'dp'}, use_global_device_ids=true, to_apply=%region_0.1 | all-reduce | flops 12288 | bytes 98304 | tf_op jit(solution)/shard_map/psum | solution.py:682
  53.6 1.2 reshape_reshape.11
  55.5 0.9 copy-done.5
  56.4 1.5 fusion.3.own_ref
  57.9 110.1 %gather.1.wo_ref.wd_ref = bf16[96,128,1024]{2,1,0:T(8,128)(2,1)} custom-call(bf16[3,128,1024]{2,1,0:T(8,128)(2,1)} %fusion.3.own_ref), custom_call_target="tpu_custom_call" | custom-call | tf_op jit(solution)/shard_map/gather/pallas_call | solution.py:161
  167.9 19.4 %qkv.1 = (bf16[3,2,592,1024]{3,2,1,0:T(8,128)(2,1)}, bf16[2,592,1024]{2,1,0:T(8,128)(2,1)}) custom-call(bf16[2,577,1024]{2,1,0:T(8,128)(2,1)} %copy.22.x_ref, f32[16,1024]{1,0:T(8,128)} %pad.4.vec_ref, bf16[32,3,128,1024]{3,2,1,0:T(8,128)(2,1)} %bitcast.31), custom_call_target="tpu_custom_call" | custom-call | tf_op jit(solution)/shard_map/qkv/pallas_call | solution.py:362
  187.4 26.9 %attend.1.mix_ref = bf16[2,592,1024]{2,1,0:T(8,128)(2,1)} custom-call(bf16[3,2,592,1024]{3,2,1,0:T(8,128)(2,1)} %get-tuple-element.18.q_ref.k_ref.v_ref, bf16[3,2,592,1024]{3,2,1,0:T(8,128)(2,1)} %get-tuple-element.18.q_ref.k_ref.v_ref, bf16[3,2,592,1024]{3,2,1,0:T(8,128)(2,1)} %get-tuple-element.18.q_ref.k_ref.v_ref), custom_call_target="tpu_custom_call" | custom-call | tf_op jit(solution)/shard_map/attend/pallas_call | solution.py:402
  214.3 105.7 %mlp512.1 = (bf16[2,577,1024]{2,1,0:T(8,128)(2,1)}, bf16[32,4,32,1024]{3,2,1,0:T(8,128)(2,1)}, bf16[32,128,1024]{2,1,0:T(8,128)(2,1)}, bf16[8,128,1024]{2,1,0:T(...) custom-call(bf16[2,577,1024]{2,1,0:T(8,128)(2,1)} %copy.22.x_ref, ...), custom_call_target="tpu_custom_call" | custom-call | tf_op jit(solution)/shard_map/mlp512/pallas_call | solution.py:543
  320.0 52.9 %attend_back.1.dz_ref = bf16[3,2,592,1024]{3,2,1,0:T(8,128)(2,1)} custom-call(bf16[3,2,592,1024]{3,2,1,0:T(8,128)(2,1)} %get-tuple-element.18.q_ref.k_ref.v_ref, bf16[3,2,592,1024]{3,2,1,0:T(8,128)(2,1)} %get-tuple-element.18.q_ref.k_ref.v_ref, bf16[3,2,592,1024]{3,2,1,0:T(8,128)(2,1)} %get-tuple-element.18.q_ref.k_ref.v_ref, ...), custom_call_target="tpu_custom_call" | custom-call | tf_op jit(solution)/shard_map/attend_back/pallas_call | solution.py:444
  372.9 36.5 %tail.1 = (bf16[2,577,1024]{2,1,0:T(8,128)(2,1)}, bf16[8,3,128,1024]{3,2,1,0:T(8,128)(2,1)}, f32[16,1024]{1,0:T(8,128)}) custom-call(bf16[2,577,1024]{2,1,0:T(8,128)(2,1)} %copy.22.x_ref, bf16[3,2,592,1024]{3,2,1,0:T(8,128)(2,1)} %attend_back.1.dz_ref, bf16[2,592,1024]{2,1,0:T(8,128)(2,1)} %get-tuple-element.21.n_ref, ...), custom_call_target="tpu_custom_call" | custom-call | tf_op jit(solution)/shard_map/tail/pallas_call | solution.py:609
  409.4 150.4 %reduce03.1 = f32[3,128,1024]{2,1,0:T(8,128)} custom-call(bf16[24,128,1024]{2,1,0:T(8,128)(2,1)} %bitcast.39, bf16[8,128,1024]{2,1,0:T(8,128)(2,1)} %get-tuple-element.26.refs_1_, bf16[32,128,1024]{2,1,0:T(8,128)(2,1)} %bitcast.37, bf16[32,128,1024]{2,1,0:T(8,128)(2,1)} %get-tuple-element.28.refs_3_), custom_call_target="tpu_custom_call" | custom-call | tf_op jit(solution)/shard_map/reduce03/pallas_call | solution.py:328
  559.8 2.5 copy.25
  562.3 1.3 copy-done.1
  563.6 1.7 reshape.160
  565.3 3.9 reshape.155
  569.2 1.0 copy.26
  570.2 1.7 reshape.161
  571.9 1.8 reshape.157
  573.7 1.4 reshape.158
  575.1 46.4 %psum.22 = f32[12,1024]{1,0:T(8,128)S(1)} all-reduce(f32[12,1024]{1,0:T(8,128)S(1)} %bitcast.41), channel_id=1, replica_groups=mesh['dp'=32] {'dp'}, use_global_device_ids=true, to_apply=%region_1.2 | all-reduce | flops 12288 | bytes 98304 | tf_op jit(solution)/shard_map/psum | solution.py:697
  621.6 1.0 slice_select_fusion
  622.5 2.7 collective-permute-start.1
  625.2 4.0 select_select_fusion
  629.3 3.8 copy.29
  633.2 1.3 multiply_reduce_fusion
  634.5 5.6 copy.30
  640.1 37.6 %psum.23 = f32[]{:T(128)} all-reduce(f32[]{:T(128)} %multiply_reduce_fusion), channel_id=1, replica_groups=mesh['dp'=32] {'dp'}, use_global_device_ids=true, to_apply=%region_3.4 | all-reduce | flops 1 | bytes 8 | tf_op jit(solution)/shard_map/psum | solution.py:707
  678.5 5.3 multiply_subtract_fusion
  (47 shorter events, 4.1 us)
Async XLA Ops:
  1.5 51.7 %collective-permute-start = (bf16[96,128]{1,0:T(8,128)(2,1)S(1)}, bf16[96,128]{1,0:T(8,128)(2,1)S(1)}, u32[]{:S(2)}, u32[]{:S(2)}) collective-permute-start(bf16[96,128]{1,0:T(8,128)(2,1)S(1)} %fusion.5), channel_id=1, source_target_pairs={{0,1},{1,2},{2,3},{3,4},{4,5},{5,6},{6,7},{7,8},{8,9},{9,10},{10,1... | collective-permute-start | bytes 73736 | tf_op jit(solution)/shard_map/ppermute | solution.py:677
  2.8 6.1 copy-start.11
  2.8 7.0 %copy-start.13 = (pred[384]{0:T(512)(128)(4,1)}, pred[384]{0:T(512)(128)(4,1)S(1)}, u32[]{:S(2)}) copy-start(pred[384]{0:T(512)(128)(4,1)S(1)} %get-tuple-element.47) | copy-start | bytes 1156
  2.8 4.0 copy-start.7
  6.8 46.4 %copy-start.2 = (f32[393600]{0:T(1024)S(1)}, f32[393600]{0:T(1024)}, u32[]{:S(2)}) copy-start(f32[393600]{0:T(1024)} %param.7) | copy-start | bytes 4723204
  55.2 1.1 copy-start.5
  562.3 1.3 copy-start.1
  565.3 3.9 copy-start
  573.7 1.4 copy-start.8
  573.7 47.9 %copy-start.12 = (pred[384]{0:T(512)(128)(4,1)S(1)}, pred[384]{0:T(512)(128)(4,1)}, u32[]{:S(2)}) copy-start(pred[384]{0:T(512)(128)(4,1)} %copy-done.11) | copy-start | bytes 1156
  573.7 47.9 %copy-start.14 = (pred[384]{0:T(512)(128)(4,1)S(1)}, pred[384]{0:T(512)(128)(4,1)}, u32[]{:S(2)}) copy-start(pred[384]{0:T(512)(128)(4,1)} %copy-done.13) | copy-start | bytes 1156
  573.7 51.5 %copy-start.4 = (f32[3072,128]{1,0:T(8,128)S(1)}, f32[3072,128]{1,0:T(8,128)}, u32[]{:S(2)}) copy-start(f32[3072,128]{1,0:T(8,128)} %reshape.155) | copy-start | bytes 4718596
  573.7 51.5 %copy-start.9 = (pred[3072]{0:T(1024)(128)(4,1)S(1)}, pred[3072]{0:T(1024)(128)(4,1)}, u32[]{:S(2)}) copy-start(pred[3072]{0:T(1024)(128)(4,1)} %broadcast_in_dim.49) | copy-start | bytes 9220
  573.7 51.5 %copy-start.10 = (pred[3072]{0:T(1024)(128)(4,1)S(1)}, pred[3072]{0:T(1024)(128)(4,1)}, u32[]{:S(2)}) copy-start(pred[3072]{0:T(1024)(128)(4,1)} %broadcast_in_dim.46) | copy-start | bytes 9220
  622.5 10.6 %collective-permute-start.1 = (f32[96,128]{1,0:T(8,128)S(1)}, f32[96,128]{1,0:T(8,128)S(1)}, u32[]{:S(2)}, u32[]{:S(2)}) collective-permute-start(f32[96,128]{1,0:T(8,128)S(1)} %slice.25), channel_id=1, source_target_pairs={{0,31},{1,0},{2,1},{3,2},{4,3},{5,4},{6,5},{7,6},{8,7},{9,8},{10,9... | collective-permute-start | bytes 147464 | tf_op jit(solution)/shard_map/ppermute | solution.py:699
  625.2 4.1 copy-start.6
  634.5 44.0 %copy-start.3 = (f32[393600]{0:T(1024)S(1)}, f32[393600]{0:T(1024)}, u32[]{:S(2)}) copy-start(f32[393600]{0:T(1024)} %param.7) | copy-start | bytes 4723204

commit v2 on v1

--- a/solution.py
+++ b/solution.py
@@ -19,6 +19,10 @@
 F32 = jnp.float32
 MESH = pl.DeviceIdType.MESH
 VMEM_ALL = 67043328
+EARLY = 1
+PER = 2
+FRONT_HI = 3
+BPER = 3
 
 EPS = 1e-06
 max_norm = 1.0
@@ -62,273 +66,404 @@
         s.abit=s.x+(s.y-s.x)*s.core; s.bbit=s.y+(s.x-s.y)*s.core
         s.up=me+8; s.dn=me-8
         s.hasup=s.z<3; s.hasdn=s.z>0
-    def barrier(s):
+    def barrier(s,extra=None):
         bar=pltpu.get_barrier_semaphore()
         for p in (s.sib,s.ap,s.bp): pl.semaphore_signal(bar,inc=1,device_id=(p,),device_id_type=MESH)
         @pl.when(s.hasup)
         def _(): pl.semaphore_signal(bar,inc=1,device_id=(s.up,),device_id_type=MESH)
         @pl.when(s.hasdn)
         def _(): pl.semaphore_signal(bar,inc=1,device_id=(s.dn,),device_id_type=MESH)
-        pl.semaphore_wait(bar,3+jnp.where(s.hasup,1,0)+jnp.where(s.hasdn,1,0))
+        more=0 if extra is None else extra
+        pl.semaphore_wait(bar,3+jnp.where(s.hasup,1,0)+jnp.where(s.hasdn,1,0)+more)
 class Gather:
-    NSEND=3*(5+6*4+7*2+7+7)
-    def __init__(s,own,w,ssem,rsem,lsem,K=3,vec=None):
-        c=s.c=Ctx(); s.own,s.w,s.ssem,s.rsem,s.lsem=own,w,ssem,rsem,lsem
-        s.K=K; s.pend=[]; s.ns=0; s.steps=[]
-        TRUE=None
-        s.start=s._start
-        for dist in range(1,6):
-            for sg in (1,-1):
-                for kind in ("z","a","b","ba"):
-                    extra={"z":0,"a":1,"b":1,"ba":2}[kind]
-                    dz=dist-extra
-                    if dz<0 or dz>3 or (kind=="z" and dz==0) or (dz==0 and sg<0): continue
-                    s.steps.append(functools.partial(s._item,kind,sg*dz))
-        s.steps.append(s._finish)
-    def _send(s,src,p,to,cond):
-        i=s.ns; s.ns+=1
-        cp=pltpu.make_async_remote_copy(src,s.w.at[p],s.ssem.at[i],s.rsem.at[p],device_id=(to,),device_id_type=MESH)
-        if cond is None: cp.start()
+    K = 3
+
+    @staticmethod
+    def sems(lo, hi):
+        dma = lambda n: pltpu.SemaphoreType.DMA((n,))
+        return [dma(3 * 96), dma(24 * (hi - lo + 1)), dma(3)]
+
+    def __init__(s, c, lo, hi, own, w, sems):
+        s.c, s.lo, s.hi, s.own, s.w = c, lo, hi, own, w
+        s.ssem, s.rsem, s.lsem = sems
+        s.ns = 0
+        s.pend = []
+        s.steps = []
+        kinds = (("z", 0), ("a", 1), ("b", 1), ("ba", 2))
+        for dist in range(1, 6):
+            for k in range(s.K):
+                if lo == hi:
+                    continue
+                for sign in (1, -1):
+                    for kind, extra in kinds:
+                        dz = dist - extra
+                        if dz < 0 or (kind == "z" and dz == 0) or (dz == 0 and sign < 0):
+                            continue
+                        if (sign > 0 and dz > hi) or (sign < 0 and dz > 3 - lo):
+                            continue
+                        s.steps.append(functools.partial(s.item, kind, sign * dz, k))
+        if lo == hi:
+            s.steps = [functools.partial(s.item, kind, None, k) for kind, _ in kinds[:1] for k in range(s.K)]
+            s.steps += [functools.partial(s.item, kind, None, k) for k in range(s.K) for kind in ("a", "b")]
+            s.steps += [functools.partial(s.item, "ba", None, k) for k in range(s.K)]
+
+    def inside(s, zz):
+        return jnp.logical_and(zz >= s.lo, zz <= s.hi)
+
+    def slot(s, dev, k):
+        return s.rsem.at[jnp.clip((dev - 8 * s.lo) * s.K + k, 0, 24 * (s.hi - s.lo + 1) - 1)]
+
+    def send(s, src, dev, k, to, *conds):
+        i = s.ns
+        s.ns += 1
+        cp = pltpu.make_async_remote_copy(
+            src, s.w.at[dev, k], s.ssem.at[i], s.slot(dev, k), device_id=(to,), device_id_type=MESH
+        )
+        conds = [f for f in conds if f is not None]
+        s.pend.append((i, conds))
+        s.when(conds, cp.start)
+
+    @staticmethod
+    def when(conds, fn):
+        if conds:
+            pl.when(functools.reduce(jnp.logical_and, [f() for f in conds]))(fn)
         else:
-            @pl.when(cond)
-            def _(): cp.start()
-        s.pend.append((cp,cond))
-    def _start(s):
-        c=s.c
-        for k in range(s.K):
-            p=c.me*s.K+k; src=s.own.at[k]
-            s._send(src,p,c.up,c.hasup); s._send(src,p,c.dn,c.hasdn)
-            s._send(src,p,c.bp,None); s._send(src,p,c.ap,None); s._send(src,p,c.sib,None)
-        s.loc=[]
-        for k in range(s.K):
-            cp=pltpu.make_async_copy(s.own.at[k],s.w.at[c.me*s.K+k],s.lsem.at[k]); cp.start(); s.loc.append(cp)
-    def _wait(s,p):
-        pltpu.make_async_copy(s.w.at[p],s.w.at[p],s.rsem.at[p]).wait()
-    def _item(s,kind,dz):
-        c=s.c
-        zz=c.z+dz
-        fl=jnp.int32(0)
-        src=c.me+8*dz
-        if "a" in kind: src=src+c.astep*(1-2*c.abit)
-        if "b" in kind: src=src+c.bstep*(1-2*c.bbit)
-        valid=None if dz==0 else ((zz<4) if dz>0 else (zz>=0))
+            fn()
+
+    def mine(s):
+        return s.inside(s.c.z)
+
+    def start(s, ks, routes):
+        c = s.c
+        to = dict(
+            dn=(c.dn, lambda: c.hasdn), up=(c.up, lambda: c.hasup), b=(c.bp, None), a=(c.ap, None), s=(c.sib, None)
+        )
+
+        @pl.when(s.mine())
+        def _():
+            for k in ks:
+                for r in routes:
+                    s.send(s.own.at[k], c.me, k, to[r][0], to[r][1])
+                    i, conds = s.pend.pop()
+                    s.pend.append((i, conds + [s.mine]))
+
+    def keep(s):
+        @pl.when(s.mine())
+        def _():
+            for k in range(s.K):
+                pltpu.make_async_copy(s.own.at[k], s.w.at[s.c.me, k], s.lsem.at[k]).start()
+
+    def keep_wait(s):
+        @pl.when(s.mine())
+        def _():
+            for k in range(s.K):
+                pltpu.make_async_copy(s.own.at[k], s.w.at[s.c.me, k], s.lsem.at[k]).wait()
+
+    def wait(s, dev, k):
+        r = s.w.at[dev, k]
+        pltpu.make_async_copy(r, r, s.slot(dev, k)).wait()
+
+    def item(s, kind, dz, k):
+        c = s.c
+        if dz is None:
+            src = c.me + 8 * (s.lo - c.z)
+            valid = (lambda: c.z != s.lo) if kind == "z" else None
+        else:
+            src = c.me + 8 * dz
+            valid = lambda: s.inside(c.z + dz)
+        if "a" in kind:
+            src = src + c.astep * (1 - 2 * c.abit)
+        if "b" in kind:
+            src = src + c.bstep * (1 - 2 * c.bbit)
+
         def body():
-            for k in range(s.K):
-                p=src*s.K+k
-                s._wait(p)
-                sends=[]
-                if kind=="z":
-                    sends.append((c.dn,c.hasdn) if dz>0 else (c.up,c.hasup))
-                if kind in("z","a"): sends.append((c.bp,None))
-                if kind=="z": sends.append((c.ap,None))
-                sends.append((c.sib,None))
-                for to,cond in sends:
-                    i=s.ns; s.ns+=1
-                    cp=pltpu.make_async_remote_copy(s.w.at[p],s.w.at[p],s.ssem.at[i],s.rsem.at[p],device_id=(to,),device_id_type=MESH)
-                    if cond is None: cp.start()
-                    else:
-                        @pl.when(cond)
-                        def _(): cp.start()
-                    s.pend.append((kind,dz,p,i,to,cond,valid))
-        if valid is None: body()
-        else: pl.when(valid)(body)
-    def _finish(s):
-        c=s.c
-        def sibw(i,_):
-            chip=i//s.K; k=i%s.K
-            s._wait((2*chip+1-c.core)*s.K+k)
+            s.wait(src, k)
+            r = s.w.at[src, k]
+            if kind == "z":
+                if (dz is None and s.lo < 3) or (dz is not None and dz < 0):
+                    beyond = (lambda: c.z > s.lo) if dz is None and s.lo > 0 else None
+                    s.send(r, src, k, c.up, lambda: c.hasup, valid, beyond)
+                if (dz is None and s.lo > 0) or (dz is not None and dz > 0):
+                    beyond = (lambda: c.z < s.lo) if dz is None and s.lo < 3 else None
+                    s.send(r, src, k, c.dn, lambda: c.hasdn, valid, beyond)
+            if kind in ("z", "a"):
+                s.send(r, src, k, c.bp, valid)
+            if kind == "z":
+                s.send(r, src, k, c.ap, valid)
+            s.send(r, src, k, c.sib, valid)
+
+        s.when([] if valid is None else [valid], body)
+
+    def sibling(s):
+        c = s.c
+
+        def one(i, _):
+            s.wait(8 * s.lo + 2 * (i // s.K) + 1 - c.core, i % s.K)
             return 0
-        lax.fori_loop(0,16*s.K,sibw,0)
-        for e in s.pend:
-            if len(e)==2:
-                cp,cond=e
-                if cond is None: cp.wait_send()
-                else: pl.when(cond)(cp.wait_send)
+
+        lax.fori_loop(0, 4 * (s.hi - s.lo + 1) * s.K, one, 0)
+
+    def sent(s):
+        for i, conds in s.pend:
+            r = s.w.at[0, 0]
+            s.when(conds, pltpu.make_async_copy(r, r, s.ssem.at[i]).wait)
+
+
+class Vector:
+    def __init__(s, c, own, vec, sem):
+        s.c, s.own, s.vec, s.sem = c, own, vec, sem
+        s.n = 31
+
+    def tell(s):
+        bar = pltpu.get_barrier_semaphore()
+
+        @pl.when(s.c.me != s.n)
+        def _():
+            pl.semaphore_signal(bar, inc=1, device_id=(s.n,), device_id_type=MESH)
+
+    def copy(s, to):
+        return pltpu.make_async_remote_copy(
+            s.own, s.vec, s.sem.at[to], s.sem.at[s.n], device_id=(to,), device_id_type=MESH
+        )
+
+    def start(s):
+        @pl.when(s.c.me == s.n)
+        def _():
+            s.vec[...] = s.own[...]
+
+            def one(i, _):
+                s.copy(i).start()
+                return 0
+
+            lax.fori_loop(0, s.n, one, 0)
+
+    def wait(s):
+        @pl.when(s.c.me != s.n)
+        def _():
+            pltpu.make_async_copy(s.vec, s.vec, s.sem.at[s.n]).wait()
+
+    def sent(s):
+        @pl.when(s.c.me == s.n)
+        def _():
+            def one(i, _):
+                s.copy(i).wait_send()
+                return 0
+
+            lax.fori_loop(0, s.n, one, 0)
+
+class Reduce:
+    K = 3
+
+    @staticmethod
+    def scratch(lo, hi, stage):
+        nz = hi - lo + 1
+        pieces = lambda n: pltpu.VMEM((n, 128, D), BF)
+        dma = lambda n: pltpu.SemaphoreType.DMA((n,))
+        sizes = [12 * nz, 6 * nz, 3 * nz, 3 * nz + 3]
+        return (
+            [pieces(n) for n in sizes]
+            + [pieces(stage)]
+            + [dma(12 * nz)]
+            + [dma(n) for n in sizes]
+            + [dma(12 * nz), dma(stage)]
+        )
+
+    def __init__(s, c, lo, hi, parts, out, scr, scale, order, direct=False):
+        s.c, s.lo, s.hi, s.parts, s.out, s.scale, s.order, s.direct = c, lo, hi, parts, out, scale, order, direct
+        s.S, s.B, s.A, s.Z, s.stage, s.sent_s, s.got_s, s.got_b, s.got_a, s.got_z, s.sent, s.loaded = scr
+        s.nst = s.stage.shape[0]
+        s.nz = hi - lo + 1
+        s.later = []
+        s.waits = []
+        s.steps = [functools.partial(s.item, i) for i in range(len(order))]
+
+    def owner(s, zz, fb, fa, core):
+        c = s.c
+        astep = 2 + 2 * core
+        bstep = 4 - 2 * core
+        abit = c.x + (c.y - c.x) * core
+        bbit = c.y + (c.x - c.y) * core
+        return zz * 8 + core + bstep * (bbit + fb * (1 - 2 * bbit)) + astep * (abit + fa * (1 - 2 * abit))
+
+    def source(s, p, fn):
+        if len(s.parts) == 1:
+            lo, hi, ref = s.parts[0]
+            fn(ref.at[p - lo])
+            return
+        for lo, hi, ref in s.parts:
+
+            @pl.when(jnp.logical_and(p >= lo, p < hi))
+            def _():
+                fn(ref.at[jnp.clip(p - lo, 0, hi - lo - 1)])
+
+    def slot(s, zz, fb, fa, k):
+        return (((zz - s.lo) * 2 + fb) * 2 + fa) * s.K + k
+
+    def places(s, order=None):
+        for kind, zz, fa, k in order or s.order:
+            yield zz, 1 if kind == "b" else 0, fa, k
+
+    def zero(s):
+        c = s.c
+
+        def clear(n):
+            s.Z[n] = jnp.zeros((128, D), BF)
+
+        for n in range(3 * s.nz + 3):
+            at_zero = n < 3 * s.nz
+            at_three = n >= 3 * s.nz or s.lo + n // 3 < 3
+            if at_zero:
+                pl.when(c.z == 0)(functools.partial(clear, n))
+            if at_three:
+                pl.when(c.z == 3)(functools.partial(clear, n))
+
+    def to_sibling(s, order=None):
+        c = s.c
+        for zz, fb, fa, k in s.places(order):
+            n = s.slot(zz, fb, fa, k)
+
+            def go(r, n=n):
+                pltpu.make_async_remote_copy(
+                    r, s.S.at[n], s.sent_s.at[n], s.got_s.at[n], device_id=(c.sib,), device_id_type=MESH
+                ).start()
+
+            s.source(s.owner(zz, fb, fa, 1 - c.core) * s.K + k, go)
+
+    def load(s, i):
+        if s.direct or i >= len(s.order):
+            return
+        (place,) = s.places([s.order[i]])
+        n = i % s.nst
+
+        def go(r):
+            pltpu.make_async_copy(r, s.stage.at[n], s.loaded.at[n]).start()
+
+        s.source(s.owner(*place[:3], s.c.core) * s.K + place[3], go)
+
+    def prefetch(s):
+        for i in range(s.nst - 1):
+            s.load(i)
+
+    def flush(s):
+        for f in s.later:
+            f()
+        s.later = []
+
+    @staticmethod
+    def wait(ref, sem):
+        pltpu.make_async_copy(ref, ref, sem).wait()
+
+    @staticmethod
+    def sum(srcs, dst, scale=None):
+        def rows(r, _):
+            rr = pl.ds(pl.multiple_of(r * 16, 16), 16)
+            t = srcs[0][rr, :].astype(F32)
+            for q in srcs[1:]:
+                t = t + q[rr, :].astype(F32)
+            if scale is not None:
+                t = t * scale
+            dst[rr, :] = t.astype(dst.dtype)
+            return 0
+
+        lax.fori_loop(0, 8, rows, 0)
+
+    def item(s, i):
+        c, K = s.c, s.K
+        kind, zz, fa, k = s.order[i]
+        fb = 1 if kind == "b" else 0
+        if s.direct:
+            lo, hi, ref = s.parts[0]
+            own = ref.at[s.owner(zz, fb, fa, c.core) * K + k - lo]
+        else:
+            own = s.stage.at[i % s.nst]
+            s.wait(own, s.loaded.at[i % s.nst])
+        s.flush()
+        n = s.slot(zz, fb, fa, k)
+        out = s.S.at[n]
+        srcs = [own, out]
+        s.wait(out, s.got_s.at[n])
+        bi = ((zz - s.lo) * 2 + fa) * K + k
+        ai = zi = (zz - s.lo) * K + k
+        z2 = s.nz * K + k
+        if kind in "az":
+            srcs.append(s.B.at[bi])
+            s.wait(s.B.at[bi], s.got_b.at[bi])
+        if kind == "z":
+            srcs.append(s.A.at[ai])
+            s.wait(s.A.at[ai], s.got_a.at[ai])
+
+        def send(dst, sem, to):
+            return pltpu.make_async_remote_copy(
+                s.S.at[n], dst, s.sent.at[n], sem, device_id=(to,), device_id_type=MESH
+            )
+
+        if kind == "b":
+            s.sum(srcs, out)
+            s.later.append(send(s.B.at[bi], s.got_b.at[bi], c.bp).start)
+            s.waits.append((n, None))
+        elif kind == "a":
+            s.sum(srcs, out)
+            s.later.append(send(s.A.at[ai], s.got_a.at[ai], c.ap).start)
+            s.waits.append((n, None))
+        else:
+            comes = jnp.where(c.z <= zz, c.z, 3 - c.z)
+            pl.when(comes > 0)(functools.partial(s.wait, s.Z.at[zi], s.got_z.at[zi]))
+            srcs.append(s.Z.at[zi])
+
+            @pl.when(c.z != zz)
+            def _():
+                s.sum(srcs, out)
+
+            @pl.when(c.z == zz)
+            def _():
+                pl.when(c.hasup)(functools.partial(s.wait, s.Z.at[z2], s.got_z.at[z2]))
+                s.sum(srcs + [s.Z.at[z2]], s.out.at[k], s.scale)
+
+            def on():
+                @pl.when(c.z < zz)
+                def _():
+                    send(s.Z.at[zi], s.got_z.at[zi], c.up).start()
+
+                to = jnp.where(c.z == zz + 1, z2, zi)
+
+                @pl.when(c.z > zz)
+                def _():
+                    send(s.Z.at[to], s.got_z.at[to], c.dn).start()
+
+            s.later.append(on)
+            s.waits.append((n, zz))
+        s.load(i + s.nst - 1)
+
+    def finish(s):
+        s.flush()
+        for n, zz in s.waits:
+            w = functools.partial(s.wait, s.S.at[0], s.sent.at[n])
+            if zz is None:
+                w()
             else:
-                kind,dz,p,i,to,cond,valid=e
-                def w(i=i):
-                    pltpu.make_async_copy(s.w.at[0],s.w.at[0],s.ssem.at[i]).wait()
-                cc=cond if valid is None else (valid if cond is None else jnp.logical_and(cond,valid))
-                if cc is None: w()
-                else: pl.when(cc)(w)
-        for cp in s.loc: cp.wait()
-def gather_kernel(own_ref,w_ref,ssem,rsem,lsem):
-    g=Gather(own_ref,w_ref,ssem,rsem,lsem)
-    g.c.barrier()
-    g.start()
-    for st in g.steps: st()
-def gather(own):
-    return pl.pallas_call(gather_kernel,out_shape=jax.ShapeDtypeStruct((96,128,1024),BF),
-       in_specs=[pl.BlockSpec(memory_space=pltpu.VMEM)],out_specs=pl.BlockSpec(memory_space=pl.ANY),
-       scratch_shapes=[pltpu.SemaphoreType.DMA((Gather.NSEND,)),pltpu.SemaphoreType.DMA((96,)),pltpu.SemaphoreType.DMA((3,))],
-       compiler_params=pltpu.CompilerParams(collective_id=1,has_side_effects=True),name="gather")(own)
-
-class Reduce:
-    K=3
-    @staticmethod
-    def counts(lo,hi):
-        nz=hi-lo+1; K=Reduce.K
-        return dict(S=nz*4*K,B=nz*2*K,A=nz*K,Z=(nz+1)*K,send=nz*2*K+nz*K+6*K)
-    @staticmethod
-    def scratch(lo,hi,nst=4):
-        c=Reduce.counts(lo,hi); pc=lambda n: pltpu.VMEM((n,128,1024),BF); sem=lambda n: pltpu.SemaphoreType.DMA((n,))
-        return [pc(c["S"]),pc(c["B"]),pc(c["A"]),pc(c["Z"]),pc(nst),sem(c["S"]),sem(c["S"]),sem(c["B"]),sem(c["A"]),sem(c["Z"]),sem(c["send"]),sem(nst)]
-    def __init__(s,c,lo,hi,parts,out,scr,scale):
-        s.c,s.lo,s.hi,s.parts,s.out,s.scale=c,lo,hi,parts,out,scale
-        s.S,s.B,s.A,s.Z,s.st,s.sS,s.rS,s.rB,s.rA,s.rZ,s.ss,s.ls=scr
-        s.nst=s.st.shape[0]; s.nz=hi-lo+1
-        s.deferred=[]; s.ns=0; s.waits=[]
-        K=s.K
-        its=[]
-        for zz in range(hi,lo-1,-1):
-            for fa in (1,0):
-                for k in range(K): its.append(("b",zz,1,fa,k))
-        for zz in range(hi,lo-1,-1):
-            for k in range(K): its.append(("a",zz,0,1,k))
-        for dist in (3,2,1,0):
-            for sg in ((1,-1) if dist else (1,)):
-                for k in range(K): its.append(("z",sg*dist,0,0,k))
-        s.its=its
-        s.steps=[functools.partial(s._item,i) for i in range(len(its))]+[s._finish]
-    def _dest(s,zz,fb,fa,color_core):
-        c=s.c
-        cc=color_core
-        astep=2+2*cc; bstep=4-2*cc
-        abit=c.x+(c.y-c.x)*cc; bbit=c.y+(c.x-c.y)*cc
-        b=bbit+fb*(1-2*bbit); a=abit+fa*(1-2*abit)
-        return zz*8+cc+bstep*b+astep*a
-    def _src(s,p,fn):
-        if len(s.parts)==1:
-            lo,hi,ref=s.parts[0]; fn(ref.at[p-lo]); return
-        for lo,hi,ref in s.parts:
-            @pl.when(jnp.logical_and(p>=lo,p<hi))
-            def _(): fn(ref.at[jnp.clip(p-lo,0,hi-lo-1)])
-    def _slotS(s,zz,fb,fa,k): return (((zz-s.lo)*2+fb)*2+fa)*s.K+k
-    def send_sibling(s):
-        c=s.c; oc=1-c.core
-        for (kind,zz,fb,fa,k) in s._order():
-            p=s._dest(zz,fb,fa,oc)*s.K+k; sl=s._slotS(zz,fb,fa,k)
-            def go(r): pltpu.make_async_remote_copy(r,s.S.at[sl],s.sS.at[sl],s.rS.at[sl],device_id=(c.sib,),device_id_type=MESH).start()
-            s._src(p,go)
-    def _order(s):
-        o=[]
-        for it in s.its:
-            if it[0] in "ba": o.append(it)
-        for zz in range(s.hi,s.lo-1,-1):
-            for k in range(s.K): o.append(("z",zz,0,0,k))
-        return o
-    def _info(s,i):
-        kind,zz,fb,fa,k=s.its[i]; valid=None
-        if kind=="z":
-            zz=s.c.z+zz; valid=jnp.logical_and(zz>=s.lo,zz<=s.hi)
-        return kind,zz,fb,fa,k,valid
-    def _load(s,i):
-        if i>=len(s.its): return
-        kind,zz,fb,fa,k,valid=s._info(i)
-        p=s._dest(zz,fb,fa,s.c.core)*s.K+k
-        def go(r): pltpu.make_async_copy(r,s.st.at[i%s.nst],s.ls.at[i%s.nst]).start()
-        if valid is None: s._src(p,go)
-        else: pl.when(valid)(lambda: s._src(p,go))
-    def prefetch(s):
-        for i in range(s.nst-1): s._load(i)
-    def _flush(s):
-        for f in s.deferred: f()
-        s.deferred=[]
-    def _wait(s,ref,sem): pltpu.make_async_copy(ref,ref,sem).wait()
-    def _sum(s,srcs,dst,scale=None):
-        def body(r,_):
-            rr=pl.ds(pl.multiple_of(r*16,16),16)
-            t=srcs[0][rr,:].astype(F32)
-            for q in srcs[1:]: t=t+q[rr,:].astype(F32)
-            if scale is not None: t=t*scale
-            dst[rr,:]=t.astype(dst.dtype)
+                pl.when(s.c.z != zz)(w)
+
+        def one(i, _):
+            s.wait(s.S.at[0], s.sent_s.at[i])
             return 0
-        lax.fori_loop(0,8,body,0)
-    def _item(s,i):
-        c=s.c; K=s.K
-        kind,zz,fb,fa,k,valid=s._info(i)
-        dist=s.its[i][1] if kind=="z" else None
-        def main():
-            own=s.st.at[i%s.nst]
-            s._wait(own,s.ls.at[i%s.nst])
-            sl=s._slotS(zz,fb,fa,k)
-            srcs=[own,s.S.at[sl]]; s._wait(s.S.at[sl],s.rS.at[sl])
-            if kind in "az":
-                bi=((zz-s.lo)*2+fa)*K+k; srcs.append(s.B.at[bi]); s._wait(s.B.at[bi],s.rB.at[bi])
-            if kind=="z":
-                ai=(zz-s.lo)*K+k; srcs.append(s.A.at[ai]); s._wait(s.A.at[ai],s.rA.at[ai])
-            return sl,srcs
-        def send(sl,dst,rsem,to,n):
-            return pltpu.make_async_remote_copy(s.S.at[sl],dst,s.ss.at[n],rsem,device_id=(to,),device_id_type=MESH)
-        prev=s.deferred; s.deferred=[]
-        if kind in "ba":
-            sl,srcs=main()
-            s._sum(srcs,s.S.at[sl])
-            n=s.ns; s.ns+=1
-            if kind=="b":
-                bi=((zz-s.lo)*2+fa)*K+k; cp=send(sl,s.B.at[bi],s.rB.at[bi],c.bp,n)
-            else:
-                ai=(zz-s.lo)*K+k; cp=send(sl,s.A.at[ai],s.rA.at[ai],c.ap,n)
-            s.deferred.append(cp.start); s.waits.append((n,None))
-        elif dist!=0:
-            n=s.ns; s.ns+=1
-            upw=dist>0
-            zi=(zz-s.lo)*K+k
-            has=c.hasdn if upw else c.hasup
-            @pl.when(valid)
-            def _():
-                sl,srcs=main()
-                @pl.when(has)
-                def _():
-                    s._wait(s.Z.at[zi],s.rZ.at[zi]); s._sum(srcs+[s.Z.at[zi]],s.S.at[sl])
-                @pl.when(jnp.logical_not(has))
-                def _(): s._sum(srcs,s.S.at[sl])
-            last=jnp.logical_and(zz==c.z-1,not upw)
-            zo=jnp.where(last,s.nz*K+k,zi)
-            def st():
-                @pl.when(valid)
-                def _():
-                    send(s._slotS(zz,fb,fa,k),s.Z.at[zo],s.rZ.at[zo],c.up if upw else c.dn,n).start()
-            s.deferred.append(st); s.waits.append((n,valid))
-        else:
-            @pl.when(valid)
-            def _():
-                sl,srcs=main()
-                z1=s.Z.at[(zz-s.lo)*K+k]; r1=s.rZ.at[(zz-s.lo)*K+k]; z2=s.Z.at[s.nz*K+k]; r2=s.rZ.at[s.nz*K+k]
-                @pl.when(jnp.logical_and(c.hasdn,c.hasup))
-                def _():
-                    s._wait(z1,r1); s._wait(z2,r2); s._sum(srcs+[z1,z2],s.out.at[k],s.scale)
-                @pl.when(jnp.logical_not(c.hasup))
-                def _():
-                    s._wait(z1,r1); s._sum(srcs+[z1],s.out.at[k],s.scale)
-                @pl.when(jnp.logical_not(c.hasdn))
-                def _():
-                    s._wait(z2,r2); s._sum(srcs+[z2],s.out.at[k],s.scale)
-        for f in prev: f()
-        s._load(i+s.nst-1)
-    def _finish(s):
-        s._flush()
-        for n,valid in s.waits:
-            w=functools.partial(s._wait,s.S.at[0],s.ss.at[n])
-            if valid is None: w()
-            else: pl.when(valid)(w)
-        def sw(i,_):
-            s._wait(s.S.at[0],s.sS.at[i]); return 0
-        lax.fori_loop(0,s.S.shape[0],sw,0)
-def reduce_kernel(*refs,lo,hi,ranges,scale):
-    n=len(ranges)
-    parts=[(a,b,r) for (a,b),r in zip(ranges,refs[:n])]
-    out=refs[n]; scr=refs[n+1:]
-    c=Ctx()
-    rd=Reduce(c,lo,hi,parts,out,scr,scale)
-    c.barrier()
-    rd.send_sibling(); rd.prefetch()
-    for st in rd.steps: st()
-def reduce_(arrs,lo,hi,ranges,scale,cid=2):
-    return pl.pallas_call(functools.partial(reduce_kernel,lo=lo,hi=hi,ranges=ranges,scale=scale),out_shape=jax.ShapeDtypeStruct((3,128,1024),F32),
-       in_specs=[pl.BlockSpec(memory_space=pl.ANY)]*len(arrs),out_specs=pl.BlockSpec(memory_space=pltpu.VMEM),
-       scratch_shapes=Reduce.scratch(lo,hi),
-       compiler_params=pltpu.CompilerParams(collective_id=cid,has_side_effects=True,vmem_limit_bytes=60<<20),name=f"reduce{lo}{hi}")(*arrs)
+
+        lax.fori_loop(0, 12 * s.nz, one, 0)
+
+
+def reduce_order(lo, hi):
+    order = []
+    planes = list(range(hi, lo - 1, -1))
+    b = lambda zz: [("b", zz, fa, k) for fa in (1, 0) for k in range(3)]
+    a = lambda zz: [("a", zz, 1, k) for k in range(3)]
+    z = lambda zz: [("z", zz, 0, k) for k in range(3)]
+    for i in range(len(planes) + 2):
+        if i < len(planes):
+            order += b(planes[i])
+        if 1 <= i <= len(planes):
+            order += a(planes[i - 1])
+        if i >= 2:
+            order += z(planes[i - 2])
+    return order
 
 
 def qkv_kernel(x_ref, vec_ref, w_ref, out_ref, n_ref):
@@ -408,6 +543,119 @@
         compiler_params=pltpu.CompilerParams(vmem_limit_bytes=VMEM_ALL),
         name="attend",
     )(z, z, z)
+
+
+def norm_block(v, vec_ref):
+    v = v.astype(F32)
+    ce = v - jnp.mean(v, axis=1, keepdims=True)
+    rc = lax.rsqrt(jnp.mean(ce * ce, axis=1, keepdims=True) + EPS)
+    return (ce * rc * (1.0 + vec_ref[8:9, :]) + vec_ref[9:10, :]).astype(BF)
+
+
+def norm_one(x_ref, vec_ref, n_ref):
+    for i in range(2):
+
+        def one(c, _):
+            n_ref[i, rows_at(c), :] = norm_block(x_ref[i, rows_at(c), :], vec_ref)
+            return 0
+
+        lax.fori_loop(0, 18, one, 0)
+        last = norm_block(x_ref[i, 576:577, :], vec_ref).astype(F32)
+        n_ref[i, 576:592, :] = jnp.concatenate([last, jnp.zeros((15, D), F32)], axis=0).astype(BF)
+
+
+def front_kernel(own, vec_own, x_ref, w, vec, z_ref, n_ref, mix_ref, vlow, wq, qsem, vsem, *sems):
+    c = Ctx()
+    zero = Gather(c, 0, 0, own, w, sems[:3])
+    rest = Gather(c, 1, FRONT_HI, own, w, sems[3:])
+    vector = Vector(c, vec_own, vlow, vsem)
+    vector.tell()
+    c.barrier(jnp.where(c.me == 31, 31, 0))
+    vector.start()
+    zero.start((0, 1, 2), ("up", "b", "a", "s"))
+    rest.start((0, 1, 2), ("dn",))
+    rest.start(range(EARLY), ("b", "a"))
+    rest.start((0, 1, 2), ("s",))
+    zero.keep()
+    rest.keep()
+    for step in zero.steps[:3]:
+        step()
+    for step in zero.steps[3:]:
+        step()
+    rest.start((0, 1, 2), ("up",))
+    rest.start(range(EARLY, 3), ("b", "a"))
+    zero.keep_wait()
+    zero.sibling()
+    loads = [pltpu.make_async_copy(w.at[0:8, j], wq.at[j % 2], qsem.at[j]) for j in range(3)]
+    loads[0].start()
+    loads[1].start()
+    vector.wait()
+    vec[...] = vlow[...].astype(F32)
+    norm_one(x_ref, vec, n_ref)
+    per = PER
+    steps = list(rest.steps)
+    for j in range(3):
+        for step in steps[:per]:
+            step()
+        steps = steps[per:]
+        loads[j].wait()
+        for i in range(2):
+            r = nn(n_ref[i], wq[j % 2].reshape(D, D))
+            if j != 1:
+                r = r + vec[j // 2 : j // 2 + 1, :]
+            z_ref[j, i] = r.astype(BF)
+        if j == 0:
+            loads[2].start()
+
+    def pair(t, _):
+        for n in range(16):
+            if steps[n * per : (n + 1) * per]:
+
+                @pl.when(t == n)
+                def _():
+                    for step in steps[n * per : (n + 1) * per]:
+                        step()
+
+        i = t // 8
+        cols = pl.ds(pl.multiple_of((t % 8) * 128, 128), 128)
+        half = SQ // 2
+        k = z_ref[1, i, :, cols]
+        v = z_ref[2, i, :, cols]
+        for r in range(2):
+            rows = slice(r * half, (r + 1) * half)
+            mix_ref[i, rows, cols] = attend_pair(z_ref[0, i, rows, cols], k, v)
+        return 0
+
+    lax.fori_loop(0, 16, pair, 0)
+    for step in steps[16 * per :]:
+        step()
+    rest.sibling()
+    rest.keep_wait()
+    zero.sent()
+    rest.sent()
+    vector.sent()
+
+
+def front(own, vec_own, x):
+    vm = pl.BlockSpec(memory_space=pltpu.VMEM)
+    dma = lambda n: pltpu.SemaphoreType.DMA((n,))
+    return pl.pallas_call(
+        front_kernel,
+        in_specs=[vm, vm, vm],
+        out_specs=[pl.BlockSpec(memory_space=pl.ANY), vm, vm, vm, vm],
+        out_shape=[
+            jax.ShapeDtypeStruct((32, 3, 128, D), BF),
+            jax.ShapeDtypeStruct((16, D), F32),
+            jax.ShapeDtypeStruct((3, 2, SQ, D), BF),
+            jax.ShapeDtypeStruct((2, SQ, D), BF),
+            jax.ShapeDtypeStruct((2, SQ, D), BF),
+        ],
+        scratch_shapes=[pltpu.VMEM((16, D), BF), pltpu.VMEM((2, 8, 128, D), BF), dma(3), dma(32)]
+        + Gather.sems(0, 0)
+        + Gather.sems(1, FRONT_HI),
+        compiler_params=pltpu.CompilerParams(collective_id=1, has_side_effects=True, vmem_limit_bytes=VMEM_ALL),
+        name="front",
+    )(own, vec_own, x)
 
 
 def attend_back_pair(q, k, v, do):
@@ -629,6 +877,291 @@
         name="tail",
     )(x, dz, n1, dhid, vec, w.reshape(32, 3, 128, D), gvec)
 
+def back_kernel(z_ref, do_ref, *refs, lo, hi, ranges, scale, per):
+    n = len(ranges)
+    parts = [(a, b, r) for (a, b), r in zip(ranges, refs[:n])]
+    dz_ref, chunk = refs[n : n + 2]
+    c = Ctx()
+    order = reduce_order(lo, hi)
+    red = Reduce(c, lo, hi, parts, chunk, refs[n + 2 :], scale, order)
+    red.zero()
+    chunk[...] = jnp.zeros_like(chunk)
+    c.barrier()
+    red.to_sibling()
+    red.prefetch()
+
+    def pair(t, _):
+        for m in range(16):
+            if red.steps[m * per : (m + 1) * per]:
+
+                @pl.when(t == m)
+                def _():
+                    for step in red.steps[m * per : (m + 1) * per]:
+                        step()
+                    red.flush()
+
+        i = t // 8
+        cols = pl.ds(pl.multiple_of((t % 8) * 128, 128), 128)
+        dq, dk, dv = attend_back_pair(z_ref[0, i, :, cols], z_ref[1, i, :, cols], z_ref[2, i, :, cols], do_ref[i, :, cols])
+        dz_ref[0, i, :, cols] = dq
+        dz_ref[1, i, :, cols] = dk
+        dz_ref[2, i, :, cols] = dv
+        return 0
+
+    lax.fori_loop(0, 16, pair, 0)
+    for step in red.steps[16 * per :]:
+        step()
+    red.finish()
+
+
+def back(z, do, parts, lo, hi, ranges, scale, per=BPER):
+    vm = pl.BlockSpec(memory_space=pltpu.VMEM)
+    return pl.pallas_call(
+        functools.partial(back_kernel, lo=lo, hi=hi, ranges=ranges, scale=scale, per=per),
+        in_specs=[vm, vm] + [pl.BlockSpec(memory_space=pl.ANY)] * len(parts),
+        out_specs=[vm, vm],
+        out_shape=[jax.ShapeDtypeStruct((3, 2, SQ, D), BF), jax.ShapeDtypeStruct((3, 128, D), F32)],
+        scratch_shapes=Reduce.scratch(lo, hi, 4),
+        compiler_params=pltpu.CompilerParams(collective_id=2, has_side_effects=True, vmem_limit_bytes=VMEM_ALL),
+        name="back",
+    )(z, do, *parts)
+
+
+def back_norm(x, dd, dh, vec_ref):
+    v = x.astype(F32)
+    ce = v - jnp.mean(v, axis=1, keepdims=True)
+    rc = lax.rsqrt(jnp.mean(ce * ce, axis=1, keepdims=True) + EPS)
+    xh = ce * rc
+    e = dd * (1.0 + vec_ref[8:9, :])
+    g = dh + rc * (e - jnp.mean(e, axis=1, keepdims=True) - xh * jnp.mean(e * xh, axis=1, keepdims=True))
+    return g.astype(BF), dd * xh
+
+
+def tail_quick_kernel(
+    x_ref, dz_ref, n_ref, dhid_ref, vec_ref, gvin_ref, w, gx_ref, chunk, gvec_ref, acc, gw, wq, qsem, *scr, scale
+):
+    c = Ctx()
+    order = [(kind, 0, fa, k) for k in range(3) for kind, fa in (("b", 1), ("b", 0), ("a", 1), ("z", 0))]
+    red = Reduce(c, 0, 0, [(0, 24, gw)], chunk, scr, scale, order, direct=True)
+    loads = [pltpu.make_async_copy(w.at[0:8, j], wq.at[j % 2], qsem.at[j]) for j in range(3)]
+    loads[0].start()
+    loads[1].start()
+    red.zero()
+    chunk[...] = jnp.zeros_like(chunk)
+    gvec_ref[...] = gvin_ref[...]
+    c.barrier()
+    queue = list(red.steps)
+
+    def take(*ids):
+        for i in ids:
+            queue[i]()
+
+    def weights(j):
+        g = tn(n_ref[...].reshape(M, D), dz_ref[j].reshape(M, D)).astype(BF)
+        for d in range(8):
+            gw[3 * d + j] = g[128 * d : 128 * (d + 1)]
+
+    def colsum(j):
+        def add(r, t):
+            rr = pl.ds(pl.multiple_of(r * 16, 16), 16)
+            return t + dz_ref[j, 0, rr, :].astype(F32) + dz_ref[j, 1, rr, :].astype(F32)
+
+        t = lax.fori_loop(0, SQ // 16, add, jnp.zeros((16, D), F32))
+        gvec_ref[j // 2 : j // 2 + 1, :] = jnp.sum(t, axis=0, keepdims=True)
+
+    def inputs(j):
+        loads[j].wait()
+        wj = wq[j % 2].reshape(D, D)
+        for i in range(2):
+            r = nt(dz_ref[j, i], wj)
+            rows = slice(i * SQ, (i + 1) * SQ)
+            acc[rows, :] = r if j == 0 else acc[rows, :] + r
+
+    some = lambda k: [o for o in order if o[3] == k]
+    weights(0)
+    colsum(0)
+    red.to_sibling(some(0))
+    weights(1)
+    red.to_sibling(some(1))
+    take(0, 1)
+    weights(2)
+    take(4, 5, 2)
+    red.to_sibling(some(2))
+    inputs(0)
+    loads[2].start()
+    take(8, 9, 6, 3)
+    red.flush()
+    inputs(1)
+    take(10, 7)
+    red.flush()
+    inputs(2)
+    take(11)
+    red.flush()
+    colsum(2)
+    a = b = jnp.zeros((CH, D), F32)
+    la = lb = jnp.zeros((1, D), F32)
+    for i in range(2):
+
+        def one(t, carry):
+            r = rows_at(t)
+            r2 = pl.ds(pl.multiple_of(i * SQ + t * CH, 16), CH)
+            dd = acc[r2, :]
+            g, s1 = back_norm(x_ref[i, r, :], dd, dhid_ref[r2, :], vec_ref)
+            gx_ref[i, r, :] = g
+            return carry[0] + s1, carry[1] + dd
+
+        a, b = lax.fori_loop(0, 18, one, (a, b))
+        r2 = slice(i * SQ + 576, i * SQ + 577)
+        dd = acc[r2, :]
+        g, s1 = back_norm(x_ref[i, 576:577, :], dd, dhid_ref[r2, :], vec_ref)
+        gx_ref[i, 576:577, :] = g
+        la, lb = la + s1, lb + dd
+    gvec_ref[8:9, :] = jnp.sum(a, axis=0, keepdims=True) + la
+    gvec_ref[9:10, :] = jnp.sum(b, axis=0, keepdims=True) + lb
+    red.finish()
+
+
+def tail_quick(x, dz, n1, dhid, vec, gvec, w, scale):
+    vm = pl.BlockSpec(memory_space=pltpu.VMEM)
+    return pl.pallas_call(
+        functools.partial(tail_quick_kernel, scale=scale),
+        in_specs=[vm] * 6 + [pl.BlockSpec(memory_space=pl.ANY)],
+        out_specs=[vm] * 3,
+        out_shape=[
+            jax.ShapeDtypeStruct((2, S, D), BF),
+            jax.ShapeDtypeStruct((3, 128, D), F32),
+            jax.ShapeDtypeStruct((16, D), F32),
+        ],
+        scratch_shapes=[
+            pltpu.VMEM((M, D), F32),
+            pltpu.VMEM((24, 128, D), BF),
+            pltpu.VMEM((2, 8, 128, D), BF),
+            pltpu.SemaphoreType.DMA((3,)),
+        ]
+        + Reduce.scratch(0, 0, 1),
+        compiler_params=pltpu.CompilerParams(collective_id=3, has_side_effects=True, vmem_limit_bytes=VMEM_ALL),
+        name="tail_quick",
+    )(x, dz, n1, dhid, vec, gvec, w)
+
+
+def close_kernel(chunk_a, chunk_b, gvec, p_ref, m_ref, v_ref, wg, pn, mn, vn, flat, e, es, ea, eb, ez, sem, *, scale):
+    c = Ctx()
+    me = c.me
+    bar = pltpu.get_barrier_semaphore()
+    others = [c.sib, c.ap, c.bp] + [lax.rem(me + 8 * i, 32) for i in (1, 2, 3)]
+    for to in others:
+        pl.semaphore_signal(bar, inc=1, device_id=(to,), device_id_type=MESH)
+    first, last = me == 0, me == 31
+
+    @pl.when(jnp.logical_not(first))
+    def _():
+        pl.semaphore_signal(bar, inc=1, device_id=(me - 1,), device_id_type=MESH)
+
+    @pl.when(jnp.logical_not(last))
+    def _():
+        pl.semaphore_signal(bar, inc=1, device_id=(me + 1,), device_id_type=MESH)
+
+    def unfold(src, k, kind):
+        for t in range(8):
+            cols = slice(128 * t, 128 * (t + 1))
+            if kind == 0:
+                flat[pl.ds(8 * k + t, 128, stride=24), :] = src[k, :, cols]
+            elif kind == 1:
+                flat[pl.ds(1024 * k + t, 128, stride=8), :] = src[k, :, cols]
+            else:
+                for j in range(4):
+                    flat[pl.ds(1024 * k + 8 * j + t, 32, stride=32), :] = src[k, 32 * j : 32 * j + 32, cols]
+
+    for k in range(3):
+        p = 3 * me + k
+        up = jnp.logical_and(p >= 32, p < 64)
+        pl.when(c.z == 0)(functools.partial(unfold, chunk_b, k, 0))
+        pl.when(up)(functools.partial(unfold, chunk_a, k, 2))
+        pl.when(jnp.logical_and(c.z > 0, jnp.logical_not(up)))(functools.partial(unfold, chunk_a, k, 1))
+
+    def square(i, t):
+        v = flat[pl.ds(pl.multiple_of(i * 64, 64), 64), :]
+        return t + v * v
+
+    sq = jnp.sum(lax.fori_loop(0, 48, square, jnp.zeros((64, 128), F32)))
+    e[0:16, :] = gvec[...]
+    e[16:24, :] = jnp.full((8, D), sq, F32)
+    pl.semaphore_wait(bar, 6 + jnp.where(first, 0, 1) + jnp.where(last, 0, 1))
+    head = flat.at[0:96]
+    room = flat.at[3072:3168]
+    edge = pltpu.make_async_remote_copy(
+        head, room, sem.at[14], sem.at[15], device_id=(jnp.maximum(me - 1, 0),), device_id_type=MESH
+    )
+    pl.when(jnp.logical_not(first))(edge.start)
+    for n, (to, dst) in enumerate(((c.sib, es), (c.ap, ea), (c.bp, eb))):
+        cp = pltpu.make_async_remote_copy(e, dst, sem.at[n], sem.at[3 + n], device_id=(to,), device_id_type=MESH)
+        cp.start()
+        cp.wait()
+        e[...] = e[...] + dst[...]
+    ez[c.z] = e[...]
+    cps = []
+    for i in (1, 2, 3):
+        to = lax.rem(me + 8 * i, 32)
+        cp = pltpu.make_async_remote_copy(
+            e, ez.at[c.z], sem.at[6 + i], sem.at[9 + i], device_id=(to,), device_id_type=MESH
+        )
+        cp.start()
+        cps.append(cp)
+    for i in (1, 2, 3):
+        cps[i - 1].wait_send()
+        zz = lax.rem(c.z + 4 - i, 4)
+        pltpu.make_async_copy(ez.at[zz], ez.at[zz], sem.at[9 + i]).wait()
+    total = ((ez[0] + ez[1]) + ez[2]) + ez[3]
+    vec = total[0:12, :] * scale
+    square_sum = total[16:17, 0:1] + jnp.sum(vec * vec)
+    clip = jnp.minimum(1.0, max_norm / (jnp.sqrt(square_sum) + 1e-06))
+
+    @pl.when(last)
+    def _():
+        for t in range(8):
+            flat[pl.ds(3072 + t, 12, stride=8), :] = vec[:, 128 * t : 128 * (t + 1)]
+
+    @pl.when(jnp.logical_not(last))
+    def _():
+        pltpu.make_async_copy(room, room, sem.at[15]).wait()
+
+    pl.when(jnp.logical_not(first))(edge.wait_send)
+
+    def apply(g, rows):
+        w = clip * g
+        m1 = beta_one * m_ref[rows, :] + (1.0 - beta_one) * w
+        m2 = beta_two * v_ref[rows, :] + (1.0 - beta_two) * w * w
+        par = p_ref[rows, :]
+        step = m1 / (1.0 - beta_one**STEP) / (jnp.sqrt(m2 / (1.0 - beta_two**STEP)) + adam_eps)
+        wg[rows, :] = g
+        pn[rows, :] = par - learn_rate * (step + decay_rate * par)
+        mn[rows, :] = m1
+        vn[rows, :] = m2
+
+    def block(i, _):
+        apply(flat[pl.ds(i * 64 + 3 * me, 64), :], pl.ds(pl.multiple_of(i * 64, 64), 64))
+        return 0
+
+    lax.fori_loop(0, 48, block, 0)
+    apply(flat[pl.ds(3072 + 3 * me, 3), :], slice(3072, 3075))
+
+
+def close(chunk_a, chunk_b, gvec, params, moment_one, moment_two, scale):
+    vm = pl.BlockSpec(memory_space=pltpu.VMEM)
+    own = jax.ShapeDtypeStruct((3075, 128), F32)
+    small = pltpu.VMEM((24, D), F32)
+    return pl.pallas_call(
+        functools.partial(close_kernel, scale=scale),
+        in_specs=[vm] * 6,
+        out_specs=[vm] * 4,
+        out_shape=[own] * 4,
+        scratch_shapes=[pltpu.VMEM((3168, 128), F32)]
+        + [small] * 4
+        + [pltpu.VMEM((4, 24, D), F32), pltpu.SemaphoreType.DMA((16,))],
+        compiler_params=pltpu.CompilerParams(collective_id=4, has_side_effects=True, vmem_limit_bytes=VMEM_ALL),
+        name="close",
+    )(chunk_a, chunk_b, gvec, *(v.reshape(3075, 128) for v in (params, moment_one, moment_two)))
+
 
 def to_pieces(rows, first):
     n = rows.shape[0] // 128
@@ -667,8 +1200,8 @@
     shard_len = params.shape[0]
     images_all = tokens.shape[0] * n
     mats = PIECES * 128 * D
-    quick = n == 32
-    if quick:
+    scale = 1.0 / images_all
+    if n == 32:
         unit = 128
         extra = 12 * D // unit
         own_units = shard_len // unit
@@ -678,32 +1211,27 @@
         joined = jnp.concatenate([before.astype(F32), low], axis=0)
         aligned = lax.dynamic_slice(joined, (extra - gap * me, 0), (own_units - gap, unit))
         own = to_pieces(aligned.reshape(-1, D), 3 * me).astype(BF)
-        vec_own = low[own_units - extra :].reshape(12, D).astype(BF).astype(F32)
-        vec = lax.psum(jnp.where(me == n - 1, vec_own, 0.0), "dp")
-        w = gather(own)
-    else:
-        flat = lax.all_gather(params.astype(BF), "dp", axis=0, tiled=True)
-        w = to_pieces(flat[:mats].reshape(-1, D), 0)
-        vec = flat[mats:].reshape(12, D).astype(F32)
-    vec = jnp.pad(vec, ((0, 4), (0, 0)))
+        vec_own = jnp.pad(low[own_units - extra :].reshape(12, D), ((0, 4), (0, 0))).astype(BF)
+        w, vec, z, n1, mixed = front(own, vec_own, tokens)
+        flat_w = w.reshape(PIECES, 128, D)
+        outputs, gup, gdn, gout, dmix, dhid, gvec = mlp(tokens, cotangent, mixed, vec, flat_w)
+        parts = [gout, gup.reshape(32, 128, D), gdn]
+        dz, chunk_a = back(z, dmix, parts, 1, 3, [(24, 32), (32, 64), (64, 96)], scale)
+        grad_tokens, chunk_b, gvec = tail_quick(tokens, dz, n1, dhid, vec, gvec, w, scale)
+        news = close(chunk_a, chunk_b, gvec, params, moment_one, moment_two, scale)
+        return (outputs, grad_tokens, *(v.reshape(shard_len) for v in news))
+    flat = lax.all_gather(params.astype(BF), "dp", axis=0, tiled=True)
+    w = to_pieces(flat[:mats].reshape(-1, D), 0)
+    vec = jnp.pad(flat[mats:].reshape(12, D).astype(F32), ((0, 4), (0, 0)))
     z, n1 = qkv(tokens, vec, w)
     mixed = attend(z)
     outputs, gup, gdn, gout, dmix, dhid, gvec = mlp(tokens, cotangent, mixed, vec, w)
     dz = attend_back(z, dmix)
     grad_tokens, gqkv, gvec = tail(tokens, dz, n1, dhid, vec, w, gvec)
     parts = [gqkv.reshape(24, 128, D), gout, gup.reshape(32, 128, D), gdn]
-    if quick:
-        chunk = reduce_(parts, 0, 3, [(0, 24), (24, 32), (32, 64), (64, 96)], 1.0 / images_all)
-        gv = lax.psum(gvec[:12], "dp") / images_all
-        rows = from_pieces(chunk, 3 * me).reshape(own_units - gap, unit)
-        after = lax.ppermute(rows[:extra], "dp", [(i, (i - 1) % n) for i in range(n)])
-        after = jnp.where(me == n - 1, gv.reshape(extra, unit), after)
-        joined = jnp.concatenate([rows, after], axis=0)
-        weight_grad = lax.dynamic_slice(joined, (gap * me, 0), (own_units, unit)).reshape(shard_len)
-    else:
-        flat = jnp.concatenate([from_pieces(jnp.concatenate(parts, axis=0), 0).reshape(-1), gvec[:12].reshape(-1).astype(BF)])
-        arrived = lax.all_to_all(flat.reshape(n, shard_len), "dp", split_axis=0, concat_axis=0, tiled=True)
-        weight_grad = jnp.sum(arrived.astype(F32), axis=0) / images_all
+    flat = jnp.concatenate([from_pieces(jnp.concatenate(parts, axis=0), 0).reshape(-1), gvec[:12].reshape(-1).astype(BF)])
+    arrived = lax.all_to_all(flat.reshape(n, shard_len), "dp", split_axis=0, concat_axis=0, tiled=True)
+    weight_grad = jnp.sum(arrived.astype(F32), axis=0) * scale
     square_sum = lax.psum(jnp.sum(weight_grad * weight_grad), "dp")
     news = update(params, moment_one, moment_two, weight_grad, square_sum)
     return (outputs, grad_tokens, weight_grad, *news)

time: 692 us -> 532 us (0.77)
  blocking collectives: 126 us -> 0 us
  other arithmetic: 14.4 us -> 1.84 us
  Pallas kernels: 502 us -> 491 us
  local copies, waits for them, and re-layouts: 36.8 us -> 28.4 us
    psum x3 -> x0, blocking collectives: 126 us -> none  [the longest x1 46.4 us: shards(): gv = lax.psum(gvec[:12], 'dp') / images_all]
    pallas_call x6 -> x4, Pallas kernels: 396 us -> 385 us  [the longest x1 133 us: front(): pl.pallas_call(front_kernel, in_specs=[vm, vm, vm], out_specs=[pl.BlockSp...]
    reshape x6 -> x1, local copies, waits for them, and re-layouts: 10.4 us -> 0.04 us  [shards(): low[own_units - extra:].reshape(12, D)]
    unnamed x34 -> x18, local copies, waits for them, and re-layouts: 17.8 us -> 25.1 us
  transfers between devices with their start and end apart: 2 -> 1, of which waited for: 0 -> 0; matrix products, arithmetic and copies ran while one was open for 3% -> 1% of each run, Pallas kernels for 0% -> 0%
where the time goes in v2:
time: 532 us; the launch traced here: 522 us
  Pallas kernels  491 us (92%)
  local copies, waits for them, and re-layouts  28.4 us (5%)
    pallas_call x1, Pallas kernels, front(): pl.pallas_call(front_kernel, in_specs=[vm, vm, vm], out_specs=[pl.BlockSp...  133 us
    pallas_call x1, Pallas kernels, back(): pl.pallas_call(functools.partial(back_kernel, lo=lo, hi=hi, ranges=ranges...  113 us
    pallas_call x1, Pallas kernels, tail_quick(): pl.pallas_call(functools.partial(tail_quick_kernel, scale=scale), in_spec...  111 us
    pallas_call x1, Pallas kernels, mlp(): pl.pallas_call(functools.partial(mlp_kernel, FB=FB, NB=NB), grid=(NB,), i...  106 us
    pallas_call x1, Pallas kernels, close(): pl.pallas_call(functools.partial(close_kernel, scale=scale), in_specs=[vm...  27.9 us
    unnamed x18, local copies, waits for them, and re-layouts  25.1 us
  transfers between devices with their start and end apart: 1, of which 0 were waited for; matrix products, arithmetic and copies ran while one was open for 1% of the time, Pallas kernels for 0%

profile of v2, /device:TPU:0, one launch (start us, length us, event | category | flops | bytes accessed | tf_op | source)
XLA Modules:
  0.0 522.5 jit_solution(8590392622228668276)
XLA Ops:
  0.6 0.8 slice_bitcast_fusion
  1.5 0.5 collective-permute-start
  2.0 0.8 slice.15
  2.8 0.0 copy-start.1
  2.8 4.0 copy.20.x_ref
  6.8 0.0 copy-done.1
  6.8 0.0 copy-start
  6.8 2.1 copy.21.g_ref
  8.9 0.6 pad.5.vec_own
  9.6 0.0 collective-permute-done
  9.6 0.0 copy-done
  9.6 0.4 fusion
  10.0 0.2 reshape_reshape.13
  10.2 0.3 reshape_reshape.14
  10.5 0.3 reshape_reshape.12
  10.8 0.2 copy.18
  11.0 1.4 fusion.1.own
  12.4 133.2 %front.1 = (bf16[32,3,128,1024]{3,2,1,0:T(8,128)(2,1)}, f32[16,1024]{1,0:T(8,128)}, bf16[3,2,592,1024]{3,2,1,0:T(8,128)(2,1)}, bf16[2,592,1024]{2,1,0:T(8,128)(2,1)}, bf16[2,592,1024]{2,1,0:T(8,128)(2,1)}) custom-call(bf16[3,128,1024]{2,1,0:T(8,128)(2,1)} %fusion.1.own, bf16[16,1024]{1,0:T(8,128)(2,1)} %pad.5.vec_own, bf16[2,577,1024]{2,1,0:T(8,128)(2,1)} %copy.20.x_ref), custom_call_target="tpu_custom_call" | custom-call | tf_op jit(solution)/shard_map/front/pallas_call | solution.py:642
  145.7 105.7 %mlp512.1 = (bf16[2,577,1024]{2,1,0:T(8,128)(2,1)}, bf16[32,4,32,1024]{3,2,1,0:T(8,128)(2,1)}, bf16[32,128,1024]{2,1,0:T(8,128)(2,1)}, bf16[8,128,1024]{2,1,0:T(...) custom-call(bf16[2,577,1024]{2,1,0:T(8,128)(2,1)} %copy.20.x_ref, ...), custom_call_target="tpu_custom_call" | custom-call | tf_op jit(solution)/shard_map/mlp512/pallas_call | solution.py:791
  251.4 5.5 %copy.23 = bf16[2,577,1024]{2,0,1:T(2,128)(2,1)} copy(bf16[2,577,1024]{2,1,0:T(8,128)(2,1)} %get-tuple-element.54) | data formatting | bytes 4726784
  256.9 112.9 %back.1 = (bf16[3,2,592,1024]{3,2,1,0:T(8,128)(2,1)}, f32[3,128,1024]{2,1,0:T(8,128)}) custom-call(bf16[3,2,592,1024]{3,2,1,0:T(8,128)(2,1)} %get-tuple-element.31.z_ref, bf16[2,592,1024]{2,1,0:T(8,128)(2,1)} %get-tuple-element.32.do_ref, bf16[8,128,1024]{2,1,0:T(8,128)(2,1)} %get-tuple-element.33.refs_0_, bf16[32,128,1024]{2,1,0:T(8,128)(2,1)} %bitcast.26, ...), custom_call_target="tpu_custom_call" | custom-call | tf_op jit(solution)/shard_map/back/pallas_call | solution.py:919
  369.8 110.8 %tail_quick.1 = (bf16[2,577,1024]{2,1,0:T(8,128)(2,1)}, f32[3,128,1024]{2,1,0:T(8,128)}, f32[16,1024]{1,0:T(8,128)}) custom-call(bf16[2,577,1024]{2,1,0:T(8,128)(2,1)} %copy.20.x_ref, bf16[3,2,592,1024]{3,2,1,0:T(8,128)(2,1)} %get-tuple-element.36.dz_ref, bf16[2,592,1024]{2,1,0:T(8,128)(2,1)} %get-tuple-element.37.n_ref, ...), custom_call_target="tpu_custom_call" | custom-call | tf_op jit(solution)/shard_map/tail_quick/pallas_call | solution.py:1026
  480.6 5.5 %copy.24 = bf16[2,577,1024]{2,0,1:T(2,128)(2,1)} copy(bf16[2,577,1024]{2,1,0:T(8,128)(2,1)} %get-tuple-element.55) | data formatting | bytes 4726784
  486.1 27.9 %close.1 = (f32[3075,128]{1,0:T(8,128)}, f32[3075,128]{1,0:T(8,128)}, f32[3075,128]{1,0:T(8,128)}, f32[3075,128]{1,0:T(8,128)}) custom-call(f32[3,128,1024]{2,1,0:T(8,128)} %get-tuple-element.41.chunk_a, f32[3,128,1024]{2,1,0:T(8,128)} %get-tuple-element.42.chunk_b, f32[16,1024]{1,0:T(8,128)} %get-tuple-element.43.gvec, f32[3075,128]{1,0:T(8,128)} %bitcast.27, ...), custom_call_target="tpu_custom_call" | custom-call | tf_op jit(solution)/shard_map/close/pallas_call | solution.py:1153
  514.0 0.0 copy-start.4
  514.0 2.8 copy.30
  516.8 0.0 copy-done.4
  516.8 1.2 copy.31
  518.1 0.7 copy-done.3
  518.8 1.2 copy.32
  520.0 0.7 copy-done.2
  520.8 1.2 copy.33
  (4 shorter events, 0.0 us)
Async XLA Ops:
  1.5 8.1 %collective-permute-start = (bf16[96,128]{1,0:T(8,128)(2,1)S(1)}, bf16[96,128]{1,0:T(8,128)(2,1)S(1)}, u32[]{:S(2)}, u32[]{:S(2)}) collective-permute-start(bf16[96,128]{1,0:T(8,128)(2,1)S(1)} %slice_bitcast_fusion), channel_id=1, source_target_pairs={{0,1},{1,2},{2,3},{3,4},{4,5},{5,6},{6,7},{7,8},{8,9},{9,10},{10,1... | collective-permute-start | bytes 73736 | tf_op jit(solution)/shard_map/ppermute | solution.py:1210
  2.8 4.0 copy-start.1
  6.8 2.8 copy-start
  514.0 2.8 copy-start.4
  516.8 2.0 copy-start.3
  518.8 2.0 copy-start.2

commit v3 on v2

--- a/solution.py
+++ b/solution.py
@@ -22,7 +22,6 @@
 EARLY = 1
 PER = 2
 FRONT_HI = 3
-BPER = 3
 
 EPS = 1e-06
 max_norm = 1.0
@@ -83,7 +82,8 @@
         dma = lambda n: pltpu.SemaphoreType.DMA((n,))
         return [dma(3 * 96), dma(24 * (hi - lo + 1)), dma(3)]
 
-    def __init__(s, c, lo, hi, own, w, sems):
+    def __init__(s, c, lo, hi, own, w, sems, base=0):
+        s.base = base
         s.c, s.lo, s.hi, s.own, s.w = c, lo, hi, own, w
         s.ssem, s.rsem, s.lsem = sems
         s.ns = 0
@@ -117,7 +117,7 @@
         i = s.ns
         s.ns += 1
         cp = pltpu.make_async_remote_copy(
-            src, s.w.at[dev, k], s.ssem.at[i], s.slot(dev, k), device_id=(to,), device_id_type=MESH
+            src, s.w.at[jnp.clip(dev - s.base, 0, s.w.shape[0] - 1), k], s.ssem.at[i], s.slot(dev, k), device_id=(to,), device_id_type=MESH
         )
         conds = [f for f in conds if f is not None]
         s.pend.append((i, conds))
@@ -129,6 +129,9 @@
             pl.when(functools.reduce(jnp.logical_and, [f() for f in conds]))(fn)
         else:
             fn()
+
+    def at_me(s):
+        return jnp.clip(s.c.me - s.base, 0, 8 * (s.hi + 1) - s.base - 1)
 
     def mine(s):
         return s.inside(s.c.z)
@@ -151,16 +154,16 @@
         @pl.when(s.mine())
         def _():
             for k in range(s.K):
-                pltpu.make_async_copy(s.own.at[k], s.w.at[s.c.me, k], s.lsem.at[k]).start()
+                pltpu.make_async_copy(s.own.at[k], s.w.at[s.at_me(), k], s.lsem.at[k]).start()
 
     def keep_wait(s):
         @pl.when(s.mine())
         def _():
             for k in range(s.K):
-                pltpu.make_async_copy(s.own.at[k], s.w.at[s.c.me, k], s.lsem.at[k]).wait()
+                pltpu.make_async_copy(s.own.at[k], s.w.at[s.at_me(), k], s.lsem.at[k]).wait()
 
     def wait(s, dev, k):
-        r = s.w.at[dev, k]
+        r = s.w.at[dev - s.base, k]
         pltpu.make_async_copy(r, r, s.slot(dev, k)).wait()
 
     def item(s, kind, dz, k):
@@ -178,7 +181,7 @@
 
         def body():
             s.wait(src, k)
-            r = s.w.at[src, k]
+            r = s.w.at[src - s.base, k]
             if kind == "z":
                 if (dz is None and s.lo < 3) or (dz is not None and dz < 0):
                     beyond = (lambda: c.z > s.lo) if dz is None and s.lo > 0 else None
@@ -194,14 +197,15 @@
 
         s.when([] if valid is None else [valid], body)
 
-    def sibling(s):
+    def sibling(s, ks=(0, 1, 2)):
         c = s.c
 
         def one(i, _):
-            s.wait(8 * s.lo + 2 * (i // s.K) + 1 - c.core, i % s.K)
+            for k in ks:
+                s.wait(8 * s.lo + 2 * i + 1 - c.core, k)
             return 0
 
-        lax.fori_loop(0, 4 * (s.hi - s.lo + 1) * s.K, one, 0)
+        lax.fori_loop(0, 4 * (s.hi - s.lo + 1), one, 0)
 
     def sent(s):
         for i, conds in s.pend:
@@ -268,7 +272,8 @@
             + [dma(12 * nz), dma(stage)]
         )
 
-    def __init__(s, c, lo, hi, parts, out, scr, scale, order, direct=False):
+    def __init__(s, c, lo, hi, parts, out, scr, scale, order, direct=False, auto=True):
+        s.auto = auto
         s.c, s.lo, s.hi, s.parts, s.out, s.scale, s.order, s.direct = c, lo, hi, parts, out, scale, order, direct
         s.S, s.B, s.A, s.Z, s.stage, s.sent_s, s.got_s, s.got_b, s.got_a, s.got_z, s.sent, s.loaded = scr
         s.nst = s.stage.shape[0]
@@ -301,7 +306,8 @@
 
     def places(s, order=None):
         for kind, zz, fa, k in order or s.order:
-            yield zz, 1 if kind == "b" else 0, fa, k
+            if kind != "f":
+                yield zz, 1 if kind == "b" else 0, fa, k
 
     def zero(s):
         c = s.c
@@ -332,13 +338,13 @@
     def load(s, i):
         if s.direct or i >= len(s.order):
             return
-        (place,) = s.places([s.order[i]])
+        kind, zz, fa, k = s.order[i]
         n = i % s.nst
 
         def go(r):
             pltpu.make_async_copy(r, s.stage.at[n], s.loaded.at[n]).start()
 
-        s.source(s.owner(*place[:3], s.c.core) * s.K + place[3], go)
+        s.source(s.owner(zz, 1 if kind == "b" else 0, fa, s.c.core) * s.K + k, go)
 
     def prefetch(s):
         for i in range(s.nst - 1):
@@ -380,44 +386,43 @@
         s.flush()
         n = s.slot(zz, fb, fa, k)
         out = s.S.at[n]
-        srcs = [own, out]
-        s.wait(out, s.got_s.at[n])
         bi = ((zz - s.lo) * 2 + fa) * K + k
-        ai = zi = (zz - s.lo) * K + k
+        zi = (zz - s.lo) * K + k
         z2 = s.nz * K + k
-        if kind in "az":
-            srcs.append(s.B.at[bi])
-            s.wait(s.B.at[bi], s.got_b.at[bi])
-        if kind == "z":
-            srcs.append(s.A.at[ai])
-            s.wait(s.A.at[ai], s.got_a.at[ai])
+
+        def gather(kinds):
+            srcs = [own]
+            if "S" in kinds:
+                srcs.append((out, s.got_s.at[n]))
+            if "B" in kinds:
+                srcs.append((s.B.at[bi], s.got_b.at[bi]))
+            if "A" in kinds:
+                srcs.append((s.A.at[zi], s.got_a.at[zi]))
+            for pair in srcs[1:]:
+                s.wait(*pair)
+            return srcs[:1] + [ref for ref, _ in srcs[1:]]
 
         def send(dst, sem, to):
             return pltpu.make_async_remote_copy(
-                s.S.at[n], dst, s.sent.at[n], sem, device_id=(to,), device_id_type=MESH
+                out, dst, s.sent.at[n], sem, device_id=(to,), device_id_type=MESH
             )
 
         if kind == "b":
-            s.sum(srcs, out)
+            s.sum(gather("S"), out)
             s.later.append(send(s.B.at[bi], s.got_b.at[bi], c.bp).start)
             s.waits.append((n, None))
         elif kind == "a":
-            s.sum(srcs, out)
-            s.later.append(send(s.A.at[ai], s.got_a.at[ai], c.ap).start)
+            s.sum(gather("SB"), out)
+            s.later.append(send(s.A.at[zi], s.got_a.at[zi], c.ap).start)
             s.waits.append((n, None))
-        else:
-            comes = jnp.where(c.z <= zz, c.z, 3 - c.z)
-            pl.when(comes > 0)(functools.partial(s.wait, s.Z.at[zi], s.got_z.at[zi]))
-            srcs.append(s.Z.at[zi])
+        elif kind == "z":
 
             @pl.when(c.z != zz)
             def _():
-                s.sum(srcs, out)
-
-            @pl.when(c.z == zz)
-            def _():
-                pl.when(c.hasup)(functools.partial(s.wait, s.Z.at[z2], s.got_z.at[z2]))
-                s.sum(srcs + [s.Z.at[z2]], s.out.at[k], s.scale)
+                srcs = gather("SBA")
+                comes = jnp.where(c.z <= zz, c.z, 3 - c.z)
+                pl.when(comes > 0)(functools.partial(s.wait, s.Z.at[zi], s.got_z.at[zi]))
+                s.sum(srcs + [s.Z.at[zi]], out)
 
             def on():
                 @pl.when(c.z < zz)
@@ -432,7 +437,17 @@
 
             s.later.append(on)
             s.waits.append((n, zz))
-        s.load(i + s.nst - 1)
+        else:
+
+            @pl.when(c.z == zz)
+            def _():
+                srcs = gather("SBA")
+                pl.when(c.hasdn)(functools.partial(s.wait, s.Z.at[zi], s.got_z.at[zi]))
+                pl.when(c.hasup)(functools.partial(s.wait, s.Z.at[z2], s.got_z.at[z2]))
+                s.sum(srcs + [s.Z.at[zi], s.Z.at[z2]], s.out.at[k], s.scale)
+
+        if s.auto:
+            s.load(i + s.nst - 1)
 
     def finish(s):
         s.flush()
@@ -443,27 +458,46 @@
             else:
                 pl.when(s.c.z != zz)(w)
 
-        def one(i, _):
-            s.wait(s.S.at[0], s.sent_s.at[i])
-            return 0
-
-        lax.fori_loop(0, 12 * s.nz, one, 0)
-
-
-def reduce_order(lo, hi):
-    order = []
-    planes = list(range(hi, lo - 1, -1))
-    b = lambda zz: [("b", zz, fa, k) for fa in (1, 0) for k in range(3)]
-    a = lambda zz: [("a", zz, 1, k) for k in range(3)]
-    z = lambda zz: [("z", zz, 0, k) for k in range(3)]
-    for i in range(len(planes) + 2):
-        if i < len(planes):
-            order += b(planes[i])
-        if 1 <= i <= len(planes):
-            order += a(planes[i - 1])
-        if i >= 2:
-            order += z(planes[i - 2])
-    return order
+        for place in s.places():
+            s.wait(s.S.at[0], s.sent_s.at[s.slot(*place)])
+
+
+BACK_STEPS = (
+    ("b301", "b211", "b310", "b212",),
+    ("b312", "b300", "b210",),
+    ("b311", "b110", "a211", "b100", "b201",),
+    (),
+    (),
+    ("b302",),
+    ("a311",),
+    ("a310",),
+    ("z301", "a312", "a210",),
+    ("z300", "b200", "a110", "b202",),
+    ("a212", "b111", "z302", "z201",),
+    (),
+    ("z200", "b112",),
+    ("b101", "a111", "z100",),
+    ("b102", "z202", "f302", "a112", "f301", "f300", "z101",),
+    ("f101", "f201", "f100", "f202", "z102",),
+    ("f102", "f200",),
+)
+TAIL_STEPS = (
+    (),
+    (),
+    ("b000", "b010",),
+    ("b011", "b001",),
+    ("a010", "a011", "b012", "b002",),
+    ("z000",),
+    ("a012", "f000", "z001",),
+    ("f001", "z002",),
+    ("f002",),
+)
+
+
+def reduce_order(groups):
+    order = [(t[0], int(t[1]), int(t[2]), int(t[3])) for g in groups for t in g]
+    ends = [sum(len(g) for g in groups[: i + 1]) for i in range(len(groups))]
+    return order, [list(range(e - len(g), e)) for e, g in zip(ends, groups)]
 
 
 def qkv_kernel(x_ref, vec_ref, w_ref, out_ref, n_ref):
@@ -877,12 +911,12 @@
         name="tail",
     )(x, dz, n1, dhid, vec, w.reshape(32, 3, 128, D), gvec)
 
-def back_kernel(z_ref, do_ref, *refs, lo, hi, ranges, scale, per):
+def back_kernel(z_ref, do_ref, *refs, lo, hi, ranges, scale):
     n = len(ranges)
     parts = [(a, b, r) for (a, b), r in zip(ranges, refs[:n])]
     dz_ref, chunk = refs[n : n + 2]
     c = Ctx()
-    order = reduce_order(lo, hi)
+    order, groups = reduce_order(BACK_STEPS)
     red = Reduce(c, lo, hi, parts, chunk, refs[n + 2 :], scale, order)
     red.zero()
     chunk[...] = jnp.zeros_like(chunk)
@@ -892,12 +926,12 @@
 
     def pair(t, _):
         for m in range(16):
-            if red.steps[m * per : (m + 1) * per]:
+            if groups[m]:
 
                 @pl.when(t == m)
                 def _():
-                    for step in red.steps[m * per : (m + 1) * per]:
-                        step()
+                    for i in groups[m]:
+                        red.steps[i]()
                     red.flush()
 
         i = t // 8
@@ -909,15 +943,15 @@
         return 0
 
     lax.fori_loop(0, 16, pair, 0)
-    for step in red.steps[16 * per :]:
-        step()
+    for i in groups[16]:
+        red.steps[i]()
     red.finish()
 
 
-def back(z, do, parts, lo, hi, ranges, scale, per=BPER):
+def back(z, do, parts, lo, hi, ranges, scale):
     vm = pl.BlockSpec(memory_space=pltpu.VMEM)
     return pl.pallas_call(
-        functools.partial(back_kernel, lo=lo, hi=hi, ranges=ranges, scale=scale, per=per),
+        functools.partial(back_kernel, lo=lo, hi=hi, ranges=ranges, scale=scale),
         in_specs=[vm, vm] + [pl.BlockSpec(memory_space=pl.ANY)] * len(parts),
         out_specs=[vm, vm],
         out_shape=[jax.ShapeDtypeStruct((3, 2, SQ, D), BF), jax.ShapeDtypeStruct((3, 128, D), F32)],
@@ -941,7 +975,7 @@
     x_ref, dz_ref, n_ref, dhid_ref, vec_ref, gvin_ref, w, gx_ref, chunk, gvec_ref, acc, gw, wq, qsem, *scr, scale
 ):
     c = Ctx()
-    order = [(kind, 0, fa, k) for k in range(3) for kind, fa in (("b", 1), ("b", 0), ("a", 1), ("z", 0))]
+    order, groups = reduce_order(TAIL_STEPS)
     red = Reduce(c, 0, 0, [(0, 24, gw)], chunk, scr, scale, order, direct=True)
     loads = [pltpu.make_async_copy(w.at[0:8, j], wq.at[j % 2], qsem.at[j]) for j in range(3)]
     loads[0].start()
@@ -950,11 +984,11 @@
     chunk[...] = jnp.zeros_like(chunk)
     gvec_ref[...] = gvin_ref[...]
     c.barrier()
-    queue = list(red.steps)
-
-    def take(*ids):
-        for i in ids:
-            queue[i]()
+
+    def take(n):
+        for i in groups[n]:
+            red.steps[i]()
+        red.flush()
 
     def weights(j):
         g = tn(n_ref[...].reshape(M, D), dz_ref[j].reshape(M, D)).astype(BF)
@@ -983,21 +1017,16 @@
     red.to_sibling(some(0))
     weights(1)
     red.to_sibling(some(1))
-    take(0, 1)
+    take(2)
     weights(2)
-    take(4, 5, 2)
+    colsum(2)
     red.to_sibling(some(2))
-    inputs(0)
-    loads[2].start()
-    take(8, 9, 6, 3)
-    red.flush()
-    inputs(1)
-    take(10, 7)
-    red.flush()
-    inputs(2)
-    take(11)
-    red.flush()
-    colsum(2)
+    take(3)
+    for j in range(3):
+        inputs(j)
+        if j == 0:
+            loads[2].start()
+        take(4 + j)
     a = b = jnp.zeros((CH, D), F32)
     la = lb = jnp.zeros((1, D), F32)
     for i in range(2):
@@ -1016,6 +1045,7 @@
         g, s1 = back_norm(x_ref[i, 576:577, :], dd, dhid_ref[r2, :], vec_ref)
         gx_ref[i, 576:577, :] = g
         la, lb = la + s1, lb + dd
+        take(7 + i)
     gvec_ref[8:9, :] = jnp.sum(a, axis=0, keepdims=True) + la
     gvec_ref[9:10, :] = jnp.sum(b, axis=0, keepdims=True) + lb
     red.finish()

time: 532 us -> 492 us (0.925)
  Pallas kernels: 491 us -> 451 us
    pallas_call x1, Pallas kernels: 111 us -> 85.2 us  [tail_quick(): pl.pallas_call(functools.partial(tail_quick_kernel, scale=scale), in_spec...]
    pallas_call x1, Pallas kernels: 113 us -> 98.2 us  [back(): pl.pallas_call(functools.partial(back_kernel, lo=lo, hi=hi, ranges=ranges...]
  transfers between devices with their start and end apart: 1 -> 1, of which waited for: 0 -> 0; matrix products, arithmetic and copies ran while one was open for 1% -> 2% of each run, Pallas kernels for 0% -> 0%
where the time goes in v3:
time: 492 us; the launch traced here: 482 us
  Pallas kernels  451 us (92%)
  local copies, waits for them, and re-layouts  28.4 us (6%)
    pallas_call x1, Pallas kernels, front(): pl.pallas_call(front_kernel, in_specs=[vm, vm, vm], out_specs=[pl.BlockSp...  133 us
    pallas_call x1, Pallas kernels, mlp(): pl.pallas_call(functools.partial(mlp_kernel, FB=FB, NB=NB), grid=(NB,), i...  106 us
    pallas_call x1, Pallas kernels, back(): pl.pallas_call(functools.partial(back_kernel, lo=lo, hi=hi, ranges=ranges...  98.2 us
    pallas_call x1, Pallas kernels, tail_quick(): pl.pallas_call(functools.partial(tail_quick_kernel, scale=scale), in_spec...  85.2 us
    pallas_call x1, Pallas kernels, close(): pl.pallas_call(functools.partial(close_kernel, scale=scale), in_specs=[vm...  28.2 us
    unnamed x18, local copies, waits for them, and re-layouts  25.1 us
  transfers between devices with their start and end apart: 1, of which 0 were waited for; matrix products, arithmetic and copies ran while one was open for 2% of the time, Pallas kernels for 0%

profile of v3, /device:TPU:0, one launch (start us, length us, event | category | flops | bytes accessed | tf_op | source)
XLA Modules:
  0.0 482.5 jit_solution(3798518735711427771)
XLA Ops:
  0.6 0.8 slice_bitcast_fusion
  1.5 0.5 collective-permute-start
  2.0 0.8 slice.15
  2.8 0.0 copy-start.1
  2.8 4.0 copy.20.x_ref
  6.8 0.0 copy-done.1
  6.8 0.0 copy-start
  6.8 2.1 copy.21.g_ref
  8.9 0.6 pad.5.vec_own
  9.6 0.0 collective-permute-done
  9.6 0.0 copy-done
  9.6 0.4 fusion
  10.0 0.2 reshape_reshape.13
  10.2 0.3 reshape_reshape.14
  10.5 0.3 reshape_reshape.12
  10.8 0.2 copy.18
  11.0 1.4 fusion.1.own
  12.4 133.2 %front.1 = (bf16[32,3,128,1024]{3,2,1,0:T(8,128)(2,1)}, f32[16,1024]{1,0:T(8,128)}, bf16[3,2,592,1024]{3,2,1,0:T(8,128)(2,1)}, bf16[2,592,1024]{2,1,0:T(8,128)(2,1)}, bf16[2,592,1024]{2,1,0:T(8,128)(2,1)}) custom-call(bf16[3,128,1024]{2,1,0:T(8,128)(2,1)} %fusion.1.own, bf16[16,1024]{1,0:T(8,128)(2,1)} %pad.5.vec_own, bf16[2,577,1024]{2,1,0:T(8,128)(2,1)} %copy.20.x_ref), custom_call_target="tpu_custom_call" | custom-call | tf_op jit(solution)/shard_map/front/pallas_call | solution.py:676
  145.6 105.7 %mlp512.1 = (bf16[2,577,1024]{2,1,0:T(8,128)(2,1)}, bf16[32,4,32,1024]{3,2,1,0:T(8,128)(2,1)}, bf16[32,128,1024]{2,1,0:T(8,128)(2,1)}, bf16[8,128,1024]{2,1,0:T(...) custom-call(bf16[2,577,1024]{2,1,0:T(8,128)(2,1)} %copy.20.x_ref, ...), custom_call_target="tpu_custom_call" | custom-call | tf_op jit(solution)/shard_map/mlp512/pallas_call | solution.py:825
  251.3 5.5 %copy.23 = bf16[2,577,1024]{2,0,1:T(2,128)(2,1)} copy(bf16[2,577,1024]{2,1,0:T(8,128)(2,1)} %get-tuple-element.54) | data formatting | bytes 4726784
  256.8 98.2 %back.1 = (bf16[3,2,592,1024]{3,2,1,0:T(8,128)(2,1)}, f32[3,128,1024]{2,1,0:T(8,128)}) custom-call(bf16[3,2,592,1024]{3,2,1,0:T(8,128)(2,1)} %get-tuple-element.31.z_ref, bf16[2,592,1024]{2,1,0:T(8,128)(2,1)} %get-tuple-element.32.do_ref, bf16[8,128,1024]{2,1,0:T(8,128)(2,1)} %get-tuple-element.33.refs_0_, bf16[32,128,1024]{2,1,0:T(8,128)(2,1)} %bitcast.26, ...), custom_call_target="tpu_custom_call" | custom-call | tf_op jit(solution)/shard_map/back/pallas_call | solution.py:953
  355.0 85.2 %tail_quick.1 = (bf16[2,577,1024]{2,1,0:T(8,128)(2,1)}, f32[3,128,1024]{2,1,0:T(8,128)}, f32[16,1024]{1,0:T(8,128)}) custom-call(bf16[2,577,1024]{2,1,0:T(8,128)(2,1)} %copy.20.x_ref, bf16[3,2,592,1024]{3,2,1,0:T(8,128)(2,1)} %get-tuple-element.36.dz_ref, bf16[2,592,1024]{2,1,0:T(8,128)(2,1)} %get-tuple-element.37.n_ref, ...), custom_call_target="tpu_custom_call" | custom-call | tf_op jit(solution)/shard_map/tail_quick/pallas_call | solution.py:1056
  440.3 5.5 %copy.24 = bf16[2,577,1024]{2,0,1:T(2,128)(2,1)} copy(bf16[2,577,1024]{2,1,0:T(8,128)(2,1)} %get-tuple-element.55) | data formatting | bytes 4726784
  445.8 28.2 %close.1 = (f32[3075,128]{1,0:T(8,128)}, f32[3075,128]{1,0:T(8,128)}, f32[3075,128]{1,0:T(8,128)}, f32[3075,128]{1,0:T(8,128)}) custom-call(f32[3,128,1024]{2,1,0:T(8,128)} %get-tuple-element.41.chunk_a, f32[3,128,1024]{2,1,0:T(8,128)} %get-tuple-element.42.chunk_b, f32[16,1024]{1,0:T(8,128)} %get-tuple-element.43.gvec, f32[3075,128]{1,0:T(8,128)} %bitcast.27, ...), custom_call_target="tpu_custom_call" | custom-call | tf_op jit(solution)/shard_map/close/pallas_call | solution.py:1183
  474.0 0.0 copy-start.4
  474.0 2.8 copy.30
  476.8 0.0 copy-done.4
  476.8 1.2 copy.31
  478.1 0.7 copy-done.3
  478.8 1.2 copy.32
  480.0 0.7 copy-done.2
  480.8 1.2 copy.33
  (4 shorter events, 0.0 us)
Async XLA Ops:
  1.5 8.1 %collective-permute-start = (bf16[96,128]{1,0:T(8,128)(2,1)S(1)}, bf16[96,128]{1,0:T(8,128)(2,1)S(1)}, u32[]{:S(2)}, u32[]{:S(2)}) collective-permute-start(bf16[96,128]{1,0:T(8,128)(2,1)S(1)} %slice_bitcast_fusion), channel_id=1, source_target_pairs={{0,1},{1,2},{2,3},{3,4},{4,5},{5,6},{6,7},{7,8},{8,9},{9,10},{10,1... | collective-permute-start | bytes 73736 | tf_op jit(solution)/shard_map/ppermute | solution.py:1240
  2.8 4.0 copy-start.1
  6.8 2.8 copy-start
  474.0 2.8 copy-start.4
  476.8 2.0 copy-start.3
  478.8 2.0 copy-start.2

commit v4 on v3

--- a/solution.py
+++ b/solution.py
@@ -19,9 +19,6 @@
 F32 = jnp.float32
 MESH = pl.DeviceIdType.MESH
 VMEM_ALL = 67043328
-EARLY = 1
-PER = 2
-FRONT_HI = 3
 
 EPS = 1e-06
 max_norm = 1.0
@@ -77,51 +74,13 @@
 class Gather:
     K = 3
 
-    @staticmethod
-    def sems(lo, hi):
-        dma = lambda n: pltpu.SemaphoreType.DMA((n,))
-        return [dma(3 * 96), dma(24 * (hi - lo + 1)), dma(3)]
-
-    def __init__(s, c, lo, hi, own, w, sems, base=0):
-        s.base = base
-        s.c, s.lo, s.hi, s.own, s.w = c, lo, hi, own, w
-        s.ssem, s.rsem, s.lsem = sems
+    def __init__(s, c, own, w, ssem, rsem, lsem):
+        s.c, s.own, s.w, s.ssem, s.rsem, s.lsem = c, own, w, ssem, rsem, lsem
         s.ns = 0
         s.pend = []
-        s.steps = []
-        kinds = (("z", 0), ("a", 1), ("b", 1), ("ba", 2))
-        for dist in range(1, 6):
-            for k in range(s.K):
-                if lo == hi:
-                    continue
-                for sign in (1, -1):
-                    for kind, extra in kinds:
-                        dz = dist - extra
-                        if dz < 0 or (kind == "z" and dz == 0) or (dz == 0 and sign < 0):
-                            continue
-                        if (sign > 0 and dz > hi) or (sign < 0 and dz > 3 - lo):
-                            continue
-                        s.steps.append(functools.partial(s.item, kind, sign * dz, k))
-        if lo == hi:
-            s.steps = [functools.partial(s.item, kind, None, k) for kind, _ in kinds[:1] for k in range(s.K)]
-            s.steps += [functools.partial(s.item, kind, None, k) for k in range(s.K) for kind in ("a", "b")]
-            s.steps += [functools.partial(s.item, "ba", None, k) for k in range(s.K)]
-
-    def inside(s, zz):
-        return jnp.logical_and(zz >= s.lo, zz <= s.hi)
 
     def slot(s, dev, k):
-        return s.rsem.at[jnp.clip((dev - 8 * s.lo) * s.K + k, 0, 24 * (s.hi - s.lo + 1) - 1)]
-
-    def send(s, src, dev, k, to, *conds):
-        i = s.ns
-        s.ns += 1
-        cp = pltpu.make_async_remote_copy(
-            src, s.w.at[jnp.clip(dev - s.base, 0, s.w.shape[0] - 1), k], s.ssem.at[i], s.slot(dev, k), device_id=(to,), device_id_type=MESH
-        )
-        conds = [f for f in conds if f is not None]
-        s.pend.append((i, conds))
-        s.when(conds, cp.start)
+        return s.rsem.at[dev * s.K + k]
 
     @staticmethod
     def when(conds, fn):
@@ -130,82 +89,74 @@
         else:
             fn()
 
-    def at_me(s):
-        return jnp.clip(s.c.me - s.base, 0, 8 * (s.hi + 1) - s.base - 1)
-
-    def mine(s):
-        return s.inside(s.c.z)
-
-    def start(s, ks, routes):
+    def send(s, src, dev, k, to, outer, *conds):
+        i = s.ns
+        s.ns += 1
+        cp = pltpu.make_async_remote_copy(
+            src, s.w.at[dev, k], s.ssem.at[i], s.slot(dev, k), device_id=(to,), device_id_type=MESH
+        )
+        s.pend.append((i, outer + list(conds)))
+        s.when(list(conds), cp.start)
+
+    def step(s, text):
+        kind = text[0]
+        zz, k = int(text[-2]), int(text[-1])
+        if kind == "o":
+            s.give(text[1], zz, k)
+        else:
+            s.item(kind, zz, k)
+
+    def give(s, route, zz, k):
         c = s.c
-        to = dict(
-            dn=(c.dn, lambda: c.hasdn), up=(c.up, lambda: c.hasup), b=(c.bp, None), a=(c.ap, None), s=(c.sib, None)
-        )
-
-        @pl.when(s.mine())
-        def _():
-            for k in ks:
-                for r in routes:
-                    s.send(s.own.at[k], c.me, k, to[r][0], to[r][1])
-                    i, conds = s.pend.pop()
-                    s.pend.append((i, conds + [s.mine]))
-
-    def keep(s):
-        @pl.when(s.mine())
-        def _():
-            for k in range(s.K):
-                pltpu.make_async_copy(s.own.at[k], s.w.at[s.at_me(), k], s.lsem.at[k]).start()
-
-    def keep_wait(s):
-        @pl.when(s.mine())
-        def _():
-            for k in range(s.K):
-                pltpu.make_async_copy(s.own.at[k], s.w.at[s.at_me(), k], s.lsem.at[k]).wait()
-
-    def wait(s, dev, k):
-        r = s.w.at[dev - s.base, k]
-        pltpu.make_async_copy(r, r, s.slot(dev, k)).wait()
-
-    def item(s, kind, dz, k):
+        to, conds = dict(
+            d=(c.dn, [lambda: c.hasdn]), u=(c.up, [lambda: c.hasup]), b=(c.bp, []), a=(c.ap, []), s=(c.sib, [])
+        )[route]
+        here = [lambda: c.z == zz]
+        s.when(here, lambda: s.send(s.own.at[k], c.me, k, to, here, *conds))
+
+    def item(s, kind, zz, k):
         c = s.c
-        if dz is None:
-            src = c.me + 8 * (s.lo - c.z)
-            valid = (lambda: c.z != s.lo) if kind == "z" else None
-        else:
-            src = c.me + 8 * dz
-            valid = lambda: s.inside(c.z + dz)
-        if "a" in kind:
+        src = c.me + 8 * (zz - c.z)
+        if kind in "ac":
             src = src + c.astep * (1 - 2 * c.abit)
-        if "b" in kind:
+        if kind in "bc":
             src = src + c.bstep * (1 - 2 * c.bbit)
+        outer = [lambda: c.z != zz] if kind == "z" else []
 
         def body():
             s.wait(src, k)
-            r = s.w.at[src - s.base, k]
+            r = s.w.at[src, k]
             if kind == "z":
-                if (dz is None and s.lo < 3) or (dz is not None and dz < 0):
-                    beyond = (lambda: c.z > s.lo) if dz is None and s.lo > 0 else None
-                    s.send(r, src, k, c.up, lambda: c.hasup, valid, beyond)
-                if (dz is None and s.lo > 0) or (dz is not None and dz > 0):
-                    beyond = (lambda: c.z < s.lo) if dz is None and s.lo < 3 else None
-                    s.send(r, src, k, c.dn, lambda: c.hasdn, valid, beyond)
-            if kind in ("z", "a"):
-                s.send(r, src, k, c.bp, valid)
+                if zz < 2:
+                    s.send(r, src, k, c.up, outer, lambda: c.z > zz, lambda: c.hasup)
+                if zz > 1:
+                    s.send(r, src, k, c.dn, outer, lambda: c.z < zz, lambda: c.hasdn)
+            if kind in "za":
+                s.send(r, src, k, c.bp, outer)
             if kind == "z":
-                s.send(r, src, k, c.ap, valid)
-            s.send(r, src, k, c.sib, valid)
-
-        s.when([] if valid is None else [valid], body)
-
-    def sibling(s, ks=(0, 1, 2)):
-        c = s.c
-
+                s.send(r, src, k, c.ap, outer)
+            s.send(r, src, k, c.sib, outer)
+
+        s.when(outer, body)
+
+    def wait(s, dev, k):
+        r = s.w.at[dev, k]
+        pltpu.make_async_copy(r, r, s.slot(dev, k)).wait()
+
+    def keep(s):
+        for k in range(s.K):
+            pltpu.make_async_copy(s.own.at[k], s.w.at[s.c.me, k], s.lsem.at[k]).start()
+
+    def kept(s, k):
+        pltpu.make_async_copy(s.own.at[k], s.w.at[s.c.me, k], s.lsem.at[k]).wait()
+
+    def sibling(s, first, last, ks):
         def one(i, _):
             for k in ks:
-                s.wait(8 * s.lo + 2 * i + 1 - c.core, k)
+                s.wait(2 * i + 1 - s.c.core, k)
             return 0
 
-        lax.fori_loop(0, 4 * (s.hi - s.lo + 1), one, 0)
+        lax.fori_loop(first, last, one, 0)
 
     def sent(s):
         for i, conds in s.pend:
@@ -598,57 +549,68 @@
         n_ref[i, 576:592, :] = jnp.concatenate([last, jnp.zeros((15, D), F32)], axis=0).astype(BF)
 
 
-def front_kernel(own, vec_own, x_ref, w, vec, z_ref, n_ref, mix_ref, vlow, wq, qsem, vsem, *sems):
+FRONT_STEPS = (
+    ("oa31", "oa30", "ou00", "oa01", "od11", "ob20", "os21", "os00", "os31", "ob31", "ob30", "ou31", "ob00", "oa32", "ou01", "ob10", "oa20", "ob21", "od32", "oa10", "z00",),
+    ("od10", "os01", "ob01", "od31", "b00", "ou32", "oa00", "z01", "ou02", "ob02", "od20", "od12", "a00", "os12", "z02", "os30", "a01", "os02", "oa02", "ob32", "b02", "od30", "a02", "od21", "os32", "oa21", "os20", "os11", "oa11", "ou20", "ob22", "oa22", "ob12", "z10", "c00", "z11", "ou10", "c01", "os10", "od22", "ob11", "b01", "ou11",),
+    ("z12", "z20", "os22", "z21", "ou21", "ou12", "oa12", "c02",),
+    ("a11",),
+    ("a10", "z22", "b10", "ou22",),
+    ("b11", "a21", "a20",),
+    ("ou30", "a12",),
+    (),
+    ("a22", "z31",),
+    (),
+    (),
+    (),
+    ("z30", "c10", "z32", "b20",),
+    (),
+    ("b31", "a30",),
+    (),
+    ("c20", "b30",),
+    ("a31", "c21", "c12", "b22", "c11", "a32",),
+    ("b21", "c30", "b32", "c22",),
+    ("b12", "c31",),
+    ("c32",),
+)
+
+
+def front_kernel(own, vec_own, x_ref, w, vec, z_ref, n_ref, mix_ref, vlow, wq, qsem, vsem, ssem, rsem, lsem):
     c = Ctx()
-    zero = Gather(c, 0, 0, own, w, sems[:3])
-    rest = Gather(c, 1, FRONT_HI, own, w, sems[3:])
+    g = Gather(c, own, w, ssem, rsem, lsem)
     vector = Vector(c, vec_own, vlow, vsem)
     vector.tell()
     c.barrier(jnp.where(c.me == 31, 31, 0))
     vector.start()
-    zero.start((0, 1, 2), ("up", "b", "a", "s"))
-    rest.start((0, 1, 2), ("dn",))
-    rest.start(range(EARLY), ("b", "a"))
-    rest.start((0, 1, 2), ("s",))
-    zero.keep()
-    rest.keep()
-    for step in zero.steps[:3]:
-        step()
-    for step in zero.steps[3:]:
-        step()
-    rest.start((0, 1, 2), ("up",))
-    rest.start(range(EARLY, 3), ("b", "a"))
-    zero.keep_wait()
-    zero.sibling()
-    loads = [pltpu.make_async_copy(w.at[0:8, j], wq.at[j % 2], qsem.at[j]) for j in range(3)]
-    loads[0].start()
-    loads[1].start()
+    g.keep()
+
+    def take(n):
+        for text in FRONT_STEPS[n]:
+            g.step(text)
+
+    take(0)
     vector.wait()
     vec[...] = vlow[...].astype(F32)
     norm_one(x_ref, vec, n_ref)
-    per = PER
-    steps = list(rest.steps)
     for j in range(3):
-        for step in steps[:per]:
-            step()
-        steps = steps[per:]
-        loads[j].wait()
+        take(1 + j)
+        g.kept(j)
+        g.sibling(0, 4, (j,))
+        load = pltpu.make_async_copy(w.at[0:8, j], wq.at[j % 2], qsem.at[j])
+        load.start()
+        load.wait()
         for i in range(2):
             r = nn(n_ref[i], wq[j % 2].reshape(D, D))
             if j != 1:
                 r = r + vec[j // 2 : j // 2 + 1, :]
             z_ref[j, i] = r.astype(BF)
-        if j == 0:
-            loads[2].start()
 
     def pair(t, _):
         for n in range(16):
-            if steps[n * per : (n + 1) * per]:
+            if FRONT_STEPS[4 + n]:
 
                 @pl.when(t == n)
                 def _():
-                    for step in steps[n * per : (n + 1) * per]:
-                        step()
+                    take(4 + n)
 
         i = t // 8
         cols = pl.ds(pl.multiple_of((t % 8) * 128, 128), 128)
@@ -661,12 +623,9 @@
         return 0
 
     lax.fori_loop(0, 16, pair, 0)
-    for step in steps[16 * per :]:
-        step()
-    rest.sibling()
-    rest.keep_wait()
-    zero.sent()
-    rest.sent()
+    take(20)
+    g.sibling(4, 16, (0, 1, 2))
+    g.sent()
     vector.sent()
 
 
@@ -685,8 +644,7 @@
             jax.ShapeDtypeStruct((2, SQ, D), BF),
         ],
         scratch_shapes=[pltpu.VMEM((16, D), BF), pltpu.VMEM((2, 8, 128, D), BF), dma(3), dma(32)]
-        + Gather.sems(0, 0)
-        + Gather.sems(1, FRONT_HI),
+        + [dma(240), dma(96), dma(3)],
         compiler_params=pltpu.CompilerParams(collective_id=1, has_side_effects=True, vmem_limit_bytes=VMEM_ALL),
         name="front",
     )(own, vec_own, x)
@@ -775,14 +733,19 @@
     bup=row[:,:FB]
     for t in range(1,nper): bup=jnp.where(jb%nper==t,row[:,t*FB:(t+1)*FB],bup)
     g=gs[...]; n=n2[...]
-    pre=nn(n,wu)+bup
-    cdf=0.5*(1.0+lax.erf(pre*0.7071067811865476))
-    act=(pre*cdf).astype(BF)
-    slope=cdf+pre*0.3989422804014327*jnp.exp(-0.5*pre*pre)
-    dpf=nt(g,wd)*slope
-    dp=dpf.astype(BF)
-    acc[...]+=nn(act,wd)
-    dn[...]+=nt(dp,wu)
+    acts=[];dps=[]
+    pres=[nn(n[i*SQ:(i+1)*SQ],wu)+bup for i in range(2)]
+    das=[nt(g[i*SQ:(i+1)*SQ],wd) for i in range(2)]
+    for i in range(2):
+        pre=pres[i]
+        cdf=0.5*(1.0+lax.erf(pre*0.7071067811865476))
+        act=(pre*cdf).astype(BF)
+        slope=cdf+pre*0.3989422804014327*jnp.exp(-0.5*pre*pre)
+        dp=(das[i]*slope).astype(BF)
+        acc[i*SQ:(i+1)*SQ,:]+=nn(act,wd)
+        dn[i*SQ:(i+1)*SQ,:]+=nt(dp,wu)
+        acts.append(act);dps.append(dp)
+    act=jnp.concatenate(acts,axis=0);dp=jnp.concatenate(dps,axis=0)
     gup_ref[...]=tn(n,dp).astype(BF).reshape(gup_ref.shape)
     gdn_ref[...]=tn(act,g).astype(BF).reshape(gdn_ref.shape)
     bsum=jnp.sum(dp.astype(F32),axis=0,keepdims=True)
@@ -1074,7 +1037,7 @@
     )(x, dz, n1, dhid, vec, gvec, w)
 
 
-def close_kernel(chunk_a, chunk_b, gvec, p_ref, m_ref, v_ref, wg, pn, mn, vn, flat, e, es, ea, eb, ez, sem, *, scale):
+def close_kernel(chunk_a, chunk_b, gvec, wg, clip_ref, flat, e, es, ea, eb, ez, sem, *, scale):
     c = Ctx()
     me = c.me
     bar = pltpu.get_barrier_semaphore()
@@ -1114,8 +1077,8 @@
         return t + v * v
 
     sq = jnp.sum(lax.fori_loop(0, 48, square, jnp.zeros((64, 128), F32)))
-    e[0:16, :] = gvec[...]
-    e[16:24, :] = jnp.full((8, D), sq, F32)
+    e[0:12, :] = gvec[0:12, :]
+    e[12:16, :] = jnp.full((4, D), sq, F32)
     pl.semaphore_wait(bar, 6 + jnp.where(first, 0, 1) + jnp.where(last, 0, 1))
     head = flat.at[0:96]
     room = flat.at[3072:3168]
@@ -1142,9 +1105,9 @@
         zz = lax.rem(c.z + 4 - i, 4)
         pltpu.make_async_copy(ez.at[zz], ez.at[zz], sem.at[9 + i]).wait()
     total = ((ez[0] + ez[1]) + ez[2]) + ez[3]
-    vec = total[0:12, :] * scale
-    square_sum = total[16:17, 0:1] + jnp.sum(vec * vec)
-    clip = jnp.minimum(1.0, max_norm / (jnp.sqrt(square_sum) + 1e-06))
+    vec = total[0:12, :]
+    square_sum = (total[12:13, 0:128] + jnp.sum(vec * vec)) * (scale * scale)
+    clip_ref[...] = jnp.broadcast_to(jnp.minimum(1.0, max_norm / (jnp.sqrt(square_sum) + 1e-06)), (8, 128))
 
     @pl.when(last)
     def _():
@@ -1157,40 +1120,28 @@
 
     pl.when(jnp.logical_not(first))(edge.wait_send)
 
-    def apply(g, rows):
-        w = clip * g
-        m1 = beta_one * m_ref[rows, :] + (1.0 - beta_one) * w
-        m2 = beta_two * v_ref[rows, :] + (1.0 - beta_two) * w * w
-        par = p_ref[rows, :]
-        step = m1 / (1.0 - beta_one**STEP) / (jnp.sqrt(m2 / (1.0 - beta_two**STEP)) + adam_eps)
-        wg[rows, :] = g
-        pn[rows, :] = par - learn_rate * (step + decay_rate * par)
-        mn[rows, :] = m1
-        vn[rows, :] = m2
-
     def block(i, _):
-        apply(flat[pl.ds(i * 64 + 3 * me, 64), :], pl.ds(pl.multiple_of(i * 64, 64), 64))
+        wg[pl.ds(pl.multiple_of(i * 64, 64), 64), :] = flat[pl.ds(i * 64 + 3 * me, 64), :]
         return 0
 
     lax.fori_loop(0, 48, block, 0)
-    apply(flat[pl.ds(3072 + 3 * me, 3), :], slice(3072, 3075))
-
-
-def close(chunk_a, chunk_b, gvec, params, moment_one, moment_two, scale):
+    wg[3072:3075, :] = flat[pl.ds(3072 + 3 * me, 3), :]
+
+
+def close(chunk_a, chunk_b, gvec, scale):
     vm = pl.BlockSpec(memory_space=pltpu.VMEM)
-    own = jax.ShapeDtypeStruct((3075, 128), F32)
-    small = pltpu.VMEM((24, D), F32)
+    small = pltpu.VMEM((16, D), F32)
     return pl.pallas_call(
         functools.partial(close_kernel, scale=scale),
-        in_specs=[vm] * 6,
-        out_specs=[vm] * 4,
-        out_shape=[own] * 4,
+        in_specs=[vm] * 3,
+        out_specs=[vm] * 2,
+        out_shape=[jax.ShapeDtypeStruct((3075, 128), F32), jax.ShapeDtypeStruct((8, 128), F32)],
         scratch_shapes=[pltpu.VMEM((3168, 128), F32)]
         + [small] * 4
-        + [pltpu.VMEM((4, 24, D), F32), pltpu.SemaphoreType.DMA((16,))],
+        + [pltpu.VMEM((4, 16, D), F32), pltpu.SemaphoreType.DMA((16,))],
         compiler_params=pltpu.CompilerParams(collective_id=4, has_side_effects=True, vmem_limit_bytes=VMEM_ALL),
         name="close",
-    )(chunk_a, chunk_b, gvec, *(v.reshape(3075, 128) for v in (params, moment_one, moment_two)))
+    )(chunk_a, chunk_b, gvec)
 
 
 def to_pieces(rows, first):
@@ -1211,8 +1162,7 @@
     return jnp.where(p < 24, three, jnp.where((p >= 32) & (p < 64), four, plain))
 
 
-def update(params, moment_one, moment_two, weight_grad, square_sum):
-    clip_factor = jnp.minimum(1.0, max_norm / (jnp.sqrt(square_sum) + 1e-06))
+def update(params, moment_one, moment_two, weight_grad, clip_factor):
     clipped = clip_factor * weight_grad
     moment_one_new = beta_one * moment_one + (1.0 - beta_one) * clipped
     moment_two_new = beta_two * moment_two + (1.0 - beta_two) * clipped * clipped
@@ -1246,10 +1196,12 @@
         flat_w = w.reshape(PIECES, 128, D)
         outputs, gup, gdn, gout, dmix, dhid, gvec = mlp(tokens, cotangent, mixed, vec, flat_w)
         parts = [gout, gup.reshape(32, 128, D), gdn]
-        dz, chunk_a = back(z, dmix, parts, 1, 3, [(24, 32), (32, 64), (64, 96)], scale)
-        grad_tokens, chunk_b, gvec = tail_quick(tokens, dz, n1, dhid, vec, gvec, w, scale)
-        news = close(chunk_a, chunk_b, gvec, params, moment_one, moment_two, scale)
-        return (outputs, grad_tokens, *(v.reshape(shard_len) for v in news))
+        dz, chunk_a = back(z, dmix, parts, 1, 3, [(24, 32), (32, 64), (64, 96)], None)
+        grad_tokens, chunk_b, gvec = tail_quick(tokens, dz, n1, dhid, vec, gvec, w, None)
+        sums, clip = close(chunk_a, chunk_b, gvec, scale)
+        weight_grad = sums.reshape(shard_len) * scale
+        news = update(params, moment_one, moment_two, weight_grad, clip[0, 0])
+        return (outputs, grad_tokens, weight_grad, *news)
     flat = lax.all_gather(params.astype(BF), "dp", axis=0, tiled=True)
     w = to_pieces(flat[:mats].reshape(-1, D), 0)
     vec = jnp.pad(flat[mats:].reshape(12, D).astype(F32), ((0, 4), (0, 0)))
@@ -1263,7 +1215,8 @@
     arrived = lax.all_to_all(flat.reshape(n, shard_len), "dp", split_axis=0, concat_axis=0, tiled=True)
     weight_grad = jnp.sum(arrived.astype(F32), axis=0) * scale
     square_sum = lax.psum(jnp.sum(weight_grad * weight_grad), "dp")
-    news = update(params, moment_one, moment_two, weight_grad, square_sum)
+    clip = jnp.minimum(1.0, max_norm / (jnp.sqrt(square_sum) + 1e-06))
+    news = update(params, moment_one, moment_two, weight_grad, clip)
     return (outputs, grad_tokens, weight_grad, *news)
 
 

time: 492 us -> 477 us (0.970)
  Pallas kernels: 451 us -> 432 us
  other arithmetic: 1.84 us -> 9.61 us
  local copies, waits for them, and re-layouts: 28.4 us -> 23.4 us
    pallas_call x1, Pallas kernels: 85.2 us -> 73.6 us  [tail_quick(): pl.pallas_call(functools.partial(tail_quick_kernel, scale=scale), in_spec...]
    pallas_call x1, Pallas kernels: 28.2 us -> 20.8 us  [close(): pl.pallas_call(functools.partial(close_kernel, scale=scale), in_specs=[vm...]
    unnamed x18 -> x14, local copies, waits for them, and re-layouts: 25.1 us -> 18 us
where the time goes in v4:
time: 477 us; the launch traced here: 468 us
  Pallas kernels  432 us (91%)
  local copies, waits for them, and re-layouts  23.4 us (5%)
  other arithmetic  9.61 us (2%)
    pallas_call x1, Pallas kernels, front(): pl.pallas_call(front_kernel, in_specs=[vm, vm, vm], out_specs=[pl.BlockSp...  137 us
    pallas_call x1, Pallas kernels, mlp(): pl.pallas_call(functools.partial(mlp_kernel, FB=FB, NB=NB), grid=(NB,), i...  102 us
    pallas_call x1, Pallas kernels, back(): pl.pallas_call(functools.partial(back_kernel, lo=lo, hi=hi, ranges=ranges...  98.9 us
    pallas_call x1, Pallas kernels, tail_quick(): pl.pallas_call(functools.partial(tail_quick_kernel, scale=scale), in_spec...  73.6 us
    pallas_call x1, Pallas kernels, close(): pl.pallas_call(functools.partial(close_kernel, scale=scale), in_specs=[vm...  20.8 us
    unnamed x14, local copies, waits for them, and re-layouts  18 us
  transfers between devices with their start and end apart: 1, of which 0 were waited for; matrix products, arithmetic and copies ran while one was open for 2% of the time, Pallas kernels for 0%

profile of v4, /device:TPU:0, one launch (start us, length us, event | category | flops | bytes accessed | tf_op | source)
XLA Modules:
  0.0 467.7 jit_solution(15904511848396279946)
XLA Ops:
  0.6 0.8 slice_bitcast_fusion
  1.5 0.5 collective-permute-start
  2.0 0.8 slice.19
  2.8 0.0 copy-start.4
  2.8 4.0 copy.20.x_ref
  6.8 0.0 copy-done.4
  6.8 0.0 copy-start
  6.8 2.1 copy.21.g_ref
  8.9 0.6 pad.5.vec_own
  9.6 0.0 collective-permute-done
  9.6 0.0 copy-done
  9.6 0.4 fusion.2
  10.0 0.2 reshape_reshape.13
  10.2 1.2 reshape_reshape.14
  11.4 0.2 reshape_reshape.12
  11.6 0.0 copy-start.3
  11.6 0.2 copy.18
  11.9 0.9 copy-done.3
  12.8 1.5 fusion.3.own
  14.3 137.0 %front.1 = (bf16[32,3,128,1024]{3,2,1,0:T(8,128)(2,1)}, f32[16,1024]{1,0:T(8,128)}, bf16[3,2,592,1024]{3,2,1,0:T(8,128)(2,1)}, bf16[2,592,1024]{2,1,0:T(8,128)(2,1)}, bf16[2,592,1024]{2,1,0:T(8,128)(2,1)}) custom-call(bf16[3,128,1024]{2,1,0:T(8,128)(2,1)} %fusion.3.own, bf16[16,1024]{1,0:T(8,128)(2,1)} %pad.5.vec_own, bf16[2,577,1024]{2,1,0:T(8,128)(2,1)} %copy.20.x_ref), custom_call_target="tpu_custom_call" | custom-call | tf_op jit(solution)/shard_map/front/pallas_call | solution.py:635
  151.3 102.1 %mlp512.1 = (bf16[2,577,1024]{2,1,0:T(8,128)(2,1)}, bf16[32,4,32,1024]{3,2,1,0:T(8,128)(2,1)}, bf16[32,128,1024]{2,1,0:T(8,128)(2,1)}, bf16[8,128,1024]{2,1,0:T(...) custom-call(bf16[2,577,1024]{2,1,0:T(8,128)(2,1)} %copy.20.x_ref, ...), custom_call_target="tpu_custom_call" | custom-call | tf_op jit(solution)/shard_map/mlp512/pallas_call | solution.py:788
  253.4 5.5 %copy.23 = bf16[2,577,1024]{2,0,1:T(2,128)(2,1)} copy(bf16[2,577,1024]{2,1,0:T(8,128)(2,1)} %get-tuple-element.50) | data formatting | bytes 4726784
  258.9 98.9 %back.1 = (bf16[3,2,592,1024]{3,2,1,0:T(8,128)(2,1)}, f32[3,128,1024]{2,1,0:T(8,128)}) custom-call(bf16[3,2,592,1024]{3,2,1,0:T(8,128)(2,1)} %get-tuple-element.29.z_ref, bf16[2,592,1024]{2,1,0:T(8,128)(2,1)} %get-tuple-element.30.do_ref, bf16[8,128,1024]{2,1,0:T(8,128)(2,1)} %get-tuple-element.31.refs_0_, bf16[32,128,1024]{2,1,0:T(8,128)(2,1)} %bitcast.30, ...), custom_call_target="tpu_custom_call" | custom-call | tf_op jit(solution)/shard_map/back/pallas_call | solution.py:916
  357.8 73.6 %tail_quick.1 = (bf16[2,577,1024]{2,1,0:T(8,128)(2,1)}, f32[3,128,1024]{2,1,0:T(8,128)}, f32[16,1024]{1,0:T(8,128)}) custom-call(bf16[2,577,1024]{2,1,0:T(8,128)(2,1)} %copy.20.x_ref, bf16[3,2,592,1024]{3,2,1,0:T(8,128)(2,1)} %get-tuple-element.34.dz_ref, bf16[2,592,1024]{2,1,0:T(8,128)(2,1)} %get-tuple-element.35.n_ref, ...), custom_call_target="tpu_custom_call" | custom-call | tf_op jit(solution)/shard_map/tail_quick/pallas_call | solution.py:1019
  431.4 5.5 %copy.24 = bf16[2,577,1024]{2,0,1:T(2,128)(2,1)} copy(bf16[2,577,1024]{2,1,0:T(8,128)(2,1)} %get-tuple-element.51) | data formatting | bytes 4726784
  436.9 20.8 %close.1 = (f32[3075,128]{1,0:T(8,128)}, f32[8,128]{1,0:T(8,128)}) custom-call(f32[3,128,1024]{2,1,0:T(8,128)} %get-tuple-element.39.chunk_a, f32[3,128,1024]{2,1,0:T(8,128)} %get-tuple-element.40.chunk_b, f32[16,1024]{1,0:T(8,128)} %get-tuple-element.41.gvec), custom_call_target="tpu_custom_call" | custom-call | tf_op jit(solution)/shard_map/close/pallas_call | solution.py:1134
  457.7 1.2 slice.17
  458.9 0.0 copy-start.1
  458.9 2.8 multiply_bitcast_fusion
  462.4 0.0 copy-done.1
  462.4 0.0 copy-done.2
  462.4 4.9 %multiply_subtract_fusion = (f32[393600]{0:T(1024)}, f32[393600]{0:T(1024)}, f32[393600]{0:T(1024)}) fusion(f32[393600]{0:T(1024)S(1)} %copy-done.1, f32[3075,128]{1,0:T(8,128)S(1)} %copy-done.2, f32[]{:T(128)} %bitcast.10, f32[393600]{0:T(1024)} %param.8, f32[393600]{0:T(1024)} %param.9), kind=kLoop, calls=%fused_computation.6 | loop fusion | flops 6297600 | bytes 11020804 | tf_op jit(solution)/shard_map/sub | solution.py:1171
  (3 shorter events, 0.0 us)
Async XLA Ops:
  1.5 8.1 %collective-permute-start = (bf16[96,128]{1,0:T(8,128)(2,1)S(1)}, bf16[96,128]{1,0:T(8,128)(2,1)S(1)}, u32[]{:S(2)}, u32[]{:S(2)}) collective-permute-start(bf16[96,128]{1,0:T(8,128)(2,1)S(1)} %slice_bitcast_fusion), channel_id=1, source_target_pairs={{0,1},{1,2},{2,3},{3,4},{4,5},{5,6},{6,7},{7,8},{8,9},{9,10},{10,1... | collective-permute-start | bytes 73736 | tf_op jit(solution)/shard_map/ppermute | solution.py:1190
  2.8 4.0 copy-start.4
  6.8 2.8 copy-start
  11.6 1.1 copy-start.3
  458.9 3.5 copy-start.1
  458.9 3.5 copy-start.2

commit v5 on v4

--- a/solution.py
+++ b/solution.py
@@ -574,7 +574,9 @@
 )
 
 
-def front_kernel(own, vec_own, x_ref, w, vec, z_ref, n_ref, mix_ref, vlow, wq, qsem, vsem, ssem, rsem, lsem):
+def front_kernel(
+    own, vec_own, x_ref, w, vec, z_out, n_out, mix_out, z_ref, n_ref, mix_ref, osem, vlow, wq, qsem, vsem, ssem, rsem, lsem
+):
     c = Ctx()
     g = Gather(c, own, w, ssem, rsem, lsem)
     vector = Vector(c, vec_own, vlow, vsem)
@@ -591,6 +593,8 @@
     vector.wait()
     vec[...] = vlow[...].astype(F32)
     norm_one(x_ref, vec, n_ref)
+    leave = [pltpu.make_async_copy(n_ref, n_out, osem.at[0])]
+    leave[0].start()
     for j in range(3):
         take(1 + j)
         g.kept(j)
@@ -603,6 +607,8 @@
             if j != 1:
                 r = r + vec[j // 2 : j // 2 + 1, :]
             z_ref[j, i] = r.astype(BF)
+    leave.append(pltpu.make_async_copy(z_ref, z_out, osem.at[1]))
+    leave[1].start()
 
     def pair(t, _):
         for n in range(16):
@@ -623,19 +629,24 @@
         return 0
 
     lax.fori_loop(0, 16, pair, 0)
+    leave.append(pltpu.make_async_copy(mix_ref, mix_out, osem.at[2]))
+    leave[2].start()
     take(20)
     g.sibling(4, 16, (0, 1, 2))
     g.sent()
     vector.sent()
+    for cp in leave:
+        cp.wait()
 
 
 def front(own, vec_own, x):
     vm = pl.BlockSpec(memory_space=pltpu.VMEM)
+    far = pl.BlockSpec(memory_space=pl.ANY)
     dma = lambda n: pltpu.SemaphoreType.DMA((n,))
     return pl.pallas_call(
         front_kernel,
         in_specs=[vm, vm, vm],
-        out_specs=[pl.BlockSpec(memory_space=pl.ANY), vm, vm, vm, vm],
+        out_specs=[far, vm, far, far, far],
         out_shape=[
             jax.ShapeDtypeStruct((32, 3, 128, D), BF),
             jax.ShapeDtypeStruct((16, D), F32),
@@ -643,7 +654,8 @@
             jax.ShapeDtypeStruct((2, SQ, D), BF),
             jax.ShapeDtypeStruct((2, SQ, D), BF),
         ],
-        scratch_shapes=[pltpu.VMEM((16, D), BF), pltpu.VMEM((2, 8, 128, D), BF), dma(3), dma(32)]
+        scratch_shapes=[pltpu.VMEM((3, 2, SQ, D), BF), pltpu.VMEM((2, SQ, D), BF), pltpu.VMEM((2, SQ, D), BF), dma(3)]
+        + [pltpu.VMEM((16, D), BF), pltpu.VMEM((2, 8, 128, D), BF), dma(3), dma(32)]
         + [dma(240), dma(96), dma(3)],
         compiler_params=pltpu.CompilerParams(collective_id=1, has_side_effects=True, vmem_limit_bytes=VMEM_ALL),
         name="front",
@@ -874,18 +886,24 @@
         name="tail",
     )(x, dz, n1, dhid, vec, w.reshape(32, 3, 128, D), gvec)
 
-def back_kernel(z_ref, do_ref, *refs, lo, hi, ranges, scale):
+def back_kernel(z_in, do_in, *refs, lo, hi, ranges, scale):
     n = len(ranges)
     parts = [(a, b, r) for (a, b), r in zip(ranges, refs[:n])]
-    dz_ref, chunk = refs[n : n + 2]
+    dz_out, chunk, z_ref, do_ref, dz_ref, iosem = refs[n : n + 6]
     c = Ctx()
+    loads = [pltpu.make_async_copy(z_in.at[j], z_ref.at[j], iosem.at[j]) for j in range(3)]
+    loads.append(pltpu.make_async_copy(do_in, do_ref, iosem.at[3]))
+    for cp in loads:
+        cp.start()
     order, groups = reduce_order(BACK_STEPS)
-    red = Reduce(c, lo, hi, parts, chunk, refs[n + 2 :], scale, order)
+    red = Reduce(c, lo, hi, parts, chunk, refs[n + 6 :], scale, order)
     red.zero()
     chunk[...] = jnp.zeros_like(chunk)
     c.barrier()
     red.to_sibling()
     red.prefetch()
+    for cp in loads:
+        cp.wait()
 
     def pair(t, _):
         for m in range(16):
@@ -906,19 +924,28 @@
         return 0
 
     lax.fori_loop(0, 16, pair, 0)
+    leave = pltpu.make_async_copy(dz_ref, dz_out, iosem.at[4])
+    leave.start()
     for i in groups[16]:
         red.steps[i]()
     red.finish()
+    leave.wait()
 
 
 def back(z, do, parts, lo, hi, ranges, scale):
     vm = pl.BlockSpec(memory_space=pltpu.VMEM)
     return pl.pallas_call(
         functools.partial(back_kernel, lo=lo, hi=hi, ranges=ranges, scale=scale),
-        in_specs=[vm, vm] + [pl.BlockSpec(memory_space=pl.ANY)] * len(parts),
-        out_specs=[vm, vm],
+        in_specs=[pl.BlockSpec(memory_space=pl.ANY)] * (2 + len(parts)),
+        out_specs=[pl.BlockSpec(memory_space=pl.ANY), vm],
         out_shape=[jax.ShapeDtypeStruct((3, 2, SQ, D), BF), jax.ShapeDtypeStruct((3, 128, D), F32)],
-        scratch_shapes=Reduce.scratch(lo, hi, 4),
+        scratch_shapes=[
+            pltpu.VMEM((3, 2, SQ, D), BF),
+            pltpu.VMEM((2, SQ, D), BF),
+            pltpu.VMEM((3, 2, SQ, D), BF),
+            pltpu.SemaphoreType.DMA((5,)),
+        ]
+        + Reduce.scratch(lo, hi, 4),
         compiler_params=pltpu.CompilerParams(collective_id=2, has_side_effects=True, vmem_limit_bytes=VMEM_ALL),
         name="back",
     )(z, do, *parts)
@@ -935,7 +962,8 @@
 
 
 def tail_quick_kernel(
-    x_ref, dz_ref, n_ref, dhid_ref, vec_ref, gvin_ref, w, gx_ref, chunk, gvec_ref, acc, gw, wq, qsem, *scr, scale
+    x_in, dz_ref, n_ref, dhid_in, vec_ref, gvin_ref, w, gx_ref, chunk, gvec_ref,
+    x_ref, dhid_ref, xsem, acc, gw, wq, qsem, *scr, scale
 ):
     c = Ctx()
     order, groups = reduce_order(TAIL_STEPS)
@@ -943,6 +971,9 @@
     loads = [pltpu.make_async_copy(w.at[0:8, j], wq.at[j % 2], qsem.at[j]) for j in range(3)]
     loads[0].start()
     loads[1].start()
+    late = [pltpu.make_async_copy(x_in, x_ref, xsem.at[0]), pltpu.make_async_copy(dhid_in, dhid_ref, xsem.at[1])]
+    for cp in late:
+        cp.start()
     red.zero()
     chunk[...] = jnp.zeros_like(chunk)
     gvec_ref[...] = gvin_ref[...]
@@ -990,6 +1021,8 @@
         if j == 0:
             loads[2].start()
         take(4 + j)
+    for cp in late:
+        cp.wait()
     a = b = jnp.zeros((CH, D), F32)
     la = lb = jnp.zeros((1, D), F32)
     for i in range(2):
@@ -1016,9 +1049,10 @@
 
 def tail_quick(x, dz, n1, dhid, vec, gvec, w, scale):
     vm = pl.BlockSpec(memory_space=pltpu.VMEM)
+    far = pl.BlockSpec(memory_space=pl.ANY)
     return pl.pallas_call(
         functools.partial(tail_quick_kernel, scale=scale),
-        in_specs=[vm] * 6 + [pl.BlockSpec(memory_space=pl.ANY)],
+        in_specs=[far, vm, vm, far, vm, vm, far],
         out_specs=[vm] * 3,
         out_shape=[
             jax.ShapeDtypeStruct((2, S, D), BF),
@@ -1026,6 +1060,9 @@
             jax.ShapeDtypeStruct((16, D), F32),
         ],
         scratch_shapes=[
+            pltpu.VMEM((2, S, D), BF),
+            pltpu.VMEM((M, D), F32),
+            pltpu.SemaphoreType.DMA((2,)),
             pltpu.VMEM((M, D), F32),
             pltpu.VMEM((24, 128, D), BF),
             pltpu.VMEM((2, 8, 128, D), BF),

time: 477 us -> 469 us (0.983)
  Pallas kernels: 432 us -> 425 us
where the time goes in v5:
time: 469 us; the launch traced here: 460 us
  Pallas kernels  425 us (91%)
  local copies, waits for them, and re-layouts  23.4 us (5%)
  other arithmetic  9.61 us (2%)
    pallas_call x1, Pallas kernels, front(): pl.pallas_call(front_kernel, in_specs=[vm, vm, vm], out_specs=[far, vm, f...  133 us
    pallas_call x1, Pallas kernels, mlp(): pl.pallas_call(functools.partial(mlp_kernel, FB=FB, NB=NB), grid=(NB,), i...  102 us
    pallas_call x1, Pallas kernels, back(): pl.pallas_call(functools.partial(back_kernel, lo=lo, hi=hi, ranges=ranges...  94.2 us
    pallas_call x1, Pallas kernels, tail_quick(): pl.pallas_call(functools.partial(tail_quick_kernel, scale=scale), in_spec...  78.1 us
    unnamed x14, local copies, waits for them, and re-layouts  18 us
    pallas_call x1, Pallas kernels, close(): pl.pallas_call(functools.partial(close_kernel, scale=scale), in_specs=[vm...  17.7 us
  transfers between devices with their start and end apart: 1, of which 0 were waited for; matrix products, arithmetic and copies ran while one was open for 2% of the time, Pallas kernels for 0%

profile of v5, /device:TPU:0, one launch (start us, length us, event | category | flops | bytes accessed | tf_op | source)
XLA Modules:
  0.0 460.4 jit_solution(4686145594016462571)
XLA Ops:
  0.6 0.8 slice_bitcast_fusion
  1.5 0.5 collective-permute-start
  2.0 0.8 slice.19
  2.8 0.0 copy-start.4
  2.8 4.0 copy.20.x_ref.x_in
  6.8 0.0 copy-done.4
  6.8 0.0 copy-start
  6.8 2.1 copy.21.g_ref
  8.9 0.6 pad.5.vec_own
  9.6 0.0 collective-permute-done
  9.6 0.0 copy-done
  9.6 0.4 fusion.2
  10.0 0.2 reshape_reshape.13
  10.2 1.2 reshape_reshape.14
  11.4 0.2 reshape_reshape.12
  11.6 0.0 copy-start.3
  11.6 0.2 copy.18
  11.9 0.9 copy-done.3
  12.8 1.5 fusion.3.own
  14.3 133.0 %front.1 = (bf16[32,3,128,1024]{3,2,1,0:T(8,128)(2,1)}, f32[16,1024]{1,0:T(8,128)}, bf16[3,2,592,1024]{3,2,1,0:T(8,128)(2,1)}, bf16[2,592,1024]{2,1,0:T(8,128)(2,1)}, bf16[2,592,1024]{2,1,0:T(8,128)(2,1)}) custom-call(bf16[3,128,1024]{2,1,0:T(8,128)(2,1)} %fusion.3.own, bf16[16,1024]{1,0:T(8,128)(2,1)} %pad.5.vec_own, bf16[2,577,1024]{2,1,0:T(8,128)(2,1)} %copy.20.x_ref.x_in), custom_call_target="tpu_custom_call" | custom-call | tf_op jit(solution)/shard_map/front/pallas_call | solution.py:646
  147.2 102.1 %mlp512.1 = (bf16[2,577,1024]{2,1,0:T(8,128)(2,1)}, bf16[32,4,32,1024]{3,2,1,0:T(8,128)(2,1)}, bf16[32,128,1024]{2,1,0:T(8,128)(2,1)}, bf16[8,128,1024]{2,1,0:T(...) custom-call(bf16[2,577,1024]{2,1,0:T(8,128)(2,1)} %copy.20.x_ref.x_in, ...), custom_call_target="tpu_custom_call" | custom-call | tf_op jit(solution)/shard_map/mlp512/pallas_call | solution.py:800
  249.3 5.5 %copy.23 = bf16[2,577,1024]{2,0,1:T(2,128)(2,1)} copy(bf16[2,577,1024]{2,1,0:T(8,128)(2,1)} %get-tuple-element.50) | data formatting | bytes 4726784
  254.8 94.2 %back.1 = (bf16[3,2,592,1024]{3,2,1,0:T(8,128)(2,1)}, f32[3,128,1024]{2,1,0:T(8,128)}) custom-call(bf16[3,2,592,1024]{3,2,1,0:T(8,128)(2,1)} %get-tuple-element.29.z_in, bf16[2,592,1024]{2,1,0:T(8,128)(2,1)} %get-tuple-element.30.do_in, bf16[8,128,1024]{2,1,0:T(8,128)(2,1)} %get-tuple-element.31.refs_0_, bf16[32,128,1024]{2,1,0:T(8,128)(2,1)} %bitcast.30, ...), custom_call_target="tpu_custom_call" | custom-call | tf_op jit(solution)/shard_map/back/pallas_call | solution.py:937
  349.1 78.1 %tail_quick.1 = (bf16[2,577,1024]{2,1,0:T(8,128)(2,1)}, f32[3,128,1024]{2,1,0:T(8,128)}, f32[16,1024]{1,0:T(8,128)}) custom-call(bf16[2,577,1024]{2,1,0:T(8,128)(2,1)} %copy.20.x_ref.x_in, bf16[3,2,592,1024]{3,2,1,0:T(8,128)(2,1)} %get-tuple-element.34.dz_ref, bf16[2,592,1024]{2,1,0:T(8,128)(2,1)} %get-tuple-element.35.n_ref, ...), custom_call_target="tpu_custom_call" | custom-call | tf_op jit(solution)/shard_map/tail_quick/pallas_call | solution.py:1053
  427.1 5.5 %copy.24 = bf16[2,577,1024]{2,0,1:T(2,128)(2,1)} copy(bf16[2,577,1024]{2,1,0:T(8,128)(2,1)} %get-tuple-element.51) | data formatting | bytes 4726784
  432.7 17.7 %close.1 = (f32[3075,128]{1,0:T(8,128)}, f32[8,128]{1,0:T(8,128)}) custom-call(f32[3,128,1024]{2,1,0:T(8,128)} %get-tuple-element.39.chunk_a, f32[3,128,1024]{2,1,0:T(8,128)} %get-tuple-element.40.chunk_b, f32[16,1024]{1,0:T(8,128)} %get-tuple-element.41.gvec), custom_call_target="tpu_custom_call" | custom-call | tf_op jit(solution)/shard_map/close/pallas_call | solution.py:1171
  450.4 1.2 slice.17
  451.6 0.0 copy-start.1
  451.6 2.8 multiply_bitcast_fusion
  455.0 0.0 copy-done.1
  455.0 0.0 copy-done.2
  455.0 4.9 %multiply_subtract_fusion = (f32[393600]{0:T(1024)}, f32[393600]{0:T(1024)}, f32[393600]{0:T(1024)}) fusion(f32[393600]{0:T(1024)S(1)} %copy-done.1, f32[3075,128]{1,0:T(8,128)S(1)} %copy-done.2, f32[]{:T(128)} %bitcast.10, f32[393600]{0:T(1024)} %param.8, f32[393600]{0:T(1024)} %param.9), kind=kLoop, calls=%fused_computation.6 | loop fusion | flops 6297600 | bytes 11020804 | tf_op jit(solution)/shard_map/sub | solution.py:1208
  (3 shorter events, 0.0 us)
Async XLA Ops:
  1.5 8.1 %collective-permute-start = (bf16[96,128]{1,0:T(8,128)(2,1)S(1)}, bf16[96,128]{1,0:T(8,128)(2,1)S(1)}, u32[]{:S(2)}, u32[]{:S(2)}) collective-permute-start(bf16[96,128]{1,0:T(8,128)(2,1)S(1)} %slice_bitcast_fusion), channel_id=1, source_target_pairs={{0,1},{1,2},{2,3},{3,4},{4,5},{5,6},{6,7},{7,8},{8,9},{9,10},{10,1... | collective-permute-start | bytes 73736 | tf_op jit(solution)/shard_map/ppermute | solution.py:1227
  2.8 4.0 copy-start.4
  6.8 2.8 copy-start
  11.6 1.1 copy-start.3
  451.6 3.5 copy-start.1
  451.6 3.5 copy-start.2

commit v6 on v5

--- a/solution.py
+++ b/solution.py
@@ -126,14 +126,13 @@
         def body():
             s.wait(src, k)
             r = s.w.at[src, k]
-            if kind == "z":
-                if zz < 2:
-                    s.send(r, src, k, c.up, outer, lambda: c.z > zz, lambda: c.hasup)
-                if zz > 1:
-                    s.send(r, src, k, c.dn, outer, lambda: c.z < zz, lambda: c.hasdn)
+            cross = (zz, k) in CROSS_FIRST
+            if kind == "z" or (cross and kind == "a"):
+                s.send(r, src, k, c.up, outer, lambda: c.z >= zz, lambda: c.hasup)
+                s.send(r, src, k, c.dn, outer, lambda: c.z <= zz, lambda: c.hasdn)
             if kind in "za":
                 s.send(r, src, k, c.bp, outer)
-            if kind == "z":
+            if kind == "z" and not cross:
                 s.send(r, src, k, c.ap, outer)
             s.send(r, src, k, c.sib, outer)
 
@@ -550,28 +549,29 @@
 
 
 FRONT_STEPS = (
-    ("oa31", "oa30", "ou00", "oa01", "od11", "ob20", "os21", "os00", "os31", "ob31", "ob30", "ou31", "ob00", "oa32", "ou01", "ob10", "oa20", "ob21", "od32", "oa10", "z00",),
-    ("od10", "os01", "ob01", "od31", "b00", "ou32", "oa00", "z01", "ou02", "ob02", "od20", "od12", "a00", "os12", "z02", "os30", "a01", "os02", "oa02", "ob32", "b02", "od30", "a02", "od21", "os32", "oa21", "os20", "os11", "oa11", "ou20", "ob22", "oa22", "ob12", "z10", "c00", "z11", "ou10", "c01", "os10", "od22", "ob11", "b01", "ou11",),
-    ("z12", "z20", "os22", "z21", "ou21", "ou12", "oa12", "c02",),
+    ("ob30", "os11", "os32", "ob00", "oa32", "ou00", "ou20", "ob21", "oa20", "ou21", "od12", "oa31", "oa00", "os10", "od10", "os00", "oa10", "os02", "ob32", "os22", "od31", "od32", "ob10", "ob20", "od22", "ob22", "od11", "ou10", "oa02", "oa30", "z00", "a00", "b00", "os21", "ob01", "oa01", "z01", "z02", "ou01", "ob31", "ou11", "ob02", "od20",),
+    ("os20", "ou02", "a01", "ou12", "os12", "ou22", "c00", "a02", "z22", "z10", "z12", "os01", "z20", "b01", "c01", "os30", "ob12", "b02", "od30", "z11", "od21", "oa11", "ou31",),
+    ("oa12", "c02", "oa21", "a10", "b10", "ou30", "ou32", "ob11",),
     ("a11",),
-    ("a10", "z22", "b10", "ou22",),
-    ("b11", "a21", "a20",),
-    ("ou30", "a12",),
     (),
-    ("a22", "z31",),
+    ("z21",),
+    ("a12", "z30",),
     (),
+    ("z31", "c10", "b12",),
+    ("os31", "z32", "a30",),
+    ("b21",),
+    ("a20", "a21",),
     (),
+    ("oa22", "a31", "c11",),
     (),
-    ("z30", "c10", "z32", "b20",),
+    ("b20", "a22", "b31", "b32", "b22", "c21", "a32",),
+    ("c30", "c12", "c20",),
+    ("c31", "b11",),
     (),
-    ("b31", "a30",),
-    (),
-    ("c20", "b30",),
-    ("a31", "c21", "c12", "b22", "c11", "a32",),
-    ("b21", "c30", "b32", "c22",),
-    ("b12", "c31",),
+    ("b30", "c22",),
     ("c32",),
 )
+CROSS_FIRST = ((1, 1), (2, 1), (1, 2), (2, 2), (1, 0))
 
 
 def front_kernel(
@@ -656,7 +656,7 @@
         ],
         scratch_shapes=[pltpu.VMEM((3, 2, SQ, D), BF), pltpu.VMEM((2, SQ, D), BF), pltpu.VMEM((2, SQ, D), BF), dma(3)]
         + [pltpu.VMEM((16, D), BF), pltpu.VMEM((2, 8, 128, D), BF), dma(3), dma(32)]
-        + [dma(240), dma(96), dma(3)],
+        + [dma(300), dma(96), dma(3)],
         compiler_params=pltpu.CompilerParams(collective_id=1, has_side_effects=True, vmem_limit_bytes=VMEM_ALL),
         name="front",
     )(own, vec_own, x)

time: 469 us -> 465 us (level)
    pallas_call x1, Pallas kernels: 78.1 us -> 69 us  [tail_quick(): pl.pallas_call(functools.partial(tail_quick_kernel, scale=scale), in_spec...]
    pallas_call x1, Pallas kernels: 17.7 us -> 26.7 us  [close(): pl.pallas_call(functools.partial(close_kernel, scale=scale), in_specs=[vm...]
where the time goes in v6:
time: 465 us; the launch traced here: 456 us
  Pallas kernels  421 us (91%)
  local copies, waits for them, and re-layouts  23.4 us (5%)
  other arithmetic  9.61 us (2%)
    pallas_call x1, Pallas kernels, front(): pl.pallas_call(front_kernel, in_specs=[vm, vm, vm], out_specs=[far, vm, f...  129 us
    pallas_call x1, Pallas kernels, mlp(): pl.pallas_call(functools.partial(mlp_kernel, FB=FB, NB=NB), grid=(NB,), i...  102 us
    pallas_call x1, Pallas kernels, back(): pl.pallas_call(functools.partial(back_kernel, lo=lo, hi=hi, ranges=ranges...  94.4 us
    pallas_call x1, Pallas kernels, tail_quick(): pl.pallas_call(functools.partial(tail_quick_kernel, scale=scale), in_spec...  69 us
    pallas_call x1, Pallas kernels, close(): pl.pallas_call(functools.partial(close_kernel, scale=scale), in_specs=[vm...  26.7 us
    unnamed x14, local copies, waits for them, and re-layouts  18 us
  transfers between devices with their start and end apart: 1, of which 0 were waited for; matrix products, arithmetic and copies ran while one was open for 2% of the time, Pallas kernels for 0%

profile of v6, /device:TPU:0, one launch (start us, length us, event | category | flops | bytes accessed | tf_op | source)
XLA Modules:
  0.0 456.0 jit_solution(16879284964719589410)
XLA Ops:
  0.6 0.8 slice_bitcast_fusion
  1.5 0.5 collective-permute-start
  2.0 0.8 slice.19
  2.8 0.0 copy-start.4
  2.8 4.0 copy.20.x_ref.x_in
  6.8 0.0 copy-done.4
  6.8 0.0 copy-start
  6.8 2.1 copy.21.g_ref
  8.9 0.6 pad.5.vec_own
  9.6 0.0 collective-permute-done
  9.6 0.0 copy-done
  9.6 0.4 fusion.2
  10.0 0.2 reshape_reshape.13
  10.2 1.2 reshape_reshape.14
  11.4 0.2 reshape_reshape.12
  11.6 0.0 copy-start.3
  11.6 0.2 copy.18
  11.9 0.9 copy-done.3
  12.8 1.5 fusion.3.own
  14.3 128.6 %front.1 = (bf16[32,3,128,1024]{3,2,1,0:T(8,128)(2,1)}, f32[16,1024]{1,0:T(8,128)}, bf16[3,2,592,1024]{3,2,1,0:T(8,128)(2,1)}, bf16[2,592,1024]{2,1,0:T(8,128)(2,1)}, bf16[2,592,1024]{2,1,0:T(8,128)(2,1)}) custom-call(bf16[3,128,1024]{2,1,0:T(8,128)(2,1)} %fusion.3.own, bf16[16,1024]{1,0:T(8,128)(2,1)} %pad.5.vec_own, bf16[2,577,1024]{2,1,0:T(8,128)(2,1)} %copy.20.x_ref.x_in), custom_call_target="tpu_custom_call" | custom-call | tf_op jit(solution)/shard_map/front/pallas_call | solution.py:646
  142.8 102.1 %mlp512.1 = (bf16[2,577,1024]{2,1,0:T(8,128)(2,1)}, bf16[32,4,32,1024]{3,2,1,0:T(8,128)(2,1)}, bf16[32,128,1024]{2,1,0:T(8,128)(2,1)}, bf16[8,128,1024]{2,1,0:T(...) custom-call(bf16[2,577,1024]{2,1,0:T(8,128)(2,1)} %copy.20.x_ref.x_in, ...), custom_call_target="tpu_custom_call" | custom-call | tf_op jit(solution)/shard_map/mlp512/pallas_call | solution.py:800
  244.9 5.5 %copy.23 = bf16[2,577,1024]{2,0,1:T(2,128)(2,1)} copy(bf16[2,577,1024]{2,1,0:T(8,128)(2,1)} %get-tuple-element.50) | data formatting | bytes 4726784
  250.4 94.4 %back.1 = (bf16[3,2,592,1024]{3,2,1,0:T(8,128)(2,1)}, f32[3,128,1024]{2,1,0:T(8,128)}) custom-call(bf16[3,2,592,1024]{3,2,1,0:T(8,128)(2,1)} %get-tuple-element.29.z_in, bf16[2,592,1024]{2,1,0:T(8,128)(2,1)} %get-tuple-element.30.do_in, bf16[8,128,1024]{2,1,0:T(8,128)(2,1)} %get-tuple-element.31.refs_0_, bf16[32,128,1024]{2,1,0:T(8,128)(2,1)} %bitcast.30, ...), custom_call_target="tpu_custom_call" | custom-call | tf_op jit(solution)/shard_map/back/pallas_call | solution.py:937
  344.8 69.0 %tail_quick.1 = (bf16[2,577,1024]{2,1,0:T(8,128)(2,1)}, f32[3,128,1024]{2,1,0:T(8,128)}, f32[16,1024]{1,0:T(8,128)}) custom-call(bf16[2,577,1024]{2,1,0:T(8,128)(2,1)} %copy.20.x_ref.x_in, bf16[3,2,592,1024]{3,2,1,0:T(8,128)(2,1)} %get-tuple-element.34.dz_ref, bf16[2,592,1024]{2,1,0:T(8,128)(2,1)} %get-tuple-element.35.n_ref, ...), custom_call_target="tpu_custom_call" | custom-call | tf_op jit(solution)/shard_map/tail_quick/pallas_call | solution.py:1053
  413.8 5.5 %copy.24 = bf16[2,577,1024]{2,0,1:T(2,128)(2,1)} copy(bf16[2,577,1024]{2,1,0:T(8,128)(2,1)} %get-tuple-element.51) | data formatting | bytes 4726784
  419.3 26.7 %close.1 = (f32[3075,128]{1,0:T(8,128)}, f32[8,128]{1,0:T(8,128)}) custom-call(f32[3,128,1024]{2,1,0:T(8,128)} %get-tuple-element.39.chunk_a, f32[3,128,1024]{2,1,0:T(8,128)} %get-tuple-element.40.chunk_b, f32[16,1024]{1,0:T(8,128)} %get-tuple-element.41.gvec), custom_call_target="tpu_custom_call" | custom-call | tf_op jit(solution)/shard_map/close/pallas_call | solution.py:1171
  446.0 1.2 slice.17
  447.2 0.0 copy-start.1
  447.2 2.8 multiply_bitcast_fusion
  450.6 0.0 copy-done.1
  450.6 0.0 copy-done.2
  450.6 4.9 %multiply_subtract_fusion = (f32[393600]{0:T(1024)}, f32[393600]{0:T(1024)}, f32[393600]{0:T(1024)}) fusion(f32[393600]{0:T(1024)S(1)} %copy-done.1, f32[3075,128]{1,0:T(8,128)S(1)} %copy-done.2, f32[]{:T(128)} %bitcast.10, f32[393600]{0:T(1024)} %param.8, f32[393600]{0:T(1024)} %param.9), kind=kLoop, calls=%fused_computation.6 | loop fusion | flops 6297600 | bytes 11020804 | tf_op jit(solution)/shard_map/sub | solution.py:1208
  (3 shorter events, 0.0 us)
Async XLA Ops:
  1.5 8.1 %collective-permute-start = (bf16[96,128]{1,0:T(8,128)(2,1)S(1)}, bf16[96,128]{1,0:T(8,128)(2,1)S(1)}, u32[]{:S(2)}, u32[]{:S(2)}) collective-permute-start(bf16[96,128]{1,0:T(8,128)(2,1)S(1)} %slice_bitcast_fusion), channel_id=1, source_target_pairs={{0,1},{1,2},{2,3},{3,4},{4,5},{5,6},{6,7},{7,8},{8,9},{9,10},{10,1... | collective-permute-start | bytes 73736 | tf_op jit(solution)/shard_map/ppermute | solution.py:1227
  2.8 4.0 copy-start.4
  6.8 2.8 copy-start
  11.6 1.1 copy-start.3
  447.2 3.5 copy-start.1
  447.2 3.5 copy-start.2

commit v7 on v6

--- a/solution.py
+++ b/solution.py
@@ -945,7 +945,7 @@
             pltpu.VMEM((3, 2, SQ, D), BF),
             pltpu.SemaphoreType.DMA((5,)),
         ]
-        + Reduce.scratch(lo, hi, 4),
+        + Reduce.scratch(lo, hi, 6),
         compiler_params=pltpu.CompilerParams(collective_id=2, has_side_effects=True, vmem_limit_bytes=VMEM_ALL),
         name="back",
     )(z, do, *parts)

time: 465 us -> 464 us (level)
  no operation moved by 1% of the time
where the time goes in v7:
time: 464 us; the launch traced here: 455 us
  Pallas kernels  420 us (91%)
  local copies, waits for them, and re-layouts  23.4 us (5%)
  other arithmetic  9.61 us (2%)
    pallas_call x1, Pallas kernels, front(): pl.pallas_call(front_kernel, in_specs=[vm, vm, vm], out_specs=[far, vm, f...  129 us
    pallas_call x1, Pallas kernels, mlp(): pl.pallas_call(functools.partial(mlp_kernel, FB=FB, NB=NB), grid=(NB,), i...  102 us
    pallas_call x1, Pallas kernels, back(): pl.pallas_call(functools.partial(back_kernel, lo=lo, hi=hi, ranges=ranges...  94.4 us
    pallas_call x1, Pallas kernels, tail_quick(): pl.pallas_call(functools.partial(tail_quick_kernel, scale=scale), in_spec...  68.3 us
    pallas_call x1, Pallas kernels, close(): pl.pallas_call(functools.partial(close_kernel, scale=scale), in_specs=[vm...  26.7 us
    unnamed x14, local copies, waits for them, and re-layouts  18 us
  transfers between devices with their start and end apart: 1, of which 0 were waited for; matrix products, arithmetic and copies ran while one was open for 2% of the time, Pallas kernels for 0%

profile of v7, /device:TPU:0, one launch (start us, length us, event | category | flops | bytes accessed | tf_op | source)
XLA Modules:
  0.0 455.3 jit_solution(12857457135753638138)
XLA Ops:
  0.6 0.8 slice_bitcast_fusion
  1.5 0.5 collective-permute-start
  2.0 0.8 slice.19
  2.8 0.0 copy-start.4
  2.8 4.0 copy.20.x_ref.x_in
  6.8 0.0 copy-done.4
  6.8 0.0 copy-start
  6.8 2.1 copy.21.g_ref
  8.9 0.6 pad.5.vec_own
  9.6 0.0 collective-permute-done
  9.6 0.0 copy-done
  9.6 0.4 fusion.2
  10.0 0.2 reshape_reshape.13
  10.2 1.2 reshape_reshape.14
  11.4 0.2 reshape_reshape.12
  11.6 0.0 copy-start.3
  11.6 0.2 copy.18
  11.9 0.9 copy-done.3
  12.8 1.5 fusion.3.own
  14.3 128.6 %front.1 = (bf16[32,3,128,1024]{3,2,1,0:T(8,128)(2,1)}, f32[16,1024]{1,0:T(8,128)}, bf16[3,2,592,1024]{3,2,1,0:T(8,128)(2,1)}, bf16[2,592,1024]{2,1,0:T(8,128)(2,1)}, bf16[2,592,1024]{2,1,0:T(8,128)(2,1)}) custom-call(bf16[3,128,1024]{2,1,0:T(8,128)(2,1)} %fusion.3.own, bf16[16,1024]{1,0:T(8,128)(2,1)} %pad.5.vec_own, bf16[2,577,1024]{2,1,0:T(8,128)(2,1)} %copy.20.x_ref.x_in), custom_call_target="tpu_custom_call" | custom-call | tf_op jit(solution)/shard_map/front/pallas_call | solution.py:646
  142.8 102.1 %mlp512.1 = (bf16[2,577,1024]{2,1,0:T(8,128)(2,1)}, bf16[32,4,32,1024]{3,2,1,0:T(8,128)(2,1)}, bf16[32,128,1024]{2,1,0:T(8,128)(2,1)}, bf16[8,128,1024]{2,1,0:T(...) custom-call(bf16[2,577,1024]{2,1,0:T(8,128)(2,1)} %copy.20.x_ref.x_in, ...), custom_call_target="tpu_custom_call" | custom-call | tf_op jit(solution)/shard_map/mlp512/pallas_call | solution.py:800
  244.9 5.5 %copy.23 = bf16[2,577,1024]{2,0,1:T(2,128)(2,1)} copy(bf16[2,577,1024]{2,1,0:T(8,128)(2,1)} %get-tuple-element.50) | data formatting | bytes 4726784
  250.4 94.4 %back.1 = (bf16[3,2,592,1024]{3,2,1,0:T(8,128)(2,1)}, f32[3,128,1024]{2,1,0:T(8,128)}) custom-call(bf16[3,2,592,1024]{3,2,1,0:T(8,128)(2,1)} %get-tuple-element.29.z_in, bf16[2,592,1024]{2,1,0:T(8,128)(2,1)} %get-tuple-element.30.do_in, bf16[8,128,1024]{2,1,0:T(8,128)(2,1)} %get-tuple-element.31.refs_0_, bf16[32,128,1024]{2,1,0:T(8,128)(2,1)} %bitcast.30, ...), custom_call_target="tpu_custom_call" | custom-call | tf_op jit(solution)/shard_map/back/pallas_call | solution.py:937
  344.8 68.3 %tail_quick.1 = (bf16[2,577,1024]{2,1,0:T(8,128)(2,1)}, f32[3,128,1024]{2,1,0:T(8,128)}, f32[16,1024]{1,0:T(8,128)}) custom-call(bf16[2,577,1024]{2,1,0:T(8,128)(2,1)} %copy.20.x_ref.x_in, bf16[3,2,592,1024]{3,2,1,0:T(8,128)(2,1)} %get-tuple-element.34.dz_ref, bf16[2,592,1024]{2,1,0:T(8,128)(2,1)} %get-tuple-element.35.n_ref, ...), custom_call_target="tpu_custom_call" | custom-call | tf_op jit(solution)/shard_map/tail_quick/pallas_call | solution.py:1053
  413.1 5.5 %copy.24 = bf16[2,577,1024]{2,0,1:T(2,128)(2,1)} copy(bf16[2,577,1024]{2,1,0:T(8,128)(2,1)} %get-tuple-element.51) | data formatting | bytes 4726784
  418.6 26.7 %close.1 = (f32[3075,128]{1,0:T(8,128)}, f32[8,128]{1,0:T(8,128)}) custom-call(f32[3,128,1024]{2,1,0:T(8,128)} %get-tuple-element.39.chunk_a, f32[3,128,1024]{2,1,0:T(8,128)} %get-tuple-element.40.chunk_b, f32[16,1024]{1,0:T(8,128)} %get-tuple-element.41.gvec), custom_call_target="tpu_custom_call" | custom-call | tf_op jit(solution)/shard_map/close/pallas_call | solution.py:1171
  445.3 1.2 slice.17
  446.5 0.0 copy-start.1
  446.5 2.8 multiply_bitcast_fusion
  449.9 0.0 copy-done.1
  449.9 0.0 copy-done.2
  449.9 4.9 %multiply_subtract_fusion = (f32[393600]{0:T(1024)}, f32[393600]{0:T(1024)}, f32[393600]{0:T(1024)}) fusion(f32[393600]{0:T(1024)S(1)} %copy-done.1, f32[3075,128]{1,0:T(8,128)S(1)} %copy-done.2, f32[]{:T(128)} %bitcast.10, f32[393600]{0:T(1024)} %param.8, f32[393600]{0:T(1024)} %param.9), kind=kLoop, calls=%fused_computation.6 | loop fusion | flops 6297600 | bytes 11020804 | tf_op jit(solution)/shard_map/sub | solution.py:1208
  (3 shorter events, 0.0 us)
Async XLA Ops:
  1.5 8.1 %collective-permute-start = (bf16[96,128]{1,0:T(8,128)(2,1)S(1)}, bf16[96,128]{1,0:T(8,128)(2,1)S(1)}, u32[]{:S(2)}, u32[]{:S(2)}) collective-permute-start(bf16[96,128]{1,0:T(8,128)(2,1)S(1)} %slice_bitcast_fusion), channel_id=1, source_target_pairs={{0,1},{1,2},{2,3},{3,4},{4,5},{5,6},{6,7},{7,8},{8,9},{9,10},{10,1... | collective-permute-start | bytes 73736 | tf_op jit(solution)/shard_map/ppermute | solution.py:1227
  2.8 4.0 copy-start.4
  6.8 2.8 copy-start
  11.6 1.1 copy-start.3
  446.5 3.5 copy-start.1
  446.5 3.5 copy-start.2
